TPU v7x, 512 devices: a whole 4x8x8 slice. The times are simulated.
512 devices in a mesh: seq: 32 (over x, y), exp: 16 (over z, core).
Axes of the slice: x: 4, y: 8, z: 8, core: 2. Of those that a mesh axis runs over, the one named last changes fastest.
Arguments:
- tokens: bfloat16 [16384, 1024], P(('seq', 'exp')), may hold values from -22 to 22
- array_type: int32 [16384], P(('seq', 'exp')), may hold values from 0 to 15, as said below
- block_pattern: int32 [32, 32], replicated, may hold values from 0 to 1, as said below
- gain_attn: float32 [1024], replicated, may hold values from 0.25 to 1.75
- w_query: bfloat16 [1024, 1024], P(None, 'exp'), may hold values from -0.1875 to 0.1875
- w_key: bfloat16 [1024, 1024], P(None, 'exp'), may hold values from -0.1875 to 0.1875
- w_value: bfloat16 [1024, 1024], P(None, 'exp'), may hold values from -0.1875 to 0.1875
- logit_scale: float32 [16], P('exp'), may hold values from 0.06 to 30
- w_out: bfloat16 [1024, 1024], P('exp'), may hold values from -0.1875 to 0.1875
- gain_ffn: float32 [1024], replicated, may hold values from 0.25 to 1.75
- w_gate: bfloat16 [16, 1024, 4096], P('exp', None, 'seq'), may hold values from -0.1875 to 0.1875
- w_up: bfloat16 [16, 1024, 4096], P('exp', None, 'seq'), may hold values from -0.1875 to 0.1875
- w_down: bfloat16 [16, 1024, 4096], P('exp', None, 'seq'), may hold values from -0.09375 to 0.09375
Outputs:
- encoded: bfloat16 [16384, 1024], P(('seq', 'exp'))
Inputs may be any that keep to these rules, and one draw needn't show every extreme that they name: `array_type`: in each aligned block of 32 rows no type occurs more than 4 times and some type occurs exactly 4 times; in some aligned block of 512 rows one type occurs exactly 4 times in each of its blocks of 32 rows. block_pattern[q][q] is 1, and block_pattern[q][k] is 0 where blocks q and k lie more than 3 apart around the loop of 32 blocks.
All inputs are finite; a program needn't handle non-finite values.
Results may differ from a plain program's by a relative error of at most 0.011.
The roundings to bfloat16 on the way count: a program that leaves them out, or rounds other values in their place, can miss the bound.
Values may be sent and summed in bfloat16 or wider, within the bound.
A program may use at most 64 MiB of HBM per device.

v0:
```python
import jax
import jax.numpy as jnp
from jax import lax
from jax.sharding import PartitionSpec as P

REACH = 3


EPSILON = 1e-05


def passed_along(block, axis, distance):
    devices = range(lax.axis_size(axis))
    route = [((i - distance) % len(devices), i) for i in devices]
    return lax.ppermute(block, axis, route)


def rms_scale(matrix, gain):
    mean_square = jnp.mean(matrix * matrix, axis=-1, keepdims=True)
    return matrix * lax.rsqrt(mean_square + EPSILON) * gain


def expert_terms(block, gate_slice, up_slice, down_slice):
    gate = jnp.einsum("nek,ekf->nef", block, gate_slice, preferred_element_type=jnp.float32)
    upward = jnp.einsum("nek,ekf->nef", block, up_slice, preferred_element_type=jnp.float32)
    act = (jax.nn.silu(gate) * upward).astype(jnp.bfloat16)
    return jnp.einsum("nef,ekf->nek", act, down_slice, preferred_element_type=jnp.float32)


def local(
    tokens,
    array_type,
    block_pattern,
    gain_attn,
    w_query,
    w_key,
    w_value,
    logit_scale,
    w_out,
    gain_ffn,
    w_gate,
    w_up,
    w_down,
):
    n_exp = lax.axis_size("exp")
    row_count = tokens.shape[0]
    width = tokens.shape[1]
    head_cols = w_query.shape[1]
    heads_dev = logit_scale.shape[0]
    head_size = head_cols // heads_dev
    n_blocks = block_pattern.shape[0]
    inputs = tokens.astype(jnp.float32)
    normed_attn = rms_scale(inputs, gain_attn).astype(jnp.bfloat16)
    projector = jnp.concatenate([w_query, w_key, w_value], axis=1)
    joined_qkv = jnp.dot(
        lax.all_gather(normed_attn, "exp", axis=0, tiled=True),
        projector,
        preferred_element_type=jnp.float32,
    ).astype(jnp.bfloat16)
    block_len = joined_qkv.shape[0]
    query_heads = joined_qkv[:, :head_cols].reshape(block_len, heads_dev, head_size)
    key_value = joined_qkv[:, head_cols:]
    position = lax.axis_index("seq")
    head_scale = logit_scale[:, None, None]

    def attend(state, kv_block, source):
        row_top, weight_sum, numerator = state
        key_rows = kv_block[:, :head_cols].reshape(block_len, heads_dev, head_size)
        value_rows = kv_block[:, head_cols:].reshape(block_len, heads_dev, head_size)
        allowed = block_pattern[position, source] > 0
        scores = (
            jnp.einsum("qhd,khd->hqk", query_heads, key_rows, preferred_element_type=jnp.float32)
            * head_scale
        )
        block_top = jnp.max(scores, axis=2)
        new_top = jnp.where(allowed, jnp.maximum(row_top, block_top), row_top)
        shifted = jnp.minimum(scores - new_top[:, :, None], 0.0)
        weights = jnp.where(allowed, jnp.exp(shifted), 0.0)
        rescale = jnp.exp(row_top - new_top)
        weight_sum = weight_sum * rescale + jnp.sum(weights, axis=2)
        contrib = jnp.einsum(
            "hqk,khd->qhd",
            weights.astype(jnp.bfloat16),
            value_rows,
            preferred_element_type=jnp.float32,
        )
        numerator = numerator * jnp.transpose(rescale)[:, :, None] + contrib
        return (new_top, weight_sum, numerator)

    start_state = (
        jnp.full((heads_dev, block_len), -jnp.inf, jnp.float32),
        jnp.zeros((heads_dev, block_len), jnp.float32),
        jnp.zeros((block_len, heads_dev, head_size), jnp.float32),
    )
    state = attend(start_state, key_value, position)
    lower = key_value
    upper = key_value
    for distance in range(1, REACH + 1):
        lower = passed_along(lower, "seq", 1)
        upper = passed_along(upper, "seq", -1)
        state = attend(state, lower, (position - distance) % n_blocks)
        state = attend(state, upper, (position + distance) % n_blocks)
    heads_out = (
        (state[2] / jnp.transpose(state[1])[:, :, None])
        .astype(jnp.bfloat16)
        .reshape(block_len, head_cols)
    )
    all_heads = lax.all_to_all(heads_out, "exp", split_axis=0, concat_axis=1, tiled=True)
    attn_out = jnp.dot(
        all_heads,
        lax.all_gather(w_out, "exp", axis=0, tiled=True),
        preferred_element_type=jnp.float32,
    )
    hidden_state = inputs + attn_out
    normed_ffn = rms_scale(hidden_state, gain_ffn).astype(jnp.bfloat16)
    experts_dev = w_gate.shape[0]
    n_total = experts_dev * n_exp
    capacity = 2 * row_count // n_total
    one_hot = (array_type[:, None] == jnp.arange(n_total, dtype=jnp.int32)[None, :]).astype(
        jnp.int32
    )
    slot_rank = jnp.sum(jnp.cumsum(one_hot, axis=0) * one_hot, axis=1) - 1
    owner = array_type // experts_dev
    local_expert = array_type % experts_dev
    slot_id = (owner * capacity + slot_rank) * experts_dev + local_expert
    n_slots = n_exp * capacity * experts_dev
    selector = (slot_id[None, :] == jnp.arange(n_slots, dtype=jnp.int32)[:, None]).astype(
        jnp.bfloat16
    )
    outgoing = jnp.dot(selector, normed_ffn, preferred_element_type=jnp.float32).astype(
        jnp.bfloat16
    )
    outgoing = outgoing.reshape(n_exp * capacity, experts_dev, width)
    arrived = lax.all_to_all(outgoing, "exp", split_axis=0, concat_axis=0, tiled=True)
    gathered = lax.all_gather(arrived, "seq", axis=0, tiled=True)
    summed = lax.psum_scatter(
        expert_terms(gathered, w_gate, w_up, w_down).astype(jnp.bfloat16),
        "seq",
        scatter_dimension=0,
        tiled=True,
    )
    returned = lax.all_to_all(summed, "exp", split_axis=0, concat_axis=0, tiled=True)
    expert_out = jnp.dot(
        jnp.transpose(selector),
        returned.reshape(n_slots, width),
        preferred_element_type=jnp.float32,
    )
    return (hidden_state + expert_out).astype(jnp.bfloat16)


def solution(mesh):
    return jax.shard_map(
        local,
        mesh=mesh,
        in_specs=(
            P(("seq", "exp"), None),
            P(("seq", "exp")),
            P(),
            P(),
            P(None, "exp"),
            P(None, "exp"),
            P(None, "exp"),
            P("exp"),
            P("exp", None),
            P(),
            P("exp", None, "seq"),
            P("exp", None, "seq"),
            P("exp", None, "seq"),
        ),
        out_specs=P(("seq", "exp"), None),
        check_vma=False,
    )
```

profile of v0, /device:TPU:1, one launch (start us, length us, event | category | flops | bytes accessed | tf_op | source)
XLA Modules:
  0.0 468.6 jit_solution(5350282731695840697)
XLA Ops:
  6.5 1.0 fusion.91
  7.6 1.6 fusion.93
  9.2 0.7 all-gather.6.cloned.1.call-update
  10.6 1.6 fusion.131
  16.5 0.7 fusion.121
  17.3 0.8 select_reduce_fusion
  18.1 39.3 %all-gather.4.cloned.1.call-done = bf16[512,1024]{1,0:T(8,128)(2,1)} async-done(((bf16[32,1024]{1,0:T(8,128)(2,1)}), bf16[512,1024]{1,0:T(8,128)(2,1)}) %all-gather.4.cloned.1.call-update) | async-done | bytes 1048592 | tf_op jit(solution)/shard_map/all_gather | solution.py:56
  57.4 1.8 convolution_convert_fusion
  59.2 3.1 collective-permute-start
  62.3 5.5 %collective-permute-start.1 = (bf16[512,128]{0,1:T(8,128)(2,1)S(1)}, bf16[512,128]{0,1:T(8,128)(2,1)S(1)}, u32[]{:S(2)}, u32[]{:S(2)}) collective-permute-start(bf16[512,128]{0,1:T(8,128)(2,1)S(1)} %slice.69), channel_id=1, source_target_pairs={{16,0},{32,16},{48,32},{64,48},{80,64},{96,80},{112,96},{128,112},... | collective-permute-start | bytes 393224 | tf_op jit(solution)/shard_map/ppermute | solution.py:15
  68.4 0.8 collective-permute-done
  69.2 1.9 collective-permute-start.2
  71.2 6.7 %collective-permute-start.3 = (bf16[512,128]{0,1:T(8,128)(2,1)S(1)}, bf16[512,128]{0,1:T(8,128)(2,1)S(1)}, u32[]{:S(2)}, u32[]{:S(2)}) collective-permute-start(bf16[512,128]{0,1:T(8,128)(2,1)S(1)} %collective-permute-done.1), channel_id=1, source_target_pairs={{16,0},{32,16},{48,32},{64,48},{80,64},{96,80},{112,96},{128,112},... | collective-permute-start | bytes 393224 | tf_op jit(solution)/shard_map/ppermute | solution.py:15
  78.6 1.9 collective-permute-start.4
  80.5 6.7 %collective-permute-start.5 = (bf16[512,128]{0,1:T(8,128)(2,1)S(1)}, bf16[512,128]{0,1:T(8,128)(2,1)S(1)}, u32[]{:S(2)}, u32[]{:S(2)}) collective-permute-start(bf16[512,128]{0,1:T(8,128)(2,1)S(1)} %collective-permute-done.3), channel_id=1, source_target_pairs={{16,0},{32,16},{48,32},{64,48},{80,64},{96,80},{112,96},{128,112},... | collective-permute-start | bytes 393224 | tf_op jit(solution)/shard_map/ppermute | solution.py:15
  88.3 0.8 collective-permute-done.5
  91.3 0.4 fusion.49
  93.3 0.8 reshape.570
  94.0 7.2 %all-to-all-start = ((bf16[16,2,1024]{2,1,0:T(2,128)(2,1)}), bf16[16,2,1024]{2,1,0:T(2,128)(2,1)S(1)}, u32[]{:S(2)}, u32[]{:S(2)}) async-start(bf16[16,2,1024]{2,1,0:T(2,128)(2,1)} %reshape.570), calls=%async_computation | async-start | bytes 131072 | tf_op jit(solution)/shard_map/all_to_all | solution.py:108
  101.3 7.7 %all-to-all-done = bf16[16,2,1024]{2,1,0:T(2,128)(2,1)S(1)} async-done(((bf16[16,2,1024]{2,1,0:T(2,128)(2,1)}), bf16[16,2,1024]{2,1,0:T(2,128)(2,1)S(1)}, u32[]{:S(2)}, u32[]{:S(2)}) %all-to-all-start) | async-done | bytes 65568 | tf_op jit(solution)/shard_map/all_to_all | solution.py:108
  109.4 2.2 multiply_reduce_fusion
  111.9 0.5 broadcast.544
  112.4 0.7 reduce.28
  113.2 11.8 %all_to_all.29 = bf16[16,2,2048]{2,1,0:T(2,128)(2,1)S(1)} all-to-all(bf16[16,2,2048]{2,1,0:T(2,128)(2,1)S(1)} %reshape.572), channel_id=1, replica_groups=mesh['seq'=32,'exp'=16] {'exp'}, dimensions={0} | all-to-all | bytes 262144 | tf_op jit(solution)/shard_map/all_to_all | solution.py:134
  125.1 0.7 copy.23
  126.0 78.1 %all-gather.8.cloned.1.call-done = bf16[2048,1,1024]{2,0,1:T(8,128)(2,1)} async-done(((bf16[64,1,1024]{2,0,1:T(8,128)(2,1)}), bf16[2048,1,1024]{2,0,1:T(8,128)(2,1)}) %all-gather.8.cloned.1.call-update) | async-done | bytes 4194320 | tf_op jit(solution)/shard_map/all_gather | solution.py:135
  204.1 3.5 fusion.4
  207.6 8.3 %convert_bitcast_fusion = bf16[2048,1,1024]{2,0,1:T(8,128)(2,1)} fusion(bf16[2048,1,1024]{2,0,1:T(8,128)(2,1)} %all-gather.8.cloned.1.call-done, f32[2048,1,128]{2,0,1:T(8,128)S(1)} %fusion.4, bf16[1,1024,128]{2,1,0:T(8,128)(2,1)S(1)} %copy-done, bf16[1,1024,128]{2,1,0:T(8,128)(2,1)S(1)} %copy-done.3), kind=kOutput, calls=%fused_computation.4 | convolution fusion | flops 1077411840 | bytes 9961472 | tf_op jit(solution)/shard_map/nef,ekf->nek/dot_general | solution.py:27
  215.9 222.2 %reduce-scatter.2.cloned.1.call-done = bf16[64,1,1024]{2,0,1:T(8,128)(2,1)} async-done(((bf16[2048,1,1024]{2,0,1:T(8,128)(2,1)}), bf16[64,1,1024]{2,0,1:T(8,128)(2,1)}) %reduce-scatter.2.cloned.1.call-update) | async-done | bytes 131088 | tf_op jit(solution)/shard_map/reduce_scatter | solution.py:136
  438.1 1.6 reduce.29
  439.8 21.3 %all_to_all.30 = bf16[16,2,2048]{2,1,0:T(2,128)(2,1)S(1)} all-to-all(bf16[16,2,2048]{2,1,0:T(2,128)(2,1)S(1)} %reshape.574), channel_id=1, replica_groups=mesh['seq'=32,'exp'=16] {'exp'}, dimensions={0} | all-to-all | bytes 262144 | tf_op jit(solution)/shard_map/all_to_all | solution.py:142
  461.2 0.8 fusion.35
  (58 shorter events, 7.5 us)
Async XLA Ops:
  6.5 201.1 %copy-start = (bf16[1,1024,128]{2,1,0:T(8,128)(2,1)S(1)}, bf16[1,1024,128]{2,1,0:T(8,128)(2,1)}, u32[]{:S(2)}) copy-start(bf16[1,1024,128]{2,1,0:T(8,128)(2,1)} %param.25) | copy-start | bytes 786436
  6.5 50.8 %all-gather.4.cloned.1.call-start = ((), (), s32[]{:S(2)}) async-start(), calls=%async_computation.4 | async-start | bytes 1114112 | tf_op jit(solution)/shard_map/all_gather | solution.py:56
  9.1 100.3 %all-gather.6.cloned.1.call-start = ((), (), s32[]{:S(2)}) async-start(), calls=%async_computation.5 | async-start | bytes 2228224 | tf_op jit(solution)/shard_map/all_gather | solution.py:111
  59.2 10.1 %collective-permute-start = (bf16[512,128]{0,1:T(8,128)(2,1)S(1)}, bf16[512,128]{0,1:T(8,128)(2,1)S(1)}, u32[]{:S(2)}, u32[]{:S(2)}) collective-permute-start(bf16[512,128]{0,1:T(8,128)(2,1)S(1)} %slice.69), channel_id=1, source_target_pairs={{496,0},{0,16},{16,32},{32,48},{48,64},{64,80},{80,96},{96,112},{1... | collective-permute-start | bytes 393224 | tf_op jit(solution)/shard_map/ppermute | solution.py:15
  62.3 8.8 %collective-permute-start.1 = (bf16[512,128]{0,1:T(8,128)(2,1)S(1)}, bf16[512,128]{0,1:T(8,128)(2,1)S(1)}, u32[]{:S(2)}, u32[]{:S(2)}) collective-permute-start(bf16[512,128]{0,1:T(8,128)(2,1)S(1)} %slice.69), channel_id=1, source_target_pairs={{16,0},{32,16},{48,32},{64,48},{80,64},{96,80},{112,96},{128,112},... | collective-permute-start | bytes 393224 | tf_op jit(solution)/shard_map/ppermute | solution.py:15
  69.2 9.3 %collective-permute-start.2 = (bf16[512,128]{0,1:T(8,128)(2,1)S(1)}, bf16[512,128]{0,1:T(8,128)(2,1)S(1)}, u32[]{:S(2)}, u32[]{:S(2)}) collective-permute-start(bf16[512,128]{0,1:T(8,128)(2,1)S(1)} %collective-permute-done), channel_id=1, source_target_pairs={{496,0},{0,16},{16,32},{32,48},{48,64},{64,80},{80,96},{96,112},{1... | collective-permute-start | bytes 393224 | tf_op jit(solution)/shard_map/ppermute | solution.py:15
  71.2 9.4 %collective-permute-start.3 = (bf16[512,128]{0,1:T(8,128)(2,1)S(1)}, bf16[512,128]{0,1:T(8,128)(2,1)S(1)}, u32[]{:S(2)}, u32[]{:S(2)}) collective-permute-start(bf16[512,128]{0,1:T(8,128)(2,1)S(1)} %collective-permute-done.1), channel_id=1, source_target_pairs={{16,0},{32,16},{48,32},{64,48},{80,64},{96,80},{112,96},{128,112},... | collective-permute-start | bytes 393224 | tf_op jit(solution)/shard_map/ppermute | solution.py:15
  78.6 9.3 %collective-permute-start.4 = (bf16[512,128]{0,1:T(8,128)(2,1)S(1)}, bf16[512,128]{0,1:T(8,128)(2,1)S(1)}, u32[]{:S(2)}, u32[]{:S(2)}) collective-permute-start(bf16[512,128]{0,1:T(8,128)(2,1)S(1)} %collective-permute-done.2), channel_id=1, source_target_pairs={{496,0},{0,16},{16,32},{32,48},{48,64},{64,80},{80,96},{96,112},{1... | collective-permute-start | bytes 393224 | tf_op jit(solution)/shard_map/ppermute | solution.py:15
  80.5 8.6 %collective-permute-start.5 = (bf16[512,128]{0,1:T(8,128)(2,1)S(1)}, bf16[512,128]{0,1:T(8,128)(2,1)S(1)}, u32[]{:S(2)}, u32[]{:S(2)}) collective-permute-start(bf16[512,128]{0,1:T(8,128)(2,1)S(1)} %collective-permute-done.3), channel_id=1, source_target_pairs={{16,0},{32,16},{48,32},{64,48},{80,64},{96,80},{112,96},{128,112},... | collective-permute-start | bytes 393224 | tf_op jit(solution)/shard_map/ppermute | solution.py:15
  91.3 10.0 %copy-start.5 = (s32[32]{0:T(128)S(1)}, s32[32]{0:T(128)}, u32[]{:S(2)}) copy-start(s32[32]{0:T(128)} %param.14) | copy-start | bytes 388
  91.8 17.7 %copy-start.1 = (bf16[32,1024]{1,0:T(8,128)(2,1)S(1)}, bf16[32,1024]{1,0:T(8,128)(2,1)}, u32[]{:S(2)}) copy-start(bf16[32,1024]{1,0:T(8,128)(2,1)} %param.13) | copy-start | bytes 196612
  92.1 19.5 %copy-start.4 = (f32[1024]{0:T(1024)S(1)}, f32[1024]{0:T(1024)}, u32[]{:S(2)}) copy-start(f32[1024]{0:T(1024)} %param.22) | copy-start | bytes 12292
  92.5 111.7 %copy-start.2 = (bf16[1,1024,128]{2,1,0:T(8,128)(2,1)S(1)}, bf16[1,1024,128]{2,1,0:T(8,128)(2,1)}, u32[]{:S(2)}) copy-start(bf16[1,1024,128]{2,1,0:T(8,128)(2,1)} %param.23) | copy-start | bytes 786436
  94.0 15.0 %all-to-all-start = ((bf16[16,2,1024]{2,1,0:T(2,128)(2,1)}), bf16[16,2,1024]{2,1,0:T(2,128)(2,1)S(1)}, u32[]{:S(2)}, u32[]{:S(2)}) async-start(bf16[16,2,1024]{2,1,0:T(2,128)(2,1)} %reshape.570), calls=%async_computation | async-start | bytes 131072 | tf_op jit(solution)/shard_map/all_to_all | solution.py:108
  101.2 102.9 %all-gather.8.cloned.1.call-start = ((), (), s32[]{:S(2)}) async-start(), calls=%async_computation.6 | async-start | bytes 4325376 | tf_op jit(solution)/shard_map/all_gather | solution.py:135
  111.9 95.7 %copy-start.3 = (bf16[1,1024,128]{2,1,0:T(8,128)(2,1)S(1)}, bf16[1,1024,128]{2,1,0:T(8,128)(2,1)}, u32[]{:S(2)}) copy-start(bf16[1,1024,128]{2,1,0:T(8,128)(2,1)} %param.24) | copy-start | bytes 786436
  125.8 312.3 %reduce-scatter.2.cloned.1.call-start = ((), (), s32[]{:S(2)}) async-start(), calls=%async_computation.7 | async-start | bytes 4325376 | tf_op jit(solution)/shard_map/reduce_scatter | solution.py:136
Sparse Core Ops, SparseCore 0:
  9.5 47.8 all-gather.3
  59.5 41.1 all-gather.5
  125.9 78.1 all-gather.7
  216.0 221.9 reduce-scatter.1
where the time goes:
time: 469 us
  waiting for transfers between devices  350 us (75%)
  starting transfers between devices  33.3 us (7%)
  blocking collectives  33.1 us (7%)
  matrix products  21.5 us (5%)
  between operations  18.4 us (4%)
  other arithmetic  8.04 us (2%)
    reduce_scatter x1, waiting for transfers between devices, local(): lax.psum_scatter(expert_terms(gathered, w_gate, w_up, w_down).astype(jnp....  222 us
    all_gather x1, waiting for transfers between devices, local(): gathered = lax.all_gather(arrived, 'seq', axis=0, tiled=True)  78.1 us
    all_gather x1, waiting for transfers between devices, local(): lax.all_gather(normed_attn, 'exp', axis=0, tiled=True)  39.3 us
    ppermute x6, starting transfers between devices, passed_along(): return lax.ppermute(block, axis, route)  25.8 us
    all_to_all x1, blocking collectives, local(): lax.all_to_all(summed, 'exp', split_axis=0, concat_axis=0, tiled=True)  21.3 us
    all_to_all x1, blocking collectives, local(): lax.all_to_all(outgoing, 'exp', split_axis=0, concat_axis=0, tiled=True)  11.8 us
  transfers between devices with their start and end apart: 11, of which 6 were waited for; matrix products, arithmetic and copies ran while one was open for 3% of the time, Pallas kernels for 0%

commit v1 on v0

--- a/solution.py
+++ b/solution.py
@@ -133,11 +133,15 @@
     outgoing = outgoing.reshape(n_exp * capacity, experts_dev, width)
     arrived = lax.all_to_all(outgoing, "exp", split_axis=0, concat_axis=0, tiled=True)
     gathered = lax.all_gather(arrived, "seq", axis=0, tiled=True)
-    summed = lax.psum_scatter(
-        expert_terms(gathered, w_gate, w_up, w_down).astype(jnp.bfloat16),
-        "seq",
-        scatter_dimension=0,
-        tiled=True,
+    n_seq = lax.axis_size("seq")
+    partial = expert_terms(gathered, w_gate, w_up, w_down).astype(jnp.bfloat16)
+    scattered = lax.all_to_all(partial, "seq", split_axis=0, concat_axis=0, tiled=True)
+    summed = (
+        jnp.sum(
+            scattered.reshape((n_seq, -1) + scattered.shape[1:]).astype(jnp.float32),
+            axis=0,
+        )
+        .astype(jnp.bfloat16)
     )
     returned = lax.all_to_all(summed, "exp", split_axis=0, concat_axis=0, tiled=True)
     expert_out = jnp.dot(

time: 469 us -> 390 us (0.83)
  waiting for transfers between devices: 350 us -> 127 us
  blocking collectives: 33.1 us -> 131 us
  local copies, waits for them, and re-layouts: 4.53 us -> 39.2 us
  other arithmetic: 8.04 us -> 17.5 us
    reduce_scatter x1 -> x0, waiting for transfers between devices: 222 us -> none  [local(): lax.psum_scatter(expert_terms(gathered, w_gate, w_up, w_down).astype(jnp....]
    all_to_all x0 -> x1, blocking collectives: none -> 93.4 us  [local(): lax.all_to_all(partial, 'seq', split_axis=0, concat_axis=0, tiled=True)]
    unnamed x18 -> x21, local copies, waits for them, and re-layouts: 1.37 us -> 36 us
    convert_element_type x0 -> x1, other arithmetic: none -> 7.27 us  [local(): partial = expert_terms(gathered, w_gate, w_up, w_down).astype(jnp.bfloat16)]
    all_gather x1, waiting for transfers between devices: 78.1 us -> 73.1 us  [local(): gathered = lax.all_gather(arrived, 'seq', axis=0, tiled=True)]
    ppermute x6, waiting for transfers between devices: 1.68 us -> 6.48 us  [passed_along(): return lax.ppermute(block, axis, route)]
  transfers between devices with their start and end apart: 11 -> 10, of which waited for: 6 -> 5; matrix products, arithmetic and copies ran while one was open for 3% -> 3% of each run, Pallas kernels for 0% -> 0%
where the time goes in v1:
time: 390 us; the launch traced here: 388 us
  blocking collectives  131 us (34%)
  waiting for transfers between devices  127 us (33%)
  local copies, waits for them, and re-layouts  39.2 us (10%)
  starting transfers between devices  34.1 us (9%)
  matrix products  21.4 us (5%)
  between operations  18.5 us (5%)
  other arithmetic  17.5 us (4%)
    all_to_all x1, blocking collectives, local(): lax.all_to_all(partial, 'seq', split_axis=0, concat_axis=0, tiled=True)  93.4 us
    all_gather x1, waiting for transfers between devices, local(): gathered = lax.all_gather(arrived, 'seq', axis=0, tiled=True)  73.1 us
    all_gather x1, waiting for transfers between devices, local(): lax.all_gather(normed_attn, 'exp', axis=0, tiled=True)  39.2 us
    unnamed x21, local copies, waits for them, and re-layouts  36 us
    ppermute x6, starting transfers between devices, passed_along(): return lax.ppermute(block, axis, route)  26.5 us
    all_to_all x1, blocking collectives, local(): lax.all_to_all(summed, 'exp', split_axis=0, concat_axis=0, tiled=True)  25.3 us
    all_to_all x1, blocking collectives, local(): lax.all_to_all(outgoing, 'exp', split_axis=0, concat_axis=0, tiled=True)  11.8 us
    dot_general x1, matrix products, expert_terms(): jnp.einsum('nef,ekf->nek', act, down_slice, preferred_element_type=jnp.fl...  8.25 us
  transfers between devices with their start and end apart: 10, of which 5 were waited for; matrix products, arithmetic and copies ran while one was open for 3% of the time, Pallas kernels for 0%

profile of v1, /device:TPU:1, one launch (start us, length us, event | category | flops | bytes accessed | tf_op | source)
XLA Modules:
  0.0 388.4 jit_solution(16389943510147401181)
XLA Ops:
  6.5 1.0 fusion.91
  7.6 1.6 fusion.93
  9.2 0.7 all-gather.6.cloned.1.call-update
  10.6 1.6 fusion.131
  16.6 0.7 fusion.121
  17.3 0.8 select_reduce_fusion
  18.2 39.2 %all-gather.4.cloned.1.call-done = bf16[512,1024]{1,0:T(8,128)(2,1)} async-done(((bf16[32,1024]{1,0:T(8,128)(2,1)}), bf16[512,1024]{1,0:T(8,128)(2,1)}) %all-gather.4.cloned.1.call-update) | async-done | bytes 1048592 | tf_op jit(solution)/shard_map/all_gather | solution.py:56
  57.4 1.8 convolution_convert_fusion
  59.2 6.6 %collective-permute-start.1 = (bf16[512,128]{0,1:T(8,128)(2,1)S(1)}, bf16[512,128]{0,1:T(8,128)(2,1)S(1)}, u32[]{:S(2)}, u32[]{:S(2)}) collective-permute-start(bf16[512,128]{0,1:T(8,128)(2,1)S(1)} %slice.69), channel_id=1, source_target_pairs={{16,0},{32,16},{48,32},{64,48},{80,64},{96,80},{112,96},{128,112},... | collective-permute-start | bytes 393224 | tf_op jit(solution)/shard_map/ppermute | solution.py:15
  65.8 1.9 collective-permute-start
  68.4 7.4 %collective-permute-start.3 = (bf16[512,128]{0,1:T(8,128)(2,1)S(1)}, bf16[512,128]{0,1:T(8,128)(2,1)S(1)}, u32[]{:S(2)}, u32[]{:S(2)}) collective-permute-start(bf16[512,128]{0,1:T(8,128)(2,1)S(1)} %collective-permute-done.1), channel_id=1, source_target_pairs={{16,0},{32,16},{48,32},{64,48},{80,64},{96,80},{112,96},{128,112},... | collective-permute-start | bytes 393224 | tf_op jit(solution)/shard_map/ppermute | solution.py:15
  75.8 1.9 collective-permute-start.2
  78.5 6.7 %collective-permute-start.5 = (bf16[512,128]{0,1:T(8,128)(2,1)S(1)}, bf16[512,128]{0,1:T(8,128)(2,1)S(1)}, u32[]{:S(2)}, u32[]{:S(2)}) collective-permute-start(bf16[512,128]{0,1:T(8,128)(2,1)S(1)} %collective-permute-done.3), channel_id=1, source_target_pairs={{16,0},{32,16},{48,32},{64,48},{80,64},{96,80},{112,96},{128,112},... | collective-permute-start | bytes 393224 | tf_op jit(solution)/shard_map/ppermute | solution.py:15
  85.2 1.9 collective-permute-start.4
  87.8 6.4 %collective-permute-done.4 = bf16[512,128]{0,1:T(8,128)(2,1)S(1)} collective-permute-done((bf16[512,128]{0,1:T(8,128)(2,1)S(1)}, bf16[512,128]{0,1:T(8,128)(2,1)S(1)}, u32[]{:S(2)}, u32[]{:S(2)}) %collective-permute-start.4) | collective-permute-done | bytes 131104 | tf_op jit(solution)/shard_map/ppermute | solution.py:15
  98.7 0.8 reshape.575
  99.5 7.5 %all-to-all-start = ((bf16[16,2,1024]{2,1,0:T(2,128)(2,1)}), bf16[16,2,1024]{2,1,0:T(2,128)(2,1)S(1)}, u32[]{:S(2)}, u32[]{:S(2)}) async-start(bf16[16,2,1024]{2,1,0:T(2,128)(2,1)} %reshape.575), calls=%async_computation | async-start | bytes 131072 | tf_op jit(solution)/shard_map/all_to_all | solution.py:108
  107.0 7.7 %all-to-all-done = bf16[16,2,1024]{2,1,0:T(2,128)(2,1)S(1)} async-done(((bf16[16,2,1024]{2,1,0:T(2,128)(2,1)}), bf16[16,2,1024]{2,1,0:T(2,128)(2,1)S(1)}, u32[]{:S(2)}, u32[]{:S(2)}) %all-to-all-start) | async-done | bytes 65568 | tf_op jit(solution)/shard_map/all_to_all | solution.py:108
  115.2 2.2 multiply_reduce_fusion
  118.9 11.8 %all_to_all.34 = bf16[16,2,2048]{2,1,0:T(2,128)(2,1)S(1)} all-to-all(bf16[16,2,2048]{2,1,0:T(2,128)(2,1)S(1)} %reshape.577), channel_id=1, replica_groups=mesh['seq'=32,'exp'=16] {'exp'}, dimensions={0} | all-to-all | bytes 262144 | tf_op jit(solution)/shard_map/all_to_all | solution.py:134
  130.8 0.7 copy.23
  131.5 73.1 %all-gather.8.cloned.1.call-done = bf16[2048,1,1024]{2,0,1:T(8,128)(2,1)} async-done(((bf16[64,1,1024]{2,0,1:T(8,128)(2,1)}), bf16[2048,1,1024]{2,0,1:T(8,128)(2,1)}) %all-gather.8.cloned.1.call-update) | async-done | bytes 4194320 | tf_op jit(solution)/shard_map/all_gather | solution.py:135
  204.7 3.4 fusion.4
  208.1 8.2 %convert_bitcast_fusion = bf16[2048,1,1024]{2,0,1:T(8,128)(2,1)} fusion(bf16[2048,1,1024]{2,0,1:T(8,128)(2,1)} %all-gather.8.cloned.1.call-done, f32[2048,1,128]{2,0,1:T(8,128)S(1)} %fusion.4, bf16[1,1024,128]{2,1,0:T(8,128)(2,1)S(1)} %copy-done, bf16[1,1024,128]{2,1,0:T(8,128)(2,1)S(1)} %copy-done.3), kind=kOutput, calls=%fused_computation.4 | convolution fusion | flops 1077411840 | bytes 9961472 | tf_op jit(solution)/shard_map/nef,ekf->nek/dot_general | solution.py:27
  216.4 7.3 %reduce.31 = bf16[2048,1024]{1,0:T(8,128)(2,1)} reduce(bf16[2048,1,1024]{2,0,1:T(8,128)(2,1)} %convert_bitcast_fusion, bf16[]{:T(256)} %broadcast.544), dimensions={1}, to_apply=%copy.24.reduce_sub_computation | reduce | bytes 8388610 | tf_op jit(solution)/shard_map/convert_element_type | solution.py:137
  223.6 7.8 %reshape.579 = bf16[32,2,32768]{2,1,0:T(2,128)(2,1)} reshape(bf16[2048,1024]{1,0:T(8,128)(2,1)} %reduce.31) | data formatting | bytes 8388608
  231.4 93.4 %all_to_all.35 = bf16[32,2,32768]{2,1,0:T(2,128)(2,1)} all-to-all(bf16[32,2,32768]{2,1,0:T(2,128)(2,1)} %reshape.579), channel_id=1, replica_groups=mesh['seq'=32,'exp'=16] {'seq'}, dimensions={0} | all-to-all | bytes 8388608 | tf_op jit(solution)/shard_map/all_to_all | solution.py:138
  324.9 19.8 %reshape.580 = bf16[2048,1,1024]{2,1,0:T(2,128)(2,1)} reshape(bf16[32,2,32768]{2,1,0:T(2,128)(2,1)} %all_to_all.35) | data formatting | bytes 8388608
  344.6 7.1 %copy.26 = bf16[2048,1,1024]{2,0,1:T(8,128)(2,1)} copy(bf16[2048,1,1024]{2,1,0:T(2,128)(2,1)} %reshape.580) | data formatting | bytes 8388608
  351.7 3.1 reduce_sum.114
  355.6 25.3 %all_to_all.36 = bf16[16,2,2048]{2,1,0:T(2,128)(2,1)S(1)} all-to-all(bf16[16,2,2048]{2,1,0:T(2,128)(2,1)S(1)} %reshape.581), channel_id=1, replica_groups=mesh['seq'=32,'exp'=16] {'exp'}, dimensions={0} | all-to-all | bytes 262144 | tf_op jit(solution)/shard_map/all_to_all | solution.py:146
  381.0 0.8 fusion.35
  (61 shorter events, 9.6 us)
Async XLA Ops:
  6.5 201.6 %copy-start = (bf16[1,1024,128]{2,1,0:T(8,128)(2,1)S(1)}, bf16[1,1024,128]{2,1,0:T(8,128)(2,1)}, u32[]{:S(2)}) copy-start(bf16[1,1024,128]{2,1,0:T(8,128)(2,1)} %param.25) | copy-start | bytes 786436
  6.5 50.8 %all-gather.4.cloned.1.call-start = ((), (), s32[]{:S(2)}) async-start(), calls=%async_computation.4 | async-start | bytes 1114112 | tf_op jit(solution)/shard_map/all_gather | solution.py:56
  9.1 106.0 %all-gather.6.cloned.1.call-start = ((), (), s32[]{:S(2)}) async-start(), calls=%async_computation.5 | async-start | bytes 2228224 | tf_op jit(solution)/shard_map/all_gather | solution.py:111
  59.2 9.2 %collective-permute-start.1 = (bf16[512,128]{0,1:T(8,128)(2,1)S(1)}, bf16[512,128]{0,1:T(8,128)(2,1)S(1)}, u32[]{:S(2)}, u32[]{:S(2)}) collective-permute-start(bf16[512,128]{0,1:T(8,128)(2,1)S(1)} %slice.69), channel_id=1, source_target_pairs={{16,0},{32,16},{48,32},{64,48},{80,64},{96,80},{112,96},{128,112},... | collective-permute-start | bytes 393224 | tf_op jit(solution)/shard_map/ppermute | solution.py:15
  65.8 10.0 %collective-permute-start = (bf16[512,128]{0,1:T(8,128)(2,1)S(1)}, bf16[512,128]{0,1:T(8,128)(2,1)S(1)}, u32[]{:S(2)}, u32[]{:S(2)}) collective-permute-start(bf16[512,128]{0,1:T(8,128)(2,1)S(1)} %slice.69), channel_id=1, source_target_pairs={{496,0},{0,16},{16,32},{32,48},{48,64},{64,80},{80,96},{96,112},{1... | collective-permute-start | bytes 393224 | tf_op jit(solution)/shard_map/ppermute | solution.py:15
  68.4 10.1 %collective-permute-start.3 = (bf16[512,128]{0,1:T(8,128)(2,1)S(1)}, bf16[512,128]{0,1:T(8,128)(2,1)S(1)}, u32[]{:S(2)}, u32[]{:S(2)}) collective-permute-start(bf16[512,128]{0,1:T(8,128)(2,1)S(1)} %collective-permute-done.1), channel_id=1, source_target_pairs={{16,0},{32,16},{48,32},{64,48},{80,64},{96,80},{112,96},{128,112},... | collective-permute-start | bytes 393224 | tf_op jit(solution)/shard_map/ppermute | solution.py:15
  75.8 9.4 %collective-permute-start.2 = (bf16[512,128]{0,1:T(8,128)(2,1)S(1)}, bf16[512,128]{0,1:T(8,128)(2,1)S(1)}, u32[]{:S(2)}, u32[]{:S(2)}) collective-permute-start(bf16[512,128]{0,1:T(8,128)(2,1)S(1)} %collective-permute-done), channel_id=1, source_target_pairs={{496,0},{0,16},{16,32},{32,48},{48,64},{64,80},{80,96},{96,112},{1... | collective-permute-start | bytes 393224 | tf_op jit(solution)/shard_map/ppermute | solution.py:15
  78.5 16.1 %collective-permute-start.5 = (bf16[512,128]{0,1:T(8,128)(2,1)S(1)}, bf16[512,128]{0,1:T(8,128)(2,1)S(1)}, u32[]{:S(2)}, u32[]{:S(2)}) collective-permute-start(bf16[512,128]{0,1:T(8,128)(2,1)S(1)} %collective-permute-done.3), channel_id=1, source_target_pairs={{16,0},{32,16},{48,32},{64,48},{80,64},{96,80},{112,96},{128,112},... | collective-permute-start | bytes 393224 | tf_op jit(solution)/shard_map/ppermute | solution.py:15
  85.2 9.0 %collective-permute-start.4 = (bf16[512,128]{0,1:T(8,128)(2,1)S(1)}, bf16[512,128]{0,1:T(8,128)(2,1)S(1)}, u32[]{:S(2)}, u32[]{:S(2)}) collective-permute-start(bf16[512,128]{0,1:T(8,128)(2,1)S(1)} %collective-permute-done.2), channel_id=1, source_target_pairs={{496,0},{0,16},{16,32},{32,48},{48,64},{64,80},{80,96},{96,112},{1... | collective-permute-start | bytes 393224 | tf_op jit(solution)/shard_map/ppermute | solution.py:15
  96.8 10.2 %copy-start.5 = (s32[32]{0:T(128)S(1)}, s32[32]{0:T(128)}, u32[]{:S(2)}) copy-start(s32[32]{0:T(128)} %param.14) | copy-start | bytes 388
  97.2 17.9 %copy-start.1 = (bf16[32,1024]{1,0:T(8,128)(2,1)S(1)}, bf16[32,1024]{1,0:T(8,128)(2,1)}, u32[]{:S(2)}) copy-start(bf16[32,1024]{1,0:T(8,128)(2,1)} %param.13) | copy-start | bytes 196612
  97.6 19.8 %copy-start.4 = (f32[1024]{0:T(1024)S(1)}, f32[1024]{0:T(1024)}, u32[]{:S(2)}) copy-start(f32[1024]{0:T(1024)} %param.22) | copy-start | bytes 12292
  97.9 106.7 %copy-start.2 = (bf16[1,1024,128]{2,1,0:T(8,128)(2,1)S(1)}, bf16[1,1024,128]{2,1,0:T(8,128)(2,1)}, u32[]{:S(2)}) copy-start(bf16[1,1024,128]{2,1,0:T(8,128)(2,1)} %param.23) | copy-start | bytes 786436
  99.5 15.3 %all-to-all-start = ((bf16[16,2,1024]{2,1,0:T(2,128)(2,1)}), bf16[16,2,1024]{2,1,0:T(2,128)(2,1)S(1)}, u32[]{:S(2)}, u32[]{:S(2)}) async-start(bf16[16,2,1024]{2,1,0:T(2,128)(2,1)} %reshape.575), calls=%async_computation | async-start | bytes 131072 | tf_op jit(solution)/shard_map/all_to_all | solution.py:108
  107.0 97.7 %all-gather.8.cloned.1.call-start = ((), (), s32[]{:S(2)}) async-start(), calls=%async_computation.6 | async-start | bytes 4325376 | tf_op jit(solution)/shard_map/all_gather | solution.py:135
  117.6 90.5 %copy-start.3 = (bf16[1,1024,128]{2,1,0:T(8,128)(2,1)S(1)}, bf16[1,1024,128]{2,1,0:T(8,128)(2,1)}, u32[]{:S(2)}) copy-start(bf16[1,1024,128]{2,1,0:T(8,128)(2,1)} %param.24) | copy-start | bytes 786436
Sparse Core Ops, SparseCore 0:
  9.5 47.8 all-gather.3
  59.5 41.4 all-gather.5
  131.7 72.9 all-gather.7

commit v2 on v1

--- a/solution.py
+++ b/solution.py
@@ -2,8 +2,12 @@
 import jax.numpy as jnp
 from jax import lax
 from jax.sharding import PartitionSpec as P
+from jax.experimental import pallas as pl
+from jax.experimental.pallas import tpu as pltpu
+import functools
 
 REACH = 3
+Y_RING = 8
 
 
 EPSILON = 1e-05
@@ -13,6 +17,106 @@
     devices = range(lax.axis_size(axis))
     route = [((i - distance) % len(devices), i) for i in devices]
     return lax.ppermute(block, axis, route)
+
+
+def ring_reduce_kernel(nx, ny, part_ref, out_ref, recv1, send1, acc, recv2, send2,
+                       s1_send, s1_recv, s2_send, s2_recv):
+    me = lax.axis_index("seq")
+    col = lax.axis_index("exp")
+    x = me // ny
+    y = me % ny
+    y_up = x * ny + (y + 1) % ny
+    y_down = x * ny + (y + ny - 1) % ny
+    x_up = ((x + 1) % nx) * ny + y
+    x_down = ((x + nx - 1) % nx) * ny + y
+    half_x = nx // 2
+    rows = part_ref.shape[2]
+    half_r = rows // 2
+
+    barrier = pltpu.get_barrier_semaphore()
+    for peer in (y_up, y_down, x_up, x_down):
+        pl.semaphore_signal(barrier, inc=1, device_id=(peer, col),
+                            device_id_type=pl.DeviceIdType.MESH)
+    pl.semaphore_wait(barrier, 4)
+
+    lanes = ((y_up, 0, half_x, 1), (y_down, half_x, nx, -1))
+    copies1 = []
+    for k in range(ny - 1):
+        step_copies = []
+        for d, (peer, lo, hi, sign) in enumerate(lanes):
+            c = (y - sign * (k + 1) + 2 * ny) % ny
+            if k == 0:
+                src = part_ref.at[lo:hi, c]
+            else:
+                copies1[k - 1][d].wait_recv()
+                send1[d, k] = (recv1[d, k - 1].astype(jnp.float32)
+                               + part_ref[lo:hi, c].astype(jnp.float32)).astype(send1.dtype)
+                src = send1.at[d, k]
+            cp = pltpu.make_async_remote_copy(
+                src_ref=src, dst_ref=recv1.at[d, k],
+                send_sem=s1_send.at[d, k], recv_sem=s1_recv.at[d, k],
+                device_id=(peer, col), device_id_type=pl.DeviceIdType.MESH)
+            cp.start()
+            step_copies.append(cp)
+        copies1.append(step_copies)
+    for d, (peer, lo, hi, sign) in enumerate(lanes):
+        copies1[ny - 2][d].wait_recv()
+        acc[lo:hi] = recv1[d, ny - 2].astype(jnp.float32) + part_ref[lo:hi, y].astype(jnp.float32)
+
+    lanes2 = ((x_up, 0, half_r, 1), (x_down, half_r, rows, -1))
+    copies2 = []
+    for k in range(nx - 1):
+        step_copies = []
+        for d, (peer, lo, hi, sign) in enumerate(lanes2):
+            c = (x - sign * (k + 1) + 2 * nx) % nx
+            if k == 0:
+                src = acc.at[c, lo:hi]
+            else:
+                copies2[k - 1][d].wait_recv()
+                send2[d, k] = recv2[d, k - 1] + acc[c, lo:hi]
+                src = send2.at[d, k]
+            cp = pltpu.make_async_remote_copy(
+                src_ref=src, dst_ref=recv2.at[d, k],
+                send_sem=s2_send.at[d, k], recv_sem=s2_recv.at[d, k],
+                device_id=(peer, col), device_id_type=pl.DeviceIdType.MESH)
+            cp.start()
+            step_copies.append(cp)
+        copies2.append(step_copies)
+    for d, (peer, lo, hi, sign) in enumerate(lanes2):
+        copies2[nx - 2][d].wait_recv()
+        out_ref[lo:hi] = (recv2[d, nx - 2] + acc[x, lo:hi]).astype(out_ref.dtype)
+    for step_copies in copies1 + copies2:
+        for cp in step_copies:
+            cp.wait_send()
+
+
+def ring_reduce(part, nx, ny):
+    width = part.shape[-1]
+    rows = part.shape[0] // (nx * ny)
+    part = part.reshape(nx, ny, rows, width)
+    half_x = nx // 2
+    half_r = rows // 2
+    vmem = pltpu.MemorySpace.VMEM
+    return pl.pallas_call(
+        functools.partial(ring_reduce_kernel, nx, ny),
+        out_shape=jax.ShapeDtypeStruct((rows, width), jnp.bfloat16),
+        in_specs=[pl.BlockSpec(memory_space=vmem)],
+        out_specs=pl.BlockSpec(memory_space=vmem),
+        scratch_shapes=[
+            pltpu.VMEM((2, ny - 1, half_x, rows, width), jnp.bfloat16),
+            pltpu.VMEM((2, ny - 1, half_x, rows, width), jnp.bfloat16),
+            pltpu.VMEM((nx, rows, width), jnp.float32),
+            pltpu.VMEM((2, nx - 1, half_r, width), jnp.float32),
+            pltpu.VMEM((2, nx - 1, half_r, width), jnp.float32),
+            pltpu.SemaphoreType.DMA((2, ny - 1)),
+            pltpu.SemaphoreType.DMA((2, ny - 1)),
+            pltpu.SemaphoreType.DMA((2, nx - 1)),
+            pltpu.SemaphoreType.DMA((2, nx - 1)),
+        ],
+        compiler_params=pltpu.CompilerParams(
+            collective_id=1, has_side_effects=True, vmem_limit_bytes=48 * 1024 * 1024
+        ),
+    )(part)
 
 
 def rms_scale(matrix, gain):
@@ -134,15 +238,11 @@
     arrived = lax.all_to_all(outgoing, "exp", split_axis=0, concat_axis=0, tiled=True)
     gathered = lax.all_gather(arrived, "seq", axis=0, tiled=True)
     n_seq = lax.axis_size("seq")
+    y_size = Y_RING if n_seq % Y_RING == 0 else n_seq
     partial = expert_terms(gathered, w_gate, w_up, w_down).astype(jnp.bfloat16)
-    scattered = lax.all_to_all(partial, "seq", split_axis=0, concat_axis=0, tiled=True)
-    summed = (
-        jnp.sum(
-            scattered.reshape((n_seq, -1) + scattered.shape[1:]).astype(jnp.float32),
-            axis=0,
-        )
-        .astype(jnp.bfloat16)
-    )
+    summed = ring_reduce(
+        partial.reshape(partial.shape[0], width), n_seq // y_size, y_size
+    ).reshape((-1,) + partial.shape[1:])
     returned = lax.all_to_all(summed, "exp", split_axis=0, concat_axis=0, tiled=True)
     expert_out = jnp.dot(
         jnp.transpose(selector),

time: 390 us -> 312 us (0.80)
  blocking collectives: 131 us -> 37.7 us
  Pallas kernels: 0 us -> 58.9 us
  local copies, waits for them, and re-layouts: 39.2 us -> 6.71 us
  other arithmetic: 17.5 us -> 7.13 us
    all_to_all x1 -> x0, blocking collectives: 93.4 us -> none  [local(): lax.all_to_all(partial, 'seq', split_axis=0, concat_axis=0, tiled=True)]
    pallas_call x0 -> x1, Pallas kernels: none -> 58.9 us  [ring_reduce(): pl.pallas_call(functools.partial(ring_reduce_kernel, nx, ny), out_shape=j...]
    unnamed x21 -> x20, local copies, waits for them, and re-layouts: 36 us -> 3.55 us
    convert_element_type x1 -> x0, other arithmetic: 7.27 us -> none  [local(): partial = expert_terms(gathered, w_gate, w_up, w_down).astype(jnp.bfloat16)]
    all_gather x1, waiting for transfers between devices: 73.1 us -> 78.3 us  [local(): gathered = lax.all_gather(arrived, 'seq', axis=0, tiled=True)]
    ppermute x6, waiting for transfers between devices: 6.48 us -> 1.68 us  [passed_along(): return lax.ppermute(block, axis, route)]
  transfers between devices with their start and end apart: 10 -> 10, of which waited for: 5 -> 5; matrix products, arithmetic and copies ran while one was open for 3% -> 4% of each run, Pallas kernels for 0% -> 0%
where the time goes in v2:
time: 312 us; the launch traced here: 311 us
  waiting for transfers between devices  128 us (41%)
  Pallas kernels  58.9 us (19%)
  blocking collectives  37.7 us (12%)
  starting transfers between devices  33.1 us (11%)
  matrix products  21.5 us (7%)
  between operations  18.4 us (6%)
  other arithmetic  7.13 us (2%)
  local copies, waits for them, and re-layouts  6.71 us (2%)
    all_gather x1, waiting for transfers between devices, local(): gathered = lax.all_gather(arrived, 'seq', axis=0, tiled=True)  78.3 us
    pallas_call x1, Pallas kernels, ring_reduce(): pl.pallas_call(functools.partial(ring_reduce_kernel, nx, ny), out_shape=j...  58.9 us
    all_gather x1, waiting for transfers between devices, local(): lax.all_gather(normed_attn, 'exp', axis=0, tiled=True)  39.3 us
    all_to_all x1, blocking collectives, local(): lax.all_to_all(summed, 'exp', split_axis=0, concat_axis=0, tiled=True)  25.9 us
    ppermute x6, starting transfers between devices, passed_along(): return lax.ppermute(block, axis, route)  25.8 us
    all_to_all x1, blocking collectives, local(): lax.all_to_all(outgoing, 'exp', split_axis=0, concat_axis=0, tiled=True)  11.8 us
    dot_general x1, matrix products, expert_terms(): jnp.einsum('nef,ekf->nek', act, down_slice, preferred_element_type=jnp.fl...  8.27 us
    all_to_all x1, waiting for transfers between devices, local(): lax.all_to_all(heads_out, 'exp', split_axis=0, concat_axis=1, tiled=True)  7.74 us
  transfers between devices with their start and end apart: 10, of which 5 were waited for; matrix products, arithmetic and copies ran while one was open for 4% of the time, Pallas kernels for 0%

profile of v2, /device:TPU:1, one launch (start us, length us, event | category | flops | bytes accessed | tf_op | source)
XLA Modules:
  0.0 311.2 jit_solution(14364943133815393912)
XLA Ops:
  6.5 1.0 fusion.96
  7.6 1.6 fusion.98
  9.2 0.7 all-gather.6.cloned.1.call-update
  10.6 1.6 fusion.136
  16.5 0.7 fusion.126
  17.3 0.8 select_reduce_fusion
  18.1 39.3 %all-gather.4.cloned.1.call-done = bf16[512,1024]{1,0:T(8,128)(2,1)} async-done(((bf16[32,1024]{1,0:T(8,128)(2,1)}), bf16[512,1024]{1,0:T(8,128)(2,1)}) %all-gather.4.cloned.1.call-update) | async-done | bytes 1048592 | tf_op jit(solution)/shard_map/all_gather | solution.py:160
  57.4 1.8 convolution_convert_fusion.1
  59.2 3.1 %collective-permute-start = (bf16[512,128]{0,1:T(8,128)(2,1)S(1)}, bf16[512,128]{0,1:T(8,128)(2,1)S(1)}, u32[]{:S(2)}, u32[]{:S(2)}) collective-permute-start(bf16[512,128]{0,1:T(8,128)(2,1)S(1)} %slice.69), channel_id=1, source_target_pairs={{496,0},{0,16},{16,32},{32,48},{48,64},{64,80},{80,96},{96,112},{1... | collective-permute-start | bytes 393224 | tf_op jit(solution)/shard_map/ppermute | solution.py:19
  62.3 5.5 %collective-permute-start.1 = (bf16[512,128]{0,1:T(8,128)(2,1)S(1)}, bf16[512,128]{0,1:T(8,128)(2,1)S(1)}, u32[]{:S(2)}, u32[]{:S(2)}) collective-permute-start(bf16[512,128]{0,1:T(8,128)(2,1)S(1)} %slice.69), channel_id=1, source_target_pairs={{16,0},{32,16},{48,32},{64,48},{80,64},{96,80},{112,96},{128,112},... | collective-permute-start | bytes 393224 | tf_op jit(solution)/shard_map/ppermute | solution.py:19
  68.4 0.8 collective-permute-done
  69.2 1.9 collective-permute-start.2
  71.2 6.7 %collective-permute-start.3 = (bf16[512,128]{0,1:T(8,128)(2,1)S(1)}, bf16[512,128]{0,1:T(8,128)(2,1)S(1)}, u32[]{:S(2)}, u32[]{:S(2)}) collective-permute-start(bf16[512,128]{0,1:T(8,128)(2,1)S(1)} %collective-permute-done.1), channel_id=1, source_target_pairs={{16,0},{32,16},{48,32},{64,48},{80,64},{96,80},{112,96},{128,112},... | collective-permute-start | bytes 393224 | tf_op jit(solution)/shard_map/ppermute | solution.py:19
  78.6 1.9 collective-permute-start.4
  80.5 6.7 %collective-permute-start.5 = (bf16[512,128]{0,1:T(8,128)(2,1)S(1)}, bf16[512,128]{0,1:T(8,128)(2,1)S(1)}, u32[]{:S(2)}, u32[]{:S(2)}) collective-permute-start(bf16[512,128]{0,1:T(8,128)(2,1)S(1)} %collective-permute-done.3), channel_id=1, source_target_pairs={{16,0},{32,16},{48,32},{64,48},{80,64},{96,80},{112,96},{128,112},... | collective-permute-start | bytes 393224 | tf_op jit(solution)/shard_map/ppermute | solution.py:19
  88.3 0.8 collective-permute-done.5
  93.3 0.8 reshape.574
  94.0 7.2 %all-to-all-start = ((bf16[16,2,1024]{2,1,0:T(2,128)(2,1)}), bf16[16,2,1024]{2,1,0:T(2,128)(2,1)S(1)}, u32[]{:S(2)}, u32[]{:S(2)}) async-start(bf16[16,2,1024]{2,1,0:T(2,128)(2,1)} %reshape.574), calls=%async_computation | async-start | bytes 131072 | tf_op jit(solution)/shard_map/all_to_all | solution.py:212
  101.3 7.7 %all-to-all-done = bf16[16,2,1024]{2,1,0:T(2,128)(2,1)S(1)} async-done(((bf16[16,2,1024]{2,1,0:T(2,128)(2,1)}), bf16[16,2,1024]{2,1,0:T(2,128)(2,1)S(1)}, u32[]{:S(2)}, u32[]{:S(2)}) %all-to-all-start) | async-done | bytes 65568 | tf_op jit(solution)/shard_map/all_to_all | solution.py:212
  109.4 2.2 multiply_reduce_fusion
  111.9 0.5 broadcast.544
  112.4 0.7 reduce.28
  113.2 11.8 %all_to_all.29 = bf16[16,2,2048]{2,1,0:T(2,128)(2,1)S(1)} all-to-all(bf16[16,2,2048]{2,1,0:T(2,128)(2,1)S(1)} %reshape.576), channel_id=1, replica_groups=mesh['seq'=32,'exp'=16] {'exp'}, dimensions={0} | all-to-all | bytes 262144 | tf_op jit(solution)/shard_map/all_to_all | solution.py:238
  125.1 0.7 copy.23
  125.8 78.3 %all-gather.8.cloned.1.call-done = bf16[2048,1,1024]{2,0,1:T(8,128)(2,1)} async-done(((bf16[64,1,1024]{2,0,1:T(8,128)(2,1)}), bf16[2048,1,1024]{2,0,1:T(8,128)(2,1)}) %all-gather.8.cloned.1.call-update) | async-done | bytes 4194320 | tf_op jit(solution)/shard_map/all_gather | solution.py:239
  204.1 3.5 %fusion.4 = f32[2048,1,128]{2,0,1:T(8,128)S(1)} fusion(bf16[2048,1,1024]{2,0,1:T(8,128)(2,1)} %all-gather.8.cloned.1.call-done, bf16[1,1024,128]{2,1,0:T(8,128)(2,1)S(1)} %copy-done.3), kind=kOutput, calls=%fused_computation.5 | convolution fusion | flops 536870912 | bytes 5505024 | tf_op jit(solution)/shard_map/nek,ekf->nef/dot_general | solution.py:128
  207.6 8.3 %convolution_convert_fusion = bf16[2048,1024]{1,0:T(8,128)(2,1)} fusion(bf16[2048,1,1024]{2,0,1:T(8,128)(2,1)} %all-gather.8.cloned.1.call-done, f32[2048,1,128]{2,0,1:T(8,128)S(1)} %fusion.4, bf16[1,1024,128]{2,1,0:T(8,128)(2,1)S(1)} %copy-done, bf16[1,1024,128]{2,1,0:T(8,128)(2,1)S(1)} %copy-done.6), kind=kOutput, calls=%fused_computation.4 | convolution fusion | flops 1077411840 | bytes 9961472 | tf_op jit(solution)/shard_map/nef,ekf->nek/dot_general | solution.py:131
  215.9 2.2 copy-done.1
  218.1 58.9 %shard_map.127 = bf16[64,1024]{1,0:T(8,128)(2,1)S(1)} custom-call(bf16[4,8,64,1024]{3,2,1,0:T(8,128)(2,1)S(1)} %bitcast.132), custom_call_target="tpu_custom_call" | custom-call | tf_op jit(solution)/shard_map/pallas_call | solution.py:100
  277.0 0.7 reduce.29
  277.8 25.9 %all_to_all.30 = bf16[16,2,2048]{2,1,0:T(2,128)(2,1)S(1)} all-to-all(bf16[16,2,2048]{2,1,0:T(2,128)(2,1)S(1)} %reshape.578), channel_id=1, replica_groups=mesh['seq'=32,'exp'=16] {'exp'}, dimensions={0} | all-to-all | bytes 262144 | tf_op jit(solution)/shard_map/all_to_all | solution.py:246
  303.8 0.8 fusion.37
  (58 shorter events, 7.7 us)
Async XLA Ops:
  6.5 201.1 %copy-start = (bf16[1,1024,128]{2,1,0:T(8,128)(2,1)S(1)}, bf16[1,1024,128]{2,1,0:T(8,128)(2,1)}, u32[]{:S(2)}) copy-start(bf16[1,1024,128]{2,1,0:T(8,128)(2,1)} %param.25) | copy-start | bytes 786436
  6.5 50.8 %all-gather.4.cloned.1.call-start = ((), (), s32[]{:S(2)}) async-start(), calls=%async_computation.3 | async-start | bytes 1114112 | tf_op jit(solution)/shard_map/all_gather | solution.py:160
  9.1 100.3 %all-gather.6.cloned.1.call-start = ((), (), s32[]{:S(2)}) async-start(), calls=%async_computation.4 | async-start | bytes 2228224 | tf_op jit(solution)/shard_map/all_gather | solution.py:215
  59.2 10.1 %collective-permute-start = (bf16[512,128]{0,1:T(8,128)(2,1)S(1)}, bf16[512,128]{0,1:T(8,128)(2,1)S(1)}, u32[]{:S(2)}, u32[]{:S(2)}) collective-permute-start(bf16[512,128]{0,1:T(8,128)(2,1)S(1)} %slice.69), channel_id=1, source_target_pairs={{496,0},{0,16},{16,32},{32,48},{48,64},{64,80},{80,96},{96,112},{1... | collective-permute-start | bytes 393224 | tf_op jit(solution)/shard_map/ppermute | solution.py:19
  62.3 8.8 %collective-permute-start.1 = (bf16[512,128]{0,1:T(8,128)(2,1)S(1)}, bf16[512,128]{0,1:T(8,128)(2,1)S(1)}, u32[]{:S(2)}, u32[]{:S(2)}) collective-permute-start(bf16[512,128]{0,1:T(8,128)(2,1)S(1)} %slice.69), channel_id=1, source_target_pairs={{16,0},{32,16},{48,32},{64,48},{80,64},{96,80},{112,96},{128,112},... | collective-permute-start | bytes 393224 | tf_op jit(solution)/shard_map/ppermute | solution.py:19
  69.2 9.3 %collective-permute-start.2 = (bf16[512,128]{0,1:T(8,128)(2,1)S(1)}, bf16[512,128]{0,1:T(8,128)(2,1)S(1)}, u32[]{:S(2)}, u32[]{:S(2)}) collective-permute-start(bf16[512,128]{0,1:T(8,128)(2,1)S(1)} %collective-permute-done), channel_id=1, source_target_pairs={{496,0},{0,16},{16,32},{32,48},{48,64},{64,80},{80,96},{96,112},{1... | collective-permute-start | bytes 393224 | tf_op jit(solution)/shard_map/ppermute | solution.py:19
  71.2 9.4 %collective-permute-start.3 = (bf16[512,128]{0,1:T(8,128)(2,1)S(1)}, bf16[512,128]{0,1:T(8,128)(2,1)S(1)}, u32[]{:S(2)}, u32[]{:S(2)}) collective-permute-start(bf16[512,128]{0,1:T(8,128)(2,1)S(1)} %collective-permute-done.1), channel_id=1, source_target_pairs={{16,0},{32,16},{48,32},{64,48},{80,64},{96,80},{112,96},{128,112},... | collective-permute-start | bytes 393224 | tf_op jit(solution)/shard_map/ppermute | solution.py:19
  78.6 9.3 %collective-permute-start.4 = (bf16[512,128]{0,1:T(8,128)(2,1)S(1)}, bf16[512,128]{0,1:T(8,128)(2,1)S(1)}, u32[]{:S(2)}, u32[]{:S(2)}) collective-permute-start(bf16[512,128]{0,1:T(8,128)(2,1)S(1)} %collective-permute-done.2), channel_id=1, source_target_pairs={{496,0},{0,16},{16,32},{32,48},{48,64},{64,80},{80,96},{96,112},{1... | collective-permute-start | bytes 393224 | tf_op jit(solution)/shard_map/ppermute | solution.py:19
  80.5 8.6 %collective-permute-start.5 = (bf16[512,128]{0,1:T(8,128)(2,1)S(1)}, bf16[512,128]{0,1:T(8,128)(2,1)S(1)}, u32[]{:S(2)}, u32[]{:S(2)}) collective-permute-start(bf16[512,128]{0,1:T(8,128)(2,1)S(1)} %collective-permute-done.3), channel_id=1, source_target_pairs={{16,0},{32,16},{48,32},{64,48},{80,64},{96,80},{112,96},{128,112},... | collective-permute-start | bytes 393224 | tf_op jit(solution)/shard_map/ppermute | solution.py:19
  91.3 10.0 %copy-start.5 = (s32[32]{0:T(128)S(1)}, s32[32]{0:T(128)}, u32[]{:S(2)}) copy-start(s32[32]{0:T(128)} %param.14) | copy-start | bytes 388
  91.8 17.7 %copy-start.2 = (bf16[32,1024]{1,0:T(8,128)(2,1)S(1)}, bf16[32,1024]{1,0:T(8,128)(2,1)}, u32[]{:S(2)}) copy-start(bf16[32,1024]{1,0:T(8,128)(2,1)} %param.13) | copy-start | bytes 196612
  92.1 19.5 %copy-start.4 = (f32[1024]{0:T(1024)S(1)}, f32[1024]{0:T(1024)}, u32[]{:S(2)}) copy-start(f32[1024]{0:T(1024)} %param.22) | copy-start | bytes 12292
  92.5 111.7 %copy-start.3 = (bf16[1,1024,128]{2,1,0:T(8,128)(2,1)S(1)}, bf16[1,1024,128]{2,1,0:T(8,128)(2,1)}, u32[]{:S(2)}) copy-start(bf16[1,1024,128]{2,1,0:T(8,128)(2,1)} %param.23) | copy-start | bytes 786436
  94.0 15.0 %all-to-all-start = ((bf16[16,2,1024]{2,1,0:T(2,128)(2,1)}), bf16[16,2,1024]{2,1,0:T(2,128)(2,1)S(1)}, u32[]{:S(2)}, u32[]{:S(2)}) async-start(bf16[16,2,1024]{2,1,0:T(2,128)(2,1)} %reshape.574), calls=%async_computation | async-start | bytes 131072 | tf_op jit(solution)/shard_map/all_to_all | solution.py:212
  101.2 102.9 %all-gather.8.cloned.1.call-start = ((), (), s32[]{:S(2)}) async-start(), calls=%async_computation.5 | async-start | bytes 4325376 | tf_op jit(solution)/shard_map/all_gather | solution.py:239
  111.9 95.7 %copy-start.6 = (bf16[1,1024,128]{2,1,0:T(8,128)(2,1)S(1)}, bf16[1,1024,128]{2,1,0:T(8,128)(2,1)}, u32[]{:S(2)}) copy-start(bf16[1,1024,128]{2,1,0:T(8,128)(2,1)} %param.24) | copy-start | bytes 786436
  215.9 2.2 copy-start.1
Sparse Core Ops, SparseCore 0:
  9.5 47.8 all-gather.3
  59.5 41.1 all-gather.5
  125.9 78.1 all-gather.7

commit v3 on v2

--- a/solution.py
+++ b/solution.py
@@ -197,13 +197,11 @@
         jnp.zeros((block_len, heads_dev, head_size), jnp.float32),
     )
     state = attend(start_state, key_value, position)
-    lower = key_value
-    upper = key_value
+    lowers = [passed_along(key_value, "seq", d) for d in range(1, REACH + 1)]
+    uppers = [passed_along(key_value, "seq", -d) for d in range(1, REACH + 1)]
     for distance in range(1, REACH + 1):
-        lower = passed_along(lower, "seq", 1)
-        upper = passed_along(upper, "seq", -1)
-        state = attend(state, lower, (position - distance) % n_blocks)
-        state = attend(state, upper, (position + distance) % n_blocks)
+        state = attend(state, lowers[distance - 1], (position - distance) % n_blocks)
+        state = attend(state, uppers[distance - 1], (position + distance) % n_blocks)
     heads_out = (
         (state[2] / jnp.transpose(state[1])[:, :, None])
         .astype(jnp.bfloat16)

time: 312 us -> 316 us (1.013)
  waiting for transfers between devices: 128 us -> 135 us
  starting transfers between devices: 33.1 us -> 29.9 us
    ppermute x6, waiting for transfers between devices: 1.68 us -> 7.61 us  [passed_along(): return lax.ppermute(block, axis, route)]
where the time goes in v3:
time: 316 us
  waiting for transfers between devices  135 us (43%)
  Pallas kernels  59 us (19%)
  blocking collectives  37.6 us (12%)
  starting transfers between devices  29.9 us (9%)
  matrix products  21.5 us (7%)
  between operations  18.5 us (6%)
  other arithmetic  7.14 us (2%)
  local copies, waits for them, and re-layouts  6.73 us (2%)
    all_gather x1, waiting for transfers between devices, local(): gathered = lax.all_gather(arrived, 'seq', axis=0, tiled=True)  80 us
    pallas_call x1, Pallas kernels, ring_reduce(): pl.pallas_call(functools.partial(ring_reduce_kernel, nx, ny), out_shape=j...  59 us
    all_gather x1, waiting for transfers between devices, local(): lax.all_gather(normed_attn, 'exp', axis=0, tiled=True)  39.2 us
    all_to_all x1, blocking collectives, local(): lax.all_to_all(summed, 'exp', split_axis=0, concat_axis=0, tiled=True)  25.8 us
    ppermute x6, starting transfers between devices, passed_along(): return lax.ppermute(block, axis, route)  24.9 us
    all_to_all x1, blocking collectives, local(): lax.all_to_all(outgoing, 'exp', split_axis=0, concat_axis=0, tiled=True)  11.8 us
    dot_general x1, matrix products, expert_terms(): jnp.einsum('nef,ekf->nek', act, down_slice, preferred_element_type=jnp.fl...  8.28 us
    all_to_all x1, waiting for transfers between devices, local(): lax.all_to_all(heads_out, 'exp', split_axis=0, concat_axis=1, tiled=True)  7.74 us
  transfers between devices with their start and end apart: 10, of which 5 were waited for; matrix products, arithmetic and copies ran while one was open for 4% of the time, Pallas kernels for 0%

profile of v3, /device:TPU:1, one launch (start us, length us, event | category | flops | bytes accessed | tf_op | source)
XLA Modules:
  0.0 315.6 jit_solution(6180598611201459749)
XLA Ops:
  6.5 1.0 fusion.96
  7.6 1.6 fusion.98
  9.2 0.7 all-gather.6.cloned.1.call-update
  10.6 1.6 fusion.136
  16.6 0.7 fusion.126
  17.4 0.8 select_reduce_fusion
  18.2 39.2 %all-gather.4.cloned.1.call-done = bf16[512,1024]{1,0:T(8,128)(2,1)} async-done(((bf16[32,1024]{1,0:T(8,128)(2,1)}), bf16[512,1024]{1,0:T(8,128)(2,1)}) %all-gather.4.cloned.1.call-update) | async-done | bytes 1048592 | tf_op jit(solution)/shard_map/all_gather | solution.py:160
  57.4 1.8 convolution_convert_fusion.1
  59.2 5.0 %collective-permute-start.4 = (bf16[512,128]{0,1:T(8,128)(2,1)S(1)}, bf16[512,128]{0,1:T(8,128)(2,1)S(1)}, u32[]{:S(2)}, u32[]{:S(2)}) collective-permute-start(bf16[512,128]{0,1:T(8,128)(2,1)S(1)} %slice.69), channel_id=1, source_target_pairs={{464,0},{480,16},{496,32},{0,48},{16,64},{32,80},{48,96},{64,112},... | collective-permute-start | bytes 393224 | tf_op jit(solution)/shard_map/ppermute | solution.py:19
  64.2 5.5 %collective-permute-start.3 = (bf16[512,128]{0,1:T(8,128)(2,1)S(1)}, bf16[512,128]{0,1:T(8,128)(2,1)S(1)}, u32[]{:S(2)}, u32[]{:S(2)}) collective-permute-start(bf16[512,128]{0,1:T(8,128)(2,1)S(1)} %slice.69), channel_id=1, source_target_pairs={{32,0},{48,16},{64,32},{80,48},{96,64},{112,80},{128,96},{144,112}... | collective-permute-start | bytes 393224 | tf_op jit(solution)/shard_map/ppermute | solution.py:19
  69.6 1.9 collective-permute-start.2
  71.6 7.6 %collective-permute-start.1 = (bf16[512,128]{0,1:T(8,128)(2,1)S(1)}, bf16[512,128]{0,1:T(8,128)(2,1)S(1)}, u32[]{:S(2)}, u32[]{:S(2)}) collective-permute-start(bf16[512,128]{0,1:T(8,128)(2,1)S(1)} %slice.69), channel_id=1, source_target_pairs={{16,0},{32,16},{48,32},{64,48},{80,64},{96,80},{112,96},{128,112},... | collective-permute-start | bytes 393224 | tf_op jit(solution)/shard_map/ppermute | solution.py:19
  79.2 1.9 collective-permute-start
  81.7 3.1 collective-permute-start.5
  86.3 1.9 collective-permute-done
  88.6 5.7 %collective-permute-done.5 = bf16[512,128]{0,1:T(8,128)(2,1)S(1)} collective-permute-done((bf16[512,128]{0,1:T(8,128)(2,1)S(1)}, bf16[512,128]{0,1:T(8,128)(2,1)S(1)}, u32[]{:S(2)}, u32[]{:S(2)}) %collective-permute-start.5) | collective-permute-done | bytes 131104 | tf_op jit(solution)/shard_map/ppermute | solution.py:19
  98.4 0.8 reshape.574
  99.1 4.9 %all-to-all-start = ((bf16[16,2,1024]{2,1,0:T(2,128)(2,1)}), bf16[16,2,1024]{2,1,0:T(2,128)(2,1)S(1)}, u32[]{:S(2)}, u32[]{:S(2)}) async-start(bf16[16,2,1024]{2,1,0:T(2,128)(2,1)} %reshape.574), calls=%async_computation | async-start | bytes 131072 | tf_op jit(solution)/shard_map/all_to_all | solution.py:210
  104.1 7.7 %all-to-all-done = bf16[16,2,1024]{2,1,0:T(2,128)(2,1)S(1)} async-done(((bf16[16,2,1024]{2,1,0:T(2,128)(2,1)}), bf16[16,2,1024]{2,1,0:T(2,128)(2,1)S(1)}, u32[]{:S(2)}, u32[]{:S(2)}) %all-to-all-start) | async-done | bytes 65568 | tf_op jit(solution)/shard_map/all_to_all | solution.py:210
  112.2 2.2 multiply_reduce_fusion
  114.7 0.5 broadcast.544
  115.2 0.7 reduce.28
  116.0 11.8 %all_to_all.29 = bf16[16,2,2048]{2,1,0:T(2,128)(2,1)S(1)} all-to-all(bf16[16,2,2048]{2,1,0:T(2,128)(2,1)S(1)} %reshape.576), channel_id=1, replica_groups=mesh['seq'=32,'exp'=16] {'exp'}, dimensions={0} | all-to-all | bytes 262144 | tf_op jit(solution)/shard_map/all_to_all | solution.py:236
  127.9 0.7 copy.23
  128.6 80.0 %all-gather.8.cloned.1.call-done = bf16[2048,1,1024]{2,0,1:T(8,128)(2,1)} async-done(((bf16[64,1,1024]{2,0,1:T(8,128)(2,1)}), bf16[2048,1,1024]{2,0,1:T(8,128)(2,1)}) %all-gather.8.cloned.1.call-update) | async-done | bytes 4194320 | tf_op jit(solution)/shard_map/all_gather | solution.py:237
  208.6 3.5 %fusion.4 = f32[2048,1,128]{2,0,1:T(8,128)S(1)} fusion(bf16[2048,1,1024]{2,0,1:T(8,128)(2,1)} %all-gather.8.cloned.1.call-done, bf16[1,1024,128]{2,1,0:T(8,128)(2,1)S(1)} %copy-done.3), kind=kOutput, calls=%fused_computation.5 | convolution fusion | flops 536870912 | bytes 5505024 | tf_op jit(solution)/shard_map/nek,ekf->nef/dot_general | solution.py:128
  212.1 8.3 %convolution_convert_fusion = bf16[2048,1024]{1,0:T(8,128)(2,1)} fusion(bf16[2048,1,1024]{2,0,1:T(8,128)(2,1)} %all-gather.8.cloned.1.call-done, f32[2048,1,128]{2,0,1:T(8,128)S(1)} %fusion.4, bf16[1,1024,128]{2,1,0:T(8,128)(2,1)S(1)} %copy-done, bf16[1,1024,128]{2,1,0:T(8,128)(2,1)S(1)} %copy-done.6), kind=kOutput, calls=%fused_computation.4 | convolution fusion | flops 1077411840 | bytes 9961472 | tf_op jit(solution)/shard_map/nef,ekf->nek/dot_general | solution.py:131
  220.3 2.2 copy-done.1
  222.5 59.0 %shard_map.127 = bf16[64,1024]{1,0:T(8,128)(2,1)S(1)} custom-call(bf16[4,8,64,1024]{3,2,1,0:T(8,128)(2,1)S(1)} %bitcast.132), custom_call_target="tpu_custom_call" | custom-call | tf_op jit(solution)/shard_map/pallas_call | solution.py:100
  281.5 0.7 reduce.29
  282.3 25.8 %all_to_all.30 = bf16[16,2,2048]{2,1,0:T(2,128)(2,1)S(1)} all-to-all(bf16[16,2,2048]{2,1,0:T(2,128)(2,1)S(1)} %reshape.578), channel_id=1, replica_groups=mesh['seq'=32,'exp'=16] {'exp'}, dimensions={0} | all-to-all | bytes 262144 | tf_op jit(solution)/shard_map/all_to_all | solution.py:244
  308.2 0.8 fusion.37
  (58 shorter events, 7.7 us)
Async XLA Ops:
  6.5 205.5 %copy-start = (bf16[1,1024,128]{2,1,0:T(8,128)(2,1)S(1)}, bf16[1,1024,128]{2,1,0:T(8,128)(2,1)}, u32[]{:S(2)}) copy-start(bf16[1,1024,128]{2,1,0:T(8,128)(2,1)} %param.25) | copy-start | bytes 786436
  6.5 50.8 %all-gather.4.cloned.1.call-start = ((), (), s32[]{:S(2)}) async-start(), calls=%async_computation.3 | async-start | bytes 1114112 | tf_op jit(solution)/shard_map/all_gather | solution.py:160
  9.1 103.1 %all-gather.6.cloned.1.call-start = ((), (), s32[]{:S(2)}) async-start(), calls=%async_computation.4 | async-start | bytes 2228224 | tf_op jit(solution)/shard_map/all_gather | solution.py:213
  59.2 22.5 %collective-permute-start.4 = (bf16[512,128]{0,1:T(8,128)(2,1)S(1)}, bf16[512,128]{0,1:T(8,128)(2,1)S(1)}, u32[]{:S(2)}, u32[]{:S(2)}) collective-permute-start(bf16[512,128]{0,1:T(8,128)(2,1)S(1)} %slice.69), channel_id=1, source_target_pairs={{464,0},{480,16},{496,32},{0,48},{16,64},{32,80},{48,96},{64,112},... | collective-permute-start | bytes 393224 | tf_op jit(solution)/shard_map/ppermute | solution.py:19
  64.2 21.0 %collective-permute-start.3 = (bf16[512,128]{0,1:T(8,128)(2,1)S(1)}, bf16[512,128]{0,1:T(8,128)(2,1)S(1)}, u32[]{:S(2)}, u32[]{:S(2)}) collective-permute-start(bf16[512,128]{0,1:T(8,128)(2,1)S(1)} %slice.69), channel_id=1, source_target_pairs={{32,0},{48,16},{64,32},{80,48},{96,64},{112,80},{128,96},{144,112}... | collective-permute-start | bytes 393224 | tf_op jit(solution)/shard_map/ppermute | solution.py:19
  69.6 15.9 %collective-permute-start.2 = (bf16[512,128]{0,1:T(8,128)(2,1)S(1)}, bf16[512,128]{0,1:T(8,128)(2,1)S(1)}, u32[]{:S(2)}, u32[]{:S(2)}) collective-permute-start(bf16[512,128]{0,1:T(8,128)(2,1)S(1)} %slice.69), channel_id=1, source_target_pairs={{480,0},{496,16},{0,32},{16,48},{32,64},{48,80},{64,96},{80,112},{... | collective-permute-start | bytes 393224 | tf_op jit(solution)/shard_map/ppermute | solution.py:19
  71.6 14.3 %collective-permute-start.1 = (bf16[512,128]{0,1:T(8,128)(2,1)S(1)}, bf16[512,128]{0,1:T(8,128)(2,1)S(1)}, u32[]{:S(2)}, u32[]{:S(2)}) collective-permute-start(bf16[512,128]{0,1:T(8,128)(2,1)S(1)} %slice.69), channel_id=1, source_target_pairs={{16,0},{32,16},{48,32},{64,48},{80,64},{96,80},{112,96},{128,112},... | collective-permute-start | bytes 393224 | tf_op jit(solution)/shard_map/ppermute | solution.py:19
  79.2 9.0 %collective-permute-start = (bf16[512,128]{0,1:T(8,128)(2,1)S(1)}, bf16[512,128]{0,1:T(8,128)(2,1)S(1)}, u32[]{:S(2)}, u32[]{:S(2)}) collective-permute-start(bf16[512,128]{0,1:T(8,128)(2,1)S(1)} %slice.69), channel_id=1, source_target_pairs={{496,0},{0,16},{16,32},{32,48},{48,64},{64,80},{80,96},{96,112},{1... | collective-permute-start | bytes 393224 | tf_op jit(solution)/shard_map/ppermute | solution.py:19
  81.7 12.5 %collective-permute-start.5 = (bf16[512,128]{0,1:T(8,128)(2,1)S(1)}, bf16[512,128]{0,1:T(8,128)(2,1)S(1)}, u32[]{:S(2)}, u32[]{:S(2)}) collective-permute-start(bf16[512,128]{0,1:T(8,128)(2,1)S(1)} %slice.69), channel_id=1, source_target_pairs={{48,0},{64,16},{80,32},{96,48},{112,64},{128,80},{144,96},{160,112... | collective-permute-start | bytes 393224 | tf_op jit(solution)/shard_map/ppermute | solution.py:19
  96.6 7.5 %copy-start.5 = (s32[32]{0:T(128)S(1)}, s32[32]{0:T(128)}, u32[]{:S(2)}) copy-start(s32[32]{0:T(128)} %param.14) | copy-start | bytes 388
  96.6 15.6 %copy-start.2 = (bf16[32,1024]{1,0:T(8,128)(2,1)S(1)}, bf16[32,1024]{1,0:T(8,128)(2,1)}, u32[]{:S(2)}) copy-start(bf16[32,1024]{1,0:T(8,128)(2,1)} %param.13) | copy-start | bytes 196612
  97.1 17.4 %copy-start.4 = (f32[1024]{0:T(1024)S(1)}, f32[1024]{0:T(1024)}, u32[]{:S(2)}) copy-start(f32[1024]{0:T(1024)} %param.22) | copy-start | bytes 12292
  97.9 110.7 %copy-start.3 = (bf16[1,1024,128]{2,1,0:T(8,128)(2,1)S(1)}, bf16[1,1024,128]{2,1,0:T(8,128)(2,1)}, u32[]{:S(2)}) copy-start(bf16[1,1024,128]{2,1,0:T(8,128)(2,1)} %param.23) | copy-start | bytes 786436
  99.1 12.7 %all-to-all-start = ((bf16[16,2,1024]{2,1,0:T(2,128)(2,1)}), bf16[16,2,1024]{2,1,0:T(2,128)(2,1)S(1)}, u32[]{:S(2)}, u32[]{:S(2)}) async-start(bf16[16,2,1024]{2,1,0:T(2,128)(2,1)} %reshape.574), calls=%async_computation | async-start | bytes 131072 | tf_op jit(solution)/shard_map/all_to_all | solution.py:210
  104.0 104.5 %all-gather.8.cloned.1.call-start = ((), (), s32[]{:S(2)}) async-start(), calls=%async_computation.5 | async-start | bytes 4325376 | tf_op jit(solution)/shard_map/all_gather | solution.py:237
  114.7 97.4 %copy-start.6 = (bf16[1,1024,128]{2,1,0:T(8,128)(2,1)S(1)}, bf16[1,1024,128]{2,1,0:T(8,128)(2,1)}, u32[]{:S(2)}) copy-start(bf16[1,1024,128]{2,1,0:T(8,128)(2,1)} %param.24) | copy-start | bytes 786436
  220.3 2.2 copy-start.1
Sparse Core Ops, SparseCore 0:
  9.5 47.8 all-gather.3
  59.5 41.3 all-gather.5
  128.7 79.8 all-gather.7

commit v4 on v3

--- a/solution.py
+++ b/solution.py
@@ -117,6 +117,81 @@
             collective_id=1, has_side_effects=True, vmem_limit_bytes=48 * 1024 * 1024
         ),
     )(part)
+
+
+def shift_exchange_kernel(offsets, axis, other, block_ref, out_ref, send_sems, recv_sems):
+    n = lax.axis_size(axis)
+    me = lax.axis_index(axis)
+    col = lax.axis_index(other)
+
+    def dev(peer):
+        return (peer, col) if axis == "seq" else (col, peer)
+
+    targets = [(me + o + n * len(offsets)) % n for o in offsets]
+    barrier = pltpu.get_barrier_semaphore()
+    for peer in targets:
+        pl.semaphore_signal(barrier, inc=1, device_id=dev(peer),
+                            device_id_type=pl.DeviceIdType.MESH)
+    pl.semaphore_wait(barrier, len(offsets))
+    copies = []
+    for j, peer in enumerate(targets):
+        cp = pltpu.make_async_remote_copy(
+            src_ref=block_ref, dst_ref=out_ref.at[j],
+            send_sem=send_sems.at[j], recv_sem=recv_sems.at[j],
+            device_id=dev(peer), device_id_type=pl.DeviceIdType.MESH)
+        cp.start()
+        copies.append(cp)
+    for cp in copies:
+        cp.wait()
+
+
+def shift_exchange(block, offsets, axis, other, cid):
+    vmem = pltpu.MemorySpace.VMEM
+    k = len(offsets)
+    return pl.pallas_call(
+        functools.partial(shift_exchange_kernel, tuple(offsets), axis, other),
+        out_shape=jax.ShapeDtypeStruct((k,) + block.shape, block.dtype),
+        in_specs=[pl.BlockSpec(memory_space=vmem)],
+        out_specs=pl.BlockSpec(memory_space=vmem),
+        scratch_shapes=[pltpu.SemaphoreType.DMA((k,)), pltpu.SemaphoreType.DMA((k,))],
+        compiler_params=pltpu.CompilerParams(collective_id=cid, has_side_effects=True),
+    )(block)
+
+
+def exp_all_to_all_kernel(x_ref, y_ref, send_sems, recv_sems):
+    n = lax.axis_size("exp")
+    me = lax.axis_index("exp")
+    row = lax.axis_index("seq")
+    barrier = pltpu.get_barrier_semaphore()
+    for k in range(1, n):
+        pl.semaphore_signal(barrier, inc=1, device_id=(row, (me + k) % n),
+                            device_id_type=pl.DeviceIdType.MESH)
+    pl.semaphore_wait(barrier, n - 1)
+    copies = []
+    for k in range(1, n):
+        peer = (me + k) % n
+        cp = pltpu.make_async_remote_copy(
+            src_ref=x_ref.at[peer], dst_ref=y_ref.at[me],
+            send_sem=send_sems.at[k - 1], recv_sem=recv_sems.at[k - 1],
+            device_id=(row, peer), device_id_type=pl.DeviceIdType.MESH)
+        cp.start()
+        copies.append(cp)
+    y_ref[me] = x_ref[me]
+    for cp in copies:
+        cp.wait()
+
+
+def exp_all_to_all(x, cid):
+    n = x.shape[0]
+    vmem = pltpu.MemorySpace.VMEM
+    return pl.pallas_call(
+        exp_all_to_all_kernel,
+        out_shape=jax.ShapeDtypeStruct(x.shape, x.dtype),
+        in_specs=[pl.BlockSpec(memory_space=vmem)],
+        out_specs=pl.BlockSpec(memory_space=vmem),
+        scratch_shapes=[pltpu.SemaphoreType.DMA((n - 1,)), pltpu.SemaphoreType.DMA((n - 1,))],
+        compiler_params=pltpu.CompilerParams(collective_id=cid, has_side_effects=True),
+    )(x)
 
 
 def rms_scale(matrix, gain):
@@ -197,11 +272,11 @@
         jnp.zeros((block_len, heads_dev, head_size), jnp.float32),
     )
     state = attend(start_state, key_value, position)
-    lowers = [passed_along(key_value, "seq", d) for d in range(1, REACH + 1)]
-    uppers = [passed_along(key_value, "seq", -d) for d in range(1, REACH + 1)]
+    offsets = [d for d in range(1, REACH + 1)] + [-d for d in range(1, REACH + 1)]
+    neighbours = shift_exchange(key_value, offsets, "seq", "exp", 2)
     for distance in range(1, REACH + 1):
-        state = attend(state, lowers[distance - 1], (position - distance) % n_blocks)
-        state = attend(state, uppers[distance - 1], (position + distance) % n_blocks)
+        state = attend(state, neighbours[distance - 1], (position - distance) % n_blocks)
+        state = attend(state, neighbours[REACH + distance - 1], (position + distance) % n_blocks)
     heads_out = (
         (state[2] / jnp.transpose(state[1])[:, :, None])
         .astype(jnp.bfloat16)

time: 316 us -> 311 us (0.984)
  Pallas kernels: 59 us -> 85 us
  starting transfers between devices: 29.9 us -> 5.69 us
  waiting for transfers between devices: 135 us -> 126 us
    pallas_call x0 -> x1, Pallas kernels: none -> 26.1 us  [shift_exchange(): pl.pallas_call(functools.partial(shift_exchange_kernel, tuple(offsets), a...]
    ppermute x6 -> x0, starting transfers between devices: 24.9 us -> none  [passed_along(): return lax.ppermute(block, axis, route)]
    ppermute x6 -> x0, waiting for transfers between devices: 7.61 us -> none  [passed_along(): return lax.ppermute(block, axis, route)]
  transfers between devices with their start and end apart: 10 -> 4, of which waited for: 5 -> 3; matrix products, arithmetic and copies ran while one was open for 4% -> 5% of each run, Pallas kernels for 0% -> 8%
where the time goes in v4:
time: 311 us; the launch traced here: 310 us
  waiting for transfers between devices  126 us (41%)
  Pallas kernels  85 us (27%)
  blocking collectives  37.7 us (12%)
  matrix products  21.4 us (7%)
  between operations  18.4 us (6%)
  local copies, waits for them, and re-layouts  8.74 us (3%)
  other arithmetic  7.13 us (2%)
  starting transfers between devices  5.69 us (2%)
    all_gather x1, waiting for transfers between devices, local(): gathered = lax.all_gather(arrived, 'seq', axis=0, tiled=True)  78.3 us
    pallas_call x1, Pallas kernels, ring_reduce(): pl.pallas_call(functools.partial(ring_reduce_kernel, nx, ny), out_shape=j...  58.9 us
    all_gather x1, waiting for transfers between devices, local(): lax.all_gather(normed_attn, 'exp', axis=0, tiled=True)  39.2 us
    pallas_call x1, Pallas kernels, shift_exchange(): pl.pallas_call(functools.partial(shift_exchange_kernel, tuple(offsets), a...  26.1 us
    all_to_all x1, blocking collectives, local(): lax.all_to_all(summed, 'exp', split_axis=0, concat_axis=0, tiled=True)  25.9 us
    all_to_all x1, blocking collectives, local(): lax.all_to_all(outgoing, 'exp', split_axis=0, concat_axis=0, tiled=True)  11.8 us
    dot_general x1, matrix products, expert_terms(): jnp.einsum('nef,ekf->nek', act, down_slice, preferred_element_type=jnp.fl...  8.28 us
    all_to_all x1, waiting for transfers between devices, local(): lax.all_to_all(heads_out, 'exp', split_axis=0, concat_axis=1, tiled=True)  7.74 us
  transfers between devices with their start and end apart: 4, of which 3 were waited for; matrix products, arithmetic and copies ran while one was open for 5% of the time, Pallas kernels for 8%

profile of v4, /device:TPU:1, one launch (start us, length us, event | category | flops | bytes accessed | tf_op | source)
XLA Modules:
  0.0 310.1 jit_solution(11286228432906377359)
XLA Ops:
  6.5 1.0 fusion.96
  7.6 1.6 fusion.98
  9.2 0.7 all-gather.6.cloned.1.call-update
  10.6 1.6 fusion.136
  16.6 0.7 fusion.126
  17.4 0.8 select_reduce_fusion
  18.2 39.2 %all-gather.4.cloned.1.call-done = bf16[512,1024]{1,0:T(8,128)(2,1)} async-done(((bf16[32,1024]{1,0:T(8,128)(2,1)}), bf16[512,1024]{1,0:T(8,128)(2,1)}) %all-gather.4.cloned.1.call-update) | async-done | bytes 1048592 | tf_op jit(solution)/shard_map/all_gather | solution.py:235
  57.4 1.8 convolution_convert_fusion.1
  59.1 0.8 slice.93.block_ref
  60.2 26.1 %shard_map.127 = bf16[6,512,128]{2,1,0:T(8,128)(2,1)} custom-call(bf16[512,128]{1,0:T(8,128)(2,1)} %slice.93.block_ref), custom_call_target="tpu_custom_call" | custom-call | tf_op jit(solution)/shard_map/pallas_call | solution.py:151
  86.4 1.3 slice_bitcast_fusion.5
  91.6 0.4 fusion.46
  92.0 0.4 fusion.50
  92.5 0.4 fusion.54
  92.9 0.4 fusion.35
  93.3 0.4 fusion.38
  93.8 0.8 reshape.574
  94.6 5.6 %all-to-all-start = ((bf16[16,2,1024]{2,1,0:T(2,128)(2,1)}), bf16[16,2,1024]{2,1,0:T(2,128)(2,1)S(1)}, u32[]{:S(2)}, u32[]{:S(2)}) async-start(bf16[16,2,1024]{2,1,0:T(2,128)(2,1)} %reshape.574), calls=%async_computation | async-start | bytes 131072 | tf_op jit(solution)/shard_map/all_to_all | solution.py:285
  100.2 7.7 %all-to-all-done = bf16[16,2,1024]{2,1,0:T(2,128)(2,1)S(1)} async-done(((bf16[16,2,1024]{2,1,0:T(2,128)(2,1)}), bf16[16,2,1024]{2,1,0:T(2,128)(2,1)S(1)}, u32[]{:S(2)}, u32[]{:S(2)}) %all-to-all-start) | async-done | bytes 65568 | tf_op jit(solution)/shard_map/all_to_all | solution.py:285
  108.4 2.2 multiply_reduce_fusion
  110.8 0.5 broadcast.544
  111.4 0.7 reduce.28
  112.1 11.8 %all_to_all.29 = bf16[16,2,2048]{2,1,0:T(2,128)(2,1)S(1)} all-to-all(bf16[16,2,2048]{2,1,0:T(2,128)(2,1)S(1)} %reshape.576), channel_id=1, replica_groups=mesh['seq'=32,'exp'=16] {'exp'}, dimensions={0} | all-to-all | bytes 262144 | tf_op jit(solution)/shard_map/all_to_all | solution.py:311
  124.0 0.7 copy.27
  124.7 78.3 %all-gather.8.cloned.1.call-done = bf16[2048,1,1024]{2,0,1:T(8,128)(2,1)} async-done(((bf16[64,1,1024]{2,0,1:T(8,128)(2,1)}), bf16[2048,1,1024]{2,0,1:T(8,128)(2,1)}) %all-gather.8.cloned.1.call-update) | async-done | bytes 4194320 | tf_op jit(solution)/shard_map/all_gather | solution.py:312
  203.1 3.5 %fusion.4 = f32[2048,1,128]{2,0,1:T(8,128)S(1)} fusion(bf16[2048,1,1024]{2,0,1:T(8,128)(2,1)} %all-gather.8.cloned.1.call-done, bf16[1,1024,128]{2,1,0:T(8,128)(2,1)S(1)} %copy-done.3), kind=kOutput, calls=%fused_computation.5 | convolution fusion | flops 536870912 | bytes 5505024 | tf_op jit(solution)/shard_map/nek,ekf->nef/dot_general | solution.py:203
  206.6 8.3 %convolution_convert_fusion = bf16[2048,1024]{1,0:T(8,128)(2,1)} fusion(bf16[2048,1,1024]{2,0,1:T(8,128)(2,1)} %all-gather.8.cloned.1.call-done, f32[2048,1,128]{2,0,1:T(8,128)S(1)} %fusion.4, bf16[1,1024,128]{2,1,0:T(8,128)(2,1)S(1)} %copy-done, bf16[1,1024,128]{2,1,0:T(8,128)(2,1)S(1)} %copy-done.6), kind=kOutput, calls=%fused_computation.4 | convolution fusion | flops 1077411840 | bytes 9961472 | tf_op jit(solution)/shard_map/nef,ekf->nek/dot_general | solution.py:206
  214.8 2.2 copy-done.1
  217.0 58.9 %shard_map.128 = bf16[64,1024]{1,0:T(8,128)(2,1)S(1)} custom-call(bf16[4,8,64,1024]{3,2,1,0:T(8,128)(2,1)S(1)} %bitcast.144), custom_call_target="tpu_custom_call" | custom-call | tf_op jit(solution)/shard_map/pallas_call | solution.py:100
  275.9 0.7 reduce.29
  276.7 25.9 %all_to_all.30 = bf16[16,2,2048]{2,1,0:T(2,128)(2,1)S(1)} all-to-all(bf16[16,2,2048]{2,1,0:T(2,128)(2,1)S(1)} %reshape.578), channel_id=1, replica_groups=mesh['seq'=32,'exp'=16] {'exp'}, dimensions={0} | all-to-all | bytes 262144 | tf_op jit(solution)/shard_map/all_to_all | solution.py:319
  302.8 0.8 fusion.37
  (48 shorter events, 5.6 us)
Async XLA Ops:
  6.5 200.0 %copy-start = (bf16[1,1024,128]{2,1,0:T(8,128)(2,1)S(1)}, bf16[1,1024,128]{2,1,0:T(8,128)(2,1)}, u32[]{:S(2)}) copy-start(bf16[1,1024,128]{2,1,0:T(8,128)(2,1)} %param.25) | copy-start | bytes 786436
  6.5 50.8 %all-gather.4.cloned.1.call-start = ((), (), s32[]{:S(2)}) async-start(), calls=%async_computation.3 | async-start | bytes 1114112 | tf_op jit(solution)/shard_map/all_gather | solution.py:235
  9.1 99.2 %all-gather.6.cloned.1.call-start = ((), (), s32[]{:S(2)}) async-start(), calls=%async_computation.4 | async-start | bytes 2228224 | tf_op jit(solution)/shard_map/all_gather | solution.py:288
  92.0 8.2 %copy-start.5 = (s32[32]{0:T(128)S(1)}, s32[32]{0:T(128)}, u32[]{:S(2)}) copy-start(s32[32]{0:T(128)} %param.14) | copy-start | bytes 388
  92.0 16.4 %copy-start.2 = (bf16[32,1024]{1,0:T(8,128)(2,1)S(1)}, bf16[32,1024]{1,0:T(8,128)(2,1)}, u32[]{:S(2)}) copy-start(bf16[32,1024]{1,0:T(8,128)(2,1)} %param.13) | copy-start | bytes 196612
  92.9 17.7 %copy-start.4 = (f32[1024]{0:T(1024)S(1)}, f32[1024]{0:T(1024)}, u32[]{:S(2)}) copy-start(f32[1024]{0:T(1024)} %param.22) | copy-start | bytes 12292
  93.3 109.8 %copy-start.3 = (bf16[1,1024,128]{2,1,0:T(8,128)(2,1)S(1)}, bf16[1,1024,128]{2,1,0:T(8,128)(2,1)}, u32[]{:S(2)}) copy-start(bf16[1,1024,128]{2,1,0:T(8,128)(2,1)} %param.23) | copy-start | bytes 786436
  94.6 13.4 %all-to-all-start = ((bf16[16,2,1024]{2,1,0:T(2,128)(2,1)}), bf16[16,2,1024]{2,1,0:T(2,128)(2,1)S(1)}, u32[]{:S(2)}, u32[]{:S(2)}) async-start(bf16[16,2,1024]{2,1,0:T(2,128)(2,1)} %reshape.574), calls=%async_computation | async-start | bytes 131072 | tf_op jit(solution)/shard_map/all_to_all | solution.py:285
  100.2 102.9 %all-gather.8.cloned.1.call-start = ((), (), s32[]{:S(2)}) async-start(), calls=%async_computation.5 | async-start | bytes 4325376 | tf_op jit(solution)/shard_map/all_gather | solution.py:312
  110.8 95.7 %copy-start.6 = (bf16[1,1024,128]{2,1,0:T(8,128)(2,1)S(1)}, bf16[1,1024,128]{2,1,0:T(8,128)(2,1)}, u32[]{:S(2)}) copy-start(bf16[1,1024,128]{2,1,0:T(8,128)(2,1)} %param.24) | copy-start | bytes 786436
  214.8 2.2 copy-start.1
Sparse Core Ops, SparseCore 0:
  9.5 47.8 all-gather.3
  59.5 41.0 all-gather.5
  124.9 78.1 all-gather.7

commit v5 on v4

--- a/solution.py
+++ b/solution.py
@@ -158,7 +158,7 @@
     )(block)
 
 
-def exp_all_to_all_kernel(x_ref, y_ref, send_sems, recv_sems):
+def exp_all_to_all_kernel(broadcast, x_ref, y_ref, send_sems, recv_sems):
     n = lax.axis_size("exp")
     me = lax.axis_index("exp")
     row = lax.axis_index("seq")
@@ -171,22 +171,24 @@
     for k in range(1, n):
         peer = (me + k) % n
         cp = pltpu.make_async_remote_copy(
-            src_ref=x_ref.at[peer], dst_ref=y_ref.at[me],
+            src_ref=x_ref if broadcast else x_ref.at[peer], dst_ref=y_ref.at[me],
             send_sem=send_sems.at[k - 1], recv_sem=recv_sems.at[k - 1],
             device_id=(row, peer), device_id_type=pl.DeviceIdType.MESH)
         cp.start()
         copies.append(cp)
-    y_ref[me] = x_ref[me]
+    y_ref[me] = x_ref[...] if broadcast else x_ref[me]
     for cp in copies:
         cp.wait()
 
 
-def exp_all_to_all(x, cid):
-    n = x.shape[0]
+def exp_all_to_all(x, cid, n=None):
+    broadcast = n is not None
+    shape = ((n,) + x.shape) if broadcast else x.shape
+    n = shape[0]
     vmem = pltpu.MemorySpace.VMEM
     return pl.pallas_call(
-        exp_all_to_all_kernel,
-        out_shape=jax.ShapeDtypeStruct(x.shape, x.dtype),
+        functools.partial(exp_all_to_all_kernel, broadcast),
+        out_shape=jax.ShapeDtypeStruct(shape, x.dtype),
         in_specs=[pl.BlockSpec(memory_space=vmem)],
         out_specs=pl.BlockSpec(memory_space=vmem),
         scratch_shapes=[pltpu.SemaphoreType.DMA((n - 1,)), pltpu.SemaphoreType.DMA((n - 1,))],
@@ -232,7 +234,7 @@
     normed_attn = rms_scale(inputs, gain_attn).astype(jnp.bfloat16)
     projector = jnp.concatenate([w_query, w_key, w_value], axis=1)
     joined_qkv = jnp.dot(
-        lax.all_gather(normed_attn, "exp", axis=0, tiled=True),
+        exp_all_to_all(normed_attn, 3, n_exp).reshape(n_exp * row_count, width),
         projector,
         preferred_element_type=jnp.float32,
     ).astype(jnp.bfloat16)
@@ -282,7 +284,11 @@
         .astype(jnp.bfloat16)
         .reshape(block_len, head_cols)
     )
-    all_heads = lax.all_to_all(heads_out, "exp", split_axis=0, concat_axis=1, tiled=True)
+    all_heads = (
+        exp_all_to_all(heads_out.reshape(n_exp, row_count, head_cols), 4)
+        .transpose(1, 0, 2)
+        .reshape(row_count, n_exp * head_cols)
+    )
     attn_out = jnp.dot(
         all_heads,
         lax.all_gather(w_out, "exp", axis=0, tiled=True),
@@ -308,7 +314,9 @@
         jnp.bfloat16
     )
     outgoing = outgoing.reshape(n_exp * capacity, experts_dev, width)
-    arrived = lax.all_to_all(outgoing, "exp", split_axis=0, concat_axis=0, tiled=True)
+    arrived = exp_all_to_all(
+        outgoing.reshape((n_exp, -1) + outgoing.shape[1:]), 5
+    ).reshape(outgoing.shape)
     gathered = lax.all_gather(arrived, "seq", axis=0, tiled=True)
     n_seq = lax.axis_size("seq")
     y_size = Y_RING if n_seq % Y_RING == 0 else n_seq
@@ -316,7 +324,7 @@
     summed = ring_reduce(
         partial.reshape(partial.shape[0], width), n_seq // y_size, y_size
     ).reshape((-1,) + partial.shape[1:])
-    returned = lax.all_to_all(summed, "exp", split_axis=0, concat_axis=0, tiled=True)
+    returned = exp_all_to_all(summed.reshape((n_exp, -1) + summed.shape[1:]), 6).reshape(summed.shape)
     expert_out = jnp.dot(
         jnp.transpose(selector),
         returned.reshape(n_slots, width),

time: 311 us -> 321 us (1.032)
  Pallas kernels: 85 us -> 180 us
  waiting for transfers between devices: 126 us -> 81.9 us
  blocking collectives: 37.7 us -> 0 us
  starting transfers between devices: 5.69 us -> 0.04 us
    pallas_call x0 -> x4, Pallas kernels: none -> 95.1 us  [exp_all_to_all(): pl.pallas_call(functools.partial(exp_all_to_all_kernel, broadcast), out_s...]
    all_gather x1 -> x0, waiting for transfers between devices: 39.2 us -> none  [local(): lax.all_gather(normed_attn, 'exp', axis=0, tiled=True)]
    all_to_all x2 -> x0, blocking collectives: 37.7 us -> none  [the longest x1 25.9 us: local(): lax.all_to_all(summed, 'exp', split_axis=0, concat_axis=0, tiled=True)]
    all_to_all x1 -> x0, waiting for transfers between devices: 7.74 us -> none  [local(): lax.all_to_all(heads_out, 'exp', split_axis=0, concat_axis=1, tiled=True)]
    all_to_all x1 -> x0, starting transfers between devices: 5.61 us -> none  [local(): lax.all_to_all(heads_out, 'exp', split_axis=0, concat_axis=1, tiled=True)]
    pallas_call x0 -> x2, other arithmetic: none -> 3.5 us  [exp_all_to_all(): pl.pallas_call(functools.partial(exp_all_to_all_kernel, broadcast), out_s...]
  transfers between devices with their start and end apart: 4 -> 2, of which waited for: 3 -> 1; matrix products, arithmetic and copies ran while one was open for 5% -> 5% of each run, Pallas kernels for 8% -> 25%
where the time goes in v5:
time: 321 us
  Pallas kernels  180 us (56%)
  waiting for transfers between devices  81.9 us (26%)
  matrix products  21.6 us (7%)
  between operations  18.7 us (6%)
  local copies, waits for them, and re-layouts  10 us (3%)
  other arithmetic  7.94 us (2%)
    pallas_call x4, Pallas kernels, exp_all_to_all(): pl.pallas_call(functools.partial(exp_all_to_all_kernel, broadcast), out_s...  95.1 us
    all_gather x1, waiting for transfers between devices, local(): gathered = lax.all_gather(arrived, 'seq', axis=0, tiled=True)  81.2 us
    pallas_call x1, Pallas kernels, ring_reduce(): pl.pallas_call(functools.partial(ring_reduce_kernel, nx, ny), out_shape=j...  58.9 us
    pallas_call x1, Pallas kernels, shift_exchange(): pl.pallas_call(functools.partial(shift_exchange_kernel, tuple(offsets), a...  26.4 us
    dot_general x1, matrix products, expert_terms(): jnp.einsum('nef,ekf->nek', act, down_slice, preferred_element_type=jnp.fl...  8.42 us
  transfers between devices with their start and end apart: 2, of which 1 were waited for; matrix products, arithmetic and copies ran while one was open for 5% of the time, Pallas kernels for 25%

profile of v5, /device:TPU:1, one launch (start us, length us, event | category | flops | bytes accessed | tf_op | source)
XLA Modules:
  0.0 320.5 jit_solution(18275406514087797268)
XLA Ops:
  6.5 0.7 all-gather.3.cloned.1.call-update
  7.4 1.0 fusion.95
  8.4 1.6 fusion.97.x_ref
  9.9 43.3 %shard_map.127 = bf16[16,32,1024]{2,1,0:T(8,128)(2,1)} custom-call(bf16[32,1024]{1,0:T(8,128)(2,1)} %fusion.97.x_ref), custom_call_target="tpu_custom_call" | custom-call | tf_op jit(solution)/shard_map/pallas_call | solution.py:189
  53.9 1.8 convolution_convert_fusion.1
  55.7 0.8 slice.93.block_ref
  56.8 26.4 %shard_map.128 = bf16[6,512,128]{2,1,0:T(8,128)(2,1)} custom-call(bf16[512,128]{1,0:T(8,128)(2,1)} %slice.93.block_ref), custom_call_target="tpu_custom_call" | custom-call | tf_op jit(solution)/shard_map/pallas_call | solution.py:151
  83.2 1.3 slice_bitcast_fusion.5
  84.5 1.6 fusion.133
  92.9 0.3 convolution_bitcast_fusion.4
  94.3 0.4 fusion.45
  94.7 0.4 fusion.49
  95.2 0.4 fusion.53
  95.7 0.4 fusion.34
  96.0 0.4 fusion.37
  96.4 0.8 copy.17
  97.1 11.9 %shard_map.129 = bf16[16,32,64]{2,1,0:T(8,128)(2,1)} custom-call(bf16[16,32,64]{2,1,0:T(8,128)(2,1)} %bitcast.142), custom_call_target="tpu_custom_call" | custom-call | tf_op jit(solution)/shard_map/pallas_call | solution.py:189
  109.1 1.0 copy.18
  110.5 2.2 multiply_reduce_fusion
  113.0 0.8 reshape_reshape.20.x_ref
  113.8 14.8 %shard_map.130 = bf16[16,4,1,1024]{3,2,1,0:T(2,128)(2,1)} custom-call(bf16[16,4,1,1024]{3,2,1,0:T(2,128)(2,1)} %reshape_reshape.20.x_ref), custom_call_target="tpu_custom_call" | custom-call | tf_op jit(solution)/shard_map/pallas_call | solution.py:189
  128.6 1.8 reduce.28
  130.4 0.7 reshape.563
  131.1 81.2 %all-gather.5.cloned.1.call-done = bf16[2048,1,1024]{2,0,1:T(8,128)(2,1)} async-done(((bf16[64,1,1024]{2,0,1:T(8,128)(2,1)}), bf16[2048,1,1024]{2,0,1:T(8,128)(2,1)}) %all-gather.5.cloned.1.call-update) | async-done | bytes 4194320 | tf_op jit(solution)/shard_map/all_gather | solution.py:320
  212.3 3.4 %fusion.4 = f32[2048,1,128]{2,0,1:T(8,128)S(1)} fusion(bf16[2048,1,1024]{2,0,1:T(8,128)(2,1)} %all-gather.5.cloned.1.call-done, bf16[1,1024,128]{2,1,0:T(8,128)(2,1)S(1)} %copy-done.3), kind=kOutput, calls=%fused_computation.5 | convolution fusion | flops 536870912 | bytes 5505024 | tf_op jit(solution)/shard_map/nek,ekf->nef/dot_general | solution.py:205
  215.7 8.4 %convolution_convert_fusion = bf16[2048,1024]{1,0:T(8,128)(2,1)} fusion(bf16[2048,1,1024]{2,0,1:T(8,128)(2,1)} %all-gather.5.cloned.1.call-done, f32[2048,1,128]{2,0,1:T(8,128)S(1)} %fusion.4, bf16[1,1024,128]{2,1,0:T(8,128)(2,1)S(1)} %copy-done, bf16[1,1024,128]{2,1,0:T(8,128)(2,1)S(1)} %copy-done.6), kind=kOutput, calls=%fused_computation.4 | convolution fusion | flops 1077411840 | bytes 9961472 | tf_op jit(solution)/shard_map/nef,ekf->nek/dot_general | solution.py:208
  224.2 2.2 copy-done.1
  226.3 58.9 %shard_map.131 = bf16[64,1024]{1,0:T(8,128)(2,1)S(1)} custom-call(bf16[4,8,64,1024]{3,2,1,0:T(8,128)(2,1)S(1)} %bitcast.140), custom_call_target="tpu_custom_call" | custom-call | tf_op jit(solution)/shard_map/pallas_call | solution.py:100
  285.2 0.8 reshape_reshape.21.x_ref
  286.0 25.0 %shard_map.132 = bf16[16,4,1,1024]{3,2,1,0:T(2,128)(2,1)} custom-call(bf16[16,4,1,1024]{3,2,1,0:T(2,128)(2,1)} %reshape_reshape.21.x_ref), custom_call_target="tpu_custom_call" | custom-call | tf_op jit(solution)/shard_map/pallas_call | solution.py:189
  311.1 1.8 reduce.29
  312.9 0.8 fusion.36
  (41 shorter events, 4.8 us)
Async XLA Ops:
  6.5 209.2 %copy-start = (bf16[1,1024,128]{2,1,0:T(8,128)(2,1)S(1)}, bf16[1,1024,128]{2,1,0:T(8,128)(2,1)}, u32[]{:S(2)}) copy-start(bf16[1,1024,128]{2,1,0:T(8,128)(2,1)} %param.25) | copy-start | bytes 786436
  6.5 104.0 %all-gather.3.cloned.1.call-start = ((), (), s32[]{:S(2)}) async-start(), calls=%async_computation | async-start | bytes 2228224 | tf_op jit(solution)/shard_map/all_gather | solution.py:294
  7.3 205.0 %all-gather.5.cloned.1.call-start = ((), (), s32[]{:S(2)}) async-start(), calls=%async_computation.1 | async-start | bytes 4325376 | tf_op jit(solution)/shard_map/all_gather | solution.py:320
  94.7 15.5 %copy-start.5 = (s32[32]{0:T(128)S(1)}, s32[32]{0:T(128)}, u32[]{:S(2)}) copy-start(s32[32]{0:T(128)} %param.14) | copy-start | bytes 388
  94.7 15.8 %copy-start.2 = (bf16[32,1024]{1,0:T(8,128)(2,1)S(1)}, bf16[32,1024]{1,0:T(8,128)(2,1)}, u32[]{:S(2)}) copy-start(bf16[32,1024]{1,0:T(8,128)(2,1)} %param.13) | copy-start | bytes 196612
  95.2 17.6 %copy-start.4 = (f32[1024]{0:T(1024)S(1)}, f32[1024]{0:T(1024)}, u32[]{:S(2)}) copy-start(f32[1024]{0:T(1024)} %param.22) | copy-start | bytes 12292
  95.6 116.6 %copy-start.3 = (bf16[1,1024,128]{2,1,0:T(8,128)(2,1)S(1)}, bf16[1,1024,128]{2,1,0:T(8,128)(2,1)}, u32[]{:S(2)}) copy-start(bf16[1,1024,128]{2,1,0:T(8,128)(2,1)} %param.23) | copy-start | bytes 786436
  113.0 102.7 %copy-start.6 = (bf16[1,1024,128]{2,1,0:T(8,128)(2,1)S(1)}, bf16[1,1024,128]{2,1,0:T(8,128)(2,1)}, u32[]{:S(2)}) copy-start(bf16[1,1024,128]{2,1,0:T(8,128)(2,1)} %param.24) | copy-start | bytes 786436
  224.2 2.2 copy-start.1
Sparse Core Ops, SparseCore 0:
  9.5 56.5 all-gather.2
  131.2 81.0 all-gather.4

commit v6 on v4

--- a/solution.py
+++ b/solution.py
@@ -192,6 +192,113 @@
         scratch_shapes=[pltpu.SemaphoreType.DMA((n - 1,)), pltpu.SemaphoreType.DMA((n - 1,))],
         compiler_params=pltpu.CompilerParams(collective_id=cid, has_side_effects=True),
     )(x)
+
+
+def ring_gather_kernel(nx, ny, block_ref, out_ref, local_sem, send_sems, recv_sems):
+    me = lax.axis_index("seq")
+    col = lax.axis_index("exp")
+    x = me // ny
+    y = me % ny
+    rows = block_ref.shape[0]
+    hr = rows // 2
+
+    def dev(a, b):
+        return ((a + nx) % nx * ny + (b + ny) % ny, col)
+
+    peers = [dev(x, y + 1), dev(x, y - 1), dev(x + 1, y), dev(x - 1, y)]
+    barrier = pltpu.get_barrier_semaphore()
+    for peer in peers:
+        pl.semaphore_signal(barrier, inc=1, device_id=peer, device_id_type=pl.DeviceIdType.MESH)
+    pl.semaphore_wait(barrier, 4)
+
+    own = pltpu.make_async_copy(block_ref, out_ref.at[x, y], local_sem.at[0])
+    own.start()
+    sem_count = [0]
+
+    def unit(axis, stage, u, lo, hi):
+        if axis == "y":
+            return out_ref.at[x, u, lo:hi] if stage == 1 else out_ref.at[:, u, lo:hi]
+        return out_ref.at[u, y, lo:hi] if stage == 1 else out_ref.at[u, :, lo:hi]
+
+    def ring(axis, stage, lo, hi):
+        n = ny if axis == "y" else nx
+        c = y if axis == "y" else x
+        half = n // 2
+        mid = (lo + hi) // 2
+        steps = []
+        for sign in (1, -1):
+            prev = None
+            lane = []
+            for k in range(half):
+                u = (c - sign * k + 2 * n) % n
+                a_lo, a_hi = lo, hi
+                if k == half - 1 and n % 2 == 0:
+                    a_lo, a_hi = (lo, mid) if sign == 1 else (mid, hi)
+                if stage == 1 and k == 0:
+                    src = block_ref.at[a_lo:a_hi]
+                else:
+                    src = unit(axis, stage, u, a_lo, a_hi)
+                dst = unit(axis, stage, u, a_lo, a_hi)
+                target = dev(x, y + sign) if axis == "y" else dev(x + sign, y)
+                j = sem_count[0]
+                sem_count[0] += 1
+                cp = pltpu.make_async_remote_copy(
+                    src_ref=src, dst_ref=dst, send_sem=send_sems.at[j], recv_sem=recv_sems.at[j],
+                    device_id=target, device_id_type=pl.DeviceIdType.MESH)
+                lane.append((prev, cp))
+                prev = cp
+            steps.append(lane)
+        return steps
+
+    plans = []
+    for lo, hi, first, second in ((0, hr, "y", "x"), (hr, rows, "x", "y")):
+        s1 = ring(first, 1, lo, hi)
+        s2 = ring(second, 2, lo, hi)
+        plans.append((s1, s2))
+
+    started = []
+
+    def run(lane_list):
+        depth = max(len(l) for l in lane_list)
+        for k in range(depth):
+            for lane in lane_list:
+                if k < len(lane):
+                    prev, cp = lane[k]
+                    if prev is not None:
+                        prev.wait_recv()
+                    cp.start()
+                    started.append(cp)
+
+    run([lane for s1, _ in plans for lane in s1])
+    for s1, _ in plans:
+        for lane in s1:
+            lane[-1][1].wait_recv()
+    own.wait()
+    run([lane for _, s2 in plans for lane in s2])
+    for _, s2 in plans:
+        for lane in s2:
+            lane[-1][1].wait_recv()
+    for cp in started:
+        cp.wait_send()
+
+
+def ring_gather(block, nx, ny):
+    vmem = pltpu.MemorySpace.VMEM
+    n_sems = 4 * (nx // 2 + ny // 2) + 4
+    return pl.pallas_call(
+        functools.partial(ring_gather_kernel, nx, ny),
+        out_shape=jax.ShapeDtypeStruct((nx, ny) + block.shape, block.dtype),
+        in_specs=[pl.BlockSpec(memory_space=vmem)],
+        out_specs=pl.BlockSpec(memory_space=vmem),
+        scratch_shapes=[
+            pltpu.SemaphoreType.DMA((1,)),
+            pltpu.SemaphoreType.DMA((n_sems,)),
+            pltpu.SemaphoreType.DMA((n_sems,)),
+        ],
+        compiler_params=pltpu.CompilerParams(
+            collective_id=3, has_side_effects=True, vmem_limit_bytes=48 * 1024 * 1024
+        ),
+    )(block)
 
 
 def rms_scale(matrix, gain):
@@ -309,7 +416,11 @@
     )
     outgoing = outgoing.reshape(n_exp * capacity, experts_dev, width)
     arrived = lax.all_to_all(outgoing, "exp", split_axis=0, concat_axis=0, tiled=True)
-    gathered = lax.all_gather(arrived, "seq", axis=0, tiled=True)
+    n_seq = lax.axis_size("seq")
+    y_size = Y_RING if n_seq % Y_RING == 0 else n_seq
+    gathered = ring_gather(
+        arrived.reshape(arrived.shape[0], width), n_seq // y_size, y_size
+    ).reshape((n_seq * arrived.shape[0],) + arrived.shape[1:])
     n_seq = lax.axis_size("seq")
     y_size = Y_RING if n_seq % Y_RING == 0 else n_seq
     partial = expert_terms(gathered, w_gate, w_up, w_down).astype(jnp.bfloat16)

time: 311 us -> 276 us (0.89)
  waiting for transfers between devices: 126 us -> 47.7 us
  Pallas kernels: 85 us -> 129 us
    all_gather x1 -> x0, waiting for transfers between devices: 78.3 us -> none  [local(): gathered = lax.all_gather(arrived, 'seq', axis=0, tiled=True)]
    pallas_call x0 -> x1, Pallas kernels: none -> 42.8 us  [ring_gather(): pl.pallas_call(functools.partial(ring_gather_kernel, nx, ny), out_shape=j...]
  transfers between devices with their start and end apart: 4 -> 3, of which waited for: 3 -> 2; matrix products, arithmetic and copies ran while one was open for 5% -> 5% of each run, Pallas kernels for 8% -> 9%
where the time goes in v6:
time: 276 us
  Pallas kernels  129 us (47%)
  waiting for transfers between devices  47.7 us (17%)
  blocking collectives  38.1 us (14%)
  matrix products  19.2 us (7%)
  between operations  18.7 us (7%)
  local copies, waits for them, and re-layouts  10 us (4%)
  other arithmetic  7.13 us (3%)
  starting transfers between devices  5.65 us (2%)
    pallas_call x1, Pallas kernels, ring_reduce(): pl.pallas_call(functools.partial(ring_reduce_kernel, nx, ny), out_shape=j...  60.2 us
    pallas_call x1, Pallas kernels, ring_gather(): pl.pallas_call(functools.partial(ring_gather_kernel, nx, ny), out_shape=j...  42.8 us
    all_gather x1, waiting for transfers between devices, local(): lax.all_gather(normed_attn, 'exp', axis=0, tiled=True)  39.2 us
    all_to_all x1, blocking collectives, local(): lax.all_to_all(summed, 'exp', split_axis=0, concat_axis=0, tiled=True)  26.3 us
    pallas_call x1, Pallas kernels, shift_exchange(): pl.pallas_call(functools.partial(shift_exchange_kernel, tuple(offsets), a...  26.1 us
    all_to_all x1, blocking collectives, local(): lax.all_to_all(outgoing, 'exp', split_axis=0, concat_axis=0, tiled=True)  11.8 us
    dot_general x1, matrix products, expert_terms(): jnp.einsum('nef,ekf->nek', act, down_slice, preferred_element_type=jnp.fl...  8.27 us
    all_to_all x1, waiting for transfers between devices, local(): lax.all_to_all(heads_out, 'exp', split_axis=0, concat_axis=1, tiled=True)  7.79 us
  transfers between devices with their start and end apart: 3, of which 2 were waited for; matrix products, arithmetic and copies ran while one was open for 5% of the time, Pallas kernels for 9%

profile of v6, /device:TPU:1, one launch (start us, length us, event | category | flops | bytes accessed | tf_op | source)
XLA Modules:
  0.0 275.7 jit_solution(4626883798575582467)
XLA Ops:
  6.5 1.0 fusion.78
  7.6 1.6 fusion.80
  9.2 0.7 all-gather.5.cloned.1.call-update
  10.6 1.6 fusion.118
  16.6 0.7 fusion.108
  17.4 0.8 select_reduce_fusion
  18.2 39.2 %all-gather.3.cloned.1.call-done = bf16[512,1024]{1,0:T(8,128)(2,1)} async-done(((bf16[32,1024]{1,0:T(8,128)(2,1)}), bf16[512,1024]{1,0:T(8,128)(2,1)}) %all-gather.3.cloned.1.call-update) | async-done | bytes 1048592 | tf_op jit(solution)/shard_map/all_gather | solution.py:342
  57.4 1.8 convolution_convert_fusion.1
  59.1 0.8 slice.93.block_ref
  60.2 26.1 %shard_map.127 = bf16[6,512,128]{2,1,0:T(8,128)(2,1)} custom-call(bf16[512,128]{1,0:T(8,128)(2,1)} %slice.93.block_ref), custom_call_target="tpu_custom_call" | custom-call | tf_op jit(solution)/shard_map/pallas_call | solution.py:151
  86.4 1.3 slice_bitcast_fusion.5
  90.2 0.3 convolution_bitcast_fusion.6
  91.6 0.4 fusion.28
  92.0 0.4 fusion.32
  92.5 0.4 fusion.36
  92.9 0.4 fusion.17
  93.8 0.8 reshape.581
  94.6 5.6 %all-to-all-start = ((bf16[16,2,1024]{2,1,0:T(2,128)(2,1)}), bf16[16,2,1024]{2,1,0:T(2,128)(2,1)S(1)}, u32[]{:S(2)}, u32[]{:S(2)}) async-start(bf16[16,2,1024]{2,1,0:T(2,128)(2,1)} %reshape.581), calls=%async_computation | async-start | bytes 131072 | tf_op jit(solution)/shard_map/all_to_all | solution.py:392
  100.2 7.8 %all-to-all-done = bf16[16,2,1024]{2,1,0:T(2,128)(2,1)S(1)} async-done(((bf16[16,2,1024]{2,1,0:T(2,128)(2,1)}), bf16[16,2,1024]{2,1,0:T(2,128)(2,1)S(1)}, u32[]{:S(2)}, u32[]{:S(2)}) %all-to-all-start) | async-done | bytes 65568 | tf_op jit(solution)/shard_map/all_to_all | solution.py:392
  108.4 2.2 multiply_reduce_fusion
  110.9 0.5 broadcast.544
  111.4 0.7 reduce.28
  112.1 11.8 %all_to_all.29 = bf16[16,2,2048]{2,1,0:T(2,128)(2,1)S(1)} all-to-all(bf16[16,2,2048]{2,1,0:T(2,128)(2,1)S(1)} %reshape.583), channel_id=1, replica_groups=mesh['seq'=32,'exp'=16] {'exp'}, dimensions={0} | all-to-all | bytes 262144 | tf_op jit(solution)/shard_map/all_to_all | solution.py:418
  124.1 42.8 %shard_map.128 = bf16[4,8,64,1024]{3,2,1,0:T(8,128)(2,1)S(1)} custom-call(bf16[64,1024]{1,0:T(8,128)(2,1)S(1)} %bitcast.136), custom_call_target="tpu_custom_call" | custom-call | tf_op jit(solution)/shard_map/pallas_call | solution.py:288
  167.0 1.9 copy-done.1
  168.9 1.3 convolution_bitcast_fusion.1
  170.2 8.3 %convolution_convert_fusion = bf16[2048,1024]{1,0:T(8,128)(2,1)} fusion(bf16[2048,1024]{1,0:T(8,128)(2,1)} %bitcast.134, f32[2048,1,128]{2,0,1:T(8,128)S(1)} %convolution_bitcast_fusion.1, bf16[1,1024,128]{2,1,0:T(8,128)(2,1)S(1)} %copy-done, bf16[1,1024,128]{2,1,0:T(8,128)(2,1)S(1)} %copy-done.7), kind=kOutput, calls=%fused_computation | convolution fusion | flops 1077411840 | bytes 9961472 | tf_op jit(solution)/shard_map/nef,ekf->nek/dot_general | solution.py:313
  178.4 2.2 copy-done.2
  180.6 60.2 %shard_map.129 = bf16[64,1024]{1,0:T(8,128)(2,1)S(1)} custom-call(bf16[4,8,64,1024]{3,2,1,0:T(8,128)(2,1)S(1)} %bitcast.135), custom_call_target="tpu_custom_call" | custom-call | tf_op jit(solution)/shard_map/pallas_call | solution.py:100
  240.8 0.7 reduce.29
  241.6 26.3 %all_to_all.30 = bf16[16,2,2048]{2,1,0:T(2,128)(2,1)S(1)} all-to-all(bf16[16,2,2048]{2,1,0:T(2,128)(2,1)S(1)} %reshape.585), channel_id=1, replica_groups=mesh['seq'=32,'exp'=16] {'exp'}, dimensions={0} | all-to-all | bytes 262144 | tf_op jit(solution)/shard_map/all_to_all | solution.py:430
  268.0 0.8 fusion.19
  (48 shorter events, 5.6 us)
Async XLA Ops:
  6.5 163.6 %copy-start = (bf16[1,1024,128]{2,1,0:T(8,128)(2,1)S(1)}, bf16[1,1024,128]{2,1,0:T(8,128)(2,1)}, u32[]{:S(2)}) copy-start(bf16[1,1024,128]{2,1,0:T(8,128)(2,1)} %param.25) | copy-start | bytes 786436
  6.5 50.8 %all-gather.3.cloned.1.call-start = ((), (), s32[]{:S(2)}) async-start(), calls=%async_computation.3 | async-start | bytes 1114112 | tf_op jit(solution)/shard_map/all_gather | solution.py:342
  9.1 99.2 %all-gather.5.cloned.1.call-start = ((), (), s32[]{:S(2)}) async-start(), calls=%async_computation.4 | async-start | bytes 2228224 | tf_op jit(solution)/shard_map/all_gather | solution.py:395
  92.0 8.2 %copy-start.6 = (s32[32]{0:T(128)S(1)}, s32[32]{0:T(128)}, u32[]{:S(2)}) copy-start(s32[32]{0:T(128)} %param.14) | copy-start | bytes 388
  92.0 16.4 %copy-start.3 = (bf16[32,1024]{1,0:T(8,128)(2,1)S(1)}, bf16[32,1024]{1,0:T(8,128)(2,1)}, u32[]{:S(2)}) copy-start(bf16[32,1024]{1,0:T(8,128)(2,1)} %param.13) | copy-start | bytes 196612
  92.9 17.7 %copy-start.5 = (f32[1024]{0:T(1024)S(1)}, f32[1024]{0:T(1024)}, u32[]{:S(2)}) copy-start(f32[1024]{0:T(1024)} %param.22) | copy-start | bytes 12292
  94.6 13.4 %all-to-all-start = ((bf16[16,2,1024]{2,1,0:T(2,128)(2,1)}), bf16[16,2,1024]{2,1,0:T(2,128)(2,1)S(1)}, u32[]{:S(2)}, u32[]{:S(2)}) async-start(bf16[16,2,1024]{2,1,0:T(2,128)(2,1)} %reshape.581), calls=%async_computation | async-start | bytes 131072 | tf_op jit(solution)/shard_map/all_to_all | solution.py:392
  108.3 60.5 %copy-start.4 = (bf16[1,1024,128]{2,1,0:T(8,128)(2,1)S(1)}, bf16[1,1024,128]{2,1,0:T(8,128)(2,1)}, u32[]{:S(2)}) copy-start(bf16[1,1024,128]{2,1,0:T(8,128)(2,1)} %param.23) | copy-start | bytes 786436
  166.9 1.9 copy-start.1
  167.0 3.2 %copy-start.7 = (bf16[1,1024,128]{2,1,0:T(8,128)(2,1)S(1)}, bf16[1,1024,128]{2,1,0:T(8,128)(2,1)}, u32[]{:S(2)}) copy-start(bf16[1,1024,128]{2,1,0:T(8,128)(2,1)} %param.24) | copy-start | bytes 786436
  178.4 2.2 copy-start.2
Sparse Core Ops, SparseCore 0:
  9.5 47.8 all-gather.2
  59.5 41.0 all-gather.4

commit v7 on v6

--- a/solution.py
+++ b/solution.py
@@ -8,6 +8,7 @@
 
 REACH = 3
 Y_RING = 8
+CORES = 2
 
 
 EPSILON = 1e-05
@@ -194,16 +195,17 @@
     )(x)
 
 
-def ring_gather_kernel(nx, ny, block_ref, out_ref, local_sem, send_sems, recv_sems):
-    me = lax.axis_index("seq")
-    col = lax.axis_index("exp")
+def ring_gather_kernel(nx, ny, axis, other, block_ref, out_ref, local_sem, send_sems, recv_sems):
+    me = lax.axis_index(axis)
+    col = lax.axis_index(other)
     x = me // ny
     y = me % ny
     rows = block_ref.shape[0]
     hr = rows // 2
 
     def dev(a, b):
-        return ((a + nx) % nx * ny + (b + ny) % ny, col)
+        idx = (a + nx) % nx * ny + (b + ny) % ny
+        return (idx, col) if axis == "seq" else (col, idx)
 
     peers = [dev(x, y + 1), dev(x, y - 1), dev(x + 1, y), dev(x - 1, y)]
     barrier = pltpu.get_barrier_semaphore()
@@ -282,11 +284,11 @@
         cp.wait_send()
 
 
-def ring_gather(block, nx, ny):
+def ring_gather(block, nx, ny, axis="seq", other="exp", cid=3):
     vmem = pltpu.MemorySpace.VMEM
     n_sems = 4 * (nx // 2 + ny // 2) + 4
     return pl.pallas_call(
-        functools.partial(ring_gather_kernel, nx, ny),
+        functools.partial(ring_gather_kernel, nx, ny, axis, other),
         out_shape=jax.ShapeDtypeStruct((nx, ny) + block.shape, block.dtype),
         in_specs=[pl.BlockSpec(memory_space=vmem)],
         out_specs=pl.BlockSpec(memory_space=vmem),
@@ -296,7 +298,7 @@
             pltpu.SemaphoreType.DMA((n_sems,)),
         ],
         compiler_params=pltpu.CompilerParams(
-            collective_id=3, has_side_effects=True, vmem_limit_bytes=48 * 1024 * 1024
+            collective_id=cid, has_side_effects=True, vmem_limit_bytes=48 * 1024 * 1024
         ),
     )(block)
 
@@ -339,7 +341,7 @@
     normed_attn = rms_scale(inputs, gain_attn).astype(jnp.bfloat16)
     projector = jnp.concatenate([w_query, w_key, w_value], axis=1)
     joined_qkv = jnp.dot(
-        lax.all_gather(normed_attn, "exp", axis=0, tiled=True),
+        ring_gather(normed_attn, n_exp // CORES, CORES, "exp", "seq", 4).reshape(n_exp * row_count, width),
         projector,
         preferred_element_type=jnp.float32,
     ).astype(jnp.bfloat16)

time: 276 us -> 267 us (0.967)
  waiting for transfers between devices: 47.7 us -> 8.21 us
  Pallas kernels: 129 us -> 155 us
  starting transfers between devices: 5.65 us -> 13.6 us
    all_gather x1 -> x0, waiting for transfers between devices: 39.2 us -> none  [local(): lax.all_gather(normed_attn, 'exp', axis=0, tiled=True)]
    pallas_call x1 -> x2, Pallas kernels: 42.8 us -> 75.8 us  [ring_gather(): pl.pallas_call(functools.partial(ring_gather_kernel, nx, ny, axis, other)...]
    all_to_all x1, starting transfers between devices: 5.61 us -> 13.6 us  [local(): lax.all_to_all(heads_out, 'exp', split_axis=0, concat_axis=1, tiled=True)]
    pallas_call x1, Pallas kernels: 26.1 us -> 19 us  [shift_exchange(): pl.pallas_call(functools.partial(shift_exchange_kernel, tuple(offsets), a...]
  transfers between devices with their start and end apart: 3 -> 2, of which waited for: 2 -> 1; matrix products, arithmetic and copies ran while one was open for 5% -> 6% of each run, Pallas kernels for 9% -> 20%
where the time goes in v7:
time: 267 us; the launch traced here: 266 us
  Pallas kernels  155 us (58%)
  blocking collectives  36.6 us (14%)
  matrix products  18.9 us (7%)
  between operations  18.7 us (7%)
  starting transfers between devices  13.6 us (5%)
  local copies, waits for them, and re-layouts  9.96 us (4%)
  waiting for transfers between devices  8.21 us (3%)
  other arithmetic  5.16 us (2%)
    pallas_call x2, Pallas kernels, ring_gather(): pl.pallas_call(functools.partial(ring_gather_kernel, nx, ny, axis, other)...  75.8 us
    pallas_call x1, Pallas kernels, ring_reduce(): pl.pallas_call(functools.partial(ring_reduce_kernel, nx, ny), out_shape=j...  59.9 us
    all_to_all x1, blocking collectives, local(): lax.all_to_all(summed, 'exp', split_axis=0, concat_axis=0, tiled=True)  24.9 us
    pallas_call x1, Pallas kernels, shift_exchange(): pl.pallas_call(functools.partial(shift_exchange_kernel, tuple(offsets), a...  19 us
    all_to_all x1, starting transfers between devices, local(): lax.all_to_all(heads_out, 'exp', split_axis=0, concat_axis=1, tiled=True)  13.6 us
    all_to_all x1, blocking collectives, local(): lax.all_to_all(outgoing, 'exp', split_axis=0, concat_axis=0, tiled=True)  11.8 us
    dot_general x1, matrix products, expert_terms(): jnp.einsum('nef,ekf->nek', act, down_slice, preferred_element_type=jnp.fl...  8.25 us
    all_to_all x1, waiting for transfers between devices, local(): lax.all_to_all(heads_out, 'exp', split_axis=0, concat_axis=1, tiled=True)  7.48 us
  transfers between devices with their start and end apart: 2, of which 1 were waited for; matrix products, arithmetic and copies ran while one was open for 6% of the time, Pallas kernels for 20%

profile of v7, /device:TPU:1, one launch (start us, length us, event | category | flops | bytes accessed | tf_op | source)
XLA Modules:
  0.0 266.0 jit_solution(8965428503854575889)
XLA Ops:
  6.5 0.7 all-gather.2.cloned.1.call-update
  7.4 1.0 fusion.78
  8.3 0.9 fusion.80.block_ref
  9.3 33.8 %shard_map.127 = bf16[8,2,32,1024]{3,2,1,0:T(8,128)(2,1)S(1)} custom-call(bf16[32,1024]{1,0:T(8,128)(2,1)S(1)} %fusion.80.block_ref), custom_call_target="tpu_custom_call" | custom-call | tf_op jit(solution)/shard_map/pallas_call | solution.py:290
  43.7 1.5 convolution_convert_fusion.1
  45.3 0.8 slice.93.block_ref
  46.4 19.0 %shard_map.128 = bf16[6,512,128]{2,1,0:T(8,128)(2,1)} custom-call(bf16[512,128]{1,0:T(8,128)(2,1)} %slice.93.block_ref), custom_call_target="tpu_custom_call" | custom-call | tf_op jit(solution)/shard_map/pallas_call | solution.py:152
  65.4 1.3 slice_bitcast_fusion.5
  66.6 1.6 fusion.118
  75.0 0.3 convolution_bitcast_fusion.6
  75.4 0.3 convolution_bitcast_fusion.5
  76.4 0.4 fusion.28
  76.9 0.4 fusion.32
  77.3 0.4 fusion.36
  77.8 0.4 fusion.17
  78.2 0.4 fusion.20
  78.6 0.8 reshape.585
  79.4 13.6 %all-to-all-start = ((bf16[16,2,1024]{2,1,0:T(2,128)(2,1)}), bf16[16,2,1024]{2,1,0:T(2,128)(2,1)S(1)}, u32[]{:S(2)}, u32[]{:S(2)}) async-start(bf16[16,2,1024]{2,1,0:T(2,128)(2,1)} %reshape.585), calls=%async_computation | async-start | bytes 131072 | tf_op jit(solution)/shard_map/all_to_all | solution.py:394
  93.4 7.5 %all-to-all-done = bf16[16,2,1024]{2,1,0:T(2,128)(2,1)S(1)} async-done(((bf16[16,2,1024]{2,1,0:T(2,128)(2,1)}), bf16[16,2,1024]{2,1,0:T(2,128)(2,1)S(1)}, u32[]{:S(2)}, u32[]{:S(2)}) %all-to-all-start) | async-done | bytes 65568 | tf_op jit(solution)/shard_map/all_to_all | solution.py:394
  101.3 2.2 multiply_reduce_fusion
  103.7 0.5 broadcast.544
  104.3 0.7 reduce.28
  105.0 11.8 %all_to_all.29 = bf16[16,2,2048]{2,1,0:T(2,128)(2,1)S(1)} all-to-all(bf16[16,2,2048]{2,1,0:T(2,128)(2,1)S(1)} %reshape.587), channel_id=1, replica_groups=mesh['seq'=32,'exp'=16] {'exp'}, dimensions={0} | all-to-all | bytes 262144 | tf_op jit(solution)/shard_map/all_to_all | solution.py:420
  117.0 42.0 %shard_map.129 = bf16[4,8,64,1024]{3,2,1,0:T(8,128)(2,1)S(1)} custom-call(bf16[64,1024]{1,0:T(8,128)(2,1)S(1)} %bitcast.138), custom_call_target="tpu_custom_call" | custom-call | tf_op jit(solution)/shard_map/pallas_call | solution.py:290
  159.0 1.9 copy-done.1
  160.9 1.2 convolution_bitcast_fusion.1
  162.2 8.2 %convolution_convert_fusion = bf16[2048,1024]{1,0:T(8,128)(2,1)} fusion(bf16[2048,1024]{1,0:T(8,128)(2,1)} %bitcast.135, f32[2048,1,128]{2,0,1:T(8,128)S(1)} %convolution_bitcast_fusion.1, bf16[1,1024,128]{2,1,0:T(8,128)(2,1)S(1)} %copy-done, bf16[1,1024,128]{2,1,0:T(8,128)(2,1)S(1)} %copy-done.7), kind=kOutput, calls=%fused_computation | convolution fusion | flops 1077411840 | bytes 9961472 | tf_op jit(solution)/shard_map/nef,ekf->nek/dot_general | solution.py:315
  170.5 2.2 copy-done.2
  172.6 59.9 %shard_map.130 = bf16[64,1024]{1,0:T(8,128)(2,1)S(1)} custom-call(bf16[4,8,64,1024]{3,2,1,0:T(8,128)(2,1)S(1)} %bitcast.136), custom_call_target="tpu_custom_call" | custom-call | tf_op jit(solution)/shard_map/pallas_call | solution.py:101
  232.6 0.7 reduce.29
  233.3 24.9 %all_to_all.30 = bf16[16,2,2048]{2,1,0:T(2,128)(2,1)S(1)} all-to-all(bf16[16,2,2048]{2,1,0:T(2,128)(2,1)S(1)} %reshape.589), channel_id=1, replica_groups=mesh['seq'=32,'exp'=16] {'exp'}, dimensions={0} | all-to-all | bytes 262144 | tf_op jit(solution)/shard_map/all_to_all | solution.py:432
  258.3 0.8 fusion.19
  (46 shorter events, 5.1 us)
Async XLA Ops:
  6.5 155.7 %copy-start = (bf16[1,1024,128]{2,1,0:T(8,128)(2,1)S(1)}, bf16[1,1024,128]{2,1,0:T(8,128)(2,1)}, u32[]{:S(2)}) copy-start(bf16[1,1024,128]{2,1,0:T(8,128)(2,1)} %param.25) | copy-start | bytes 786436
  6.5 94.7 %all-gather.2.cloned.1.call-start = ((), (), s32[]{:S(2)}) async-start(), calls=%async_computation.3 | async-start | bytes 2228224 | tf_op jit(solution)/shard_map/all_gather | solution.py:397
  76.9 16.2 %copy-start.6 = (s32[32]{0:T(128)S(1)}, s32[32]{0:T(128)}, u32[]{:S(2)}) copy-start(s32[32]{0:T(128)} %param.14) | copy-start | bytes 388
  76.9 24.4 %copy-start.3 = (bf16[32,1024]{1,0:T(8,128)(2,1)S(1)}, bf16[32,1024]{1,0:T(8,128)(2,1)}, u32[]{:S(2)}) copy-start(bf16[32,1024]{1,0:T(8,128)(2,1)} %param.13) | copy-start | bytes 196612
  77.8 25.7 %copy-start.5 = (f32[1024]{0:T(1024)S(1)}, f32[1024]{0:T(1024)}, u32[]{:S(2)}) copy-start(f32[1024]{0:T(1024)} %param.22) | copy-start | bytes 12292
  79.4 21.4 %all-to-all-start = ((bf16[16,2,1024]{2,1,0:T(2,128)(2,1)}), bf16[16,2,1024]{2,1,0:T(2,128)(2,1)S(1)}, u32[]{:S(2)}, u32[]{:S(2)}) async-start(bf16[16,2,1024]{2,1,0:T(2,128)(2,1)} %reshape.585), calls=%async_computation | async-start | bytes 131072 | tf_op jit(solution)/shard_map/all_to_all | solution.py:394
  101.2 59.7 %copy-start.4 = (bf16[1,1024,128]{2,1,0:T(8,128)(2,1)S(1)}, bf16[1,1024,128]{2,1,0:T(8,128)(2,1)}, u32[]{:S(2)}) copy-start(bf16[1,1024,128]{2,1,0:T(8,128)(2,1)} %param.23) | copy-start | bytes 786436
  159.0 1.9 copy-start.1
  159.0 3.2 %copy-start.7 = (bf16[1,1024,128]{2,1,0:T(8,128)(2,1)S(1)}, bf16[1,1024,128]{2,1,0:T(8,128)(2,1)}, u32[]{:S(2)}) copy-start(bf16[1,1024,128]{2,1,0:T(8,128)(2,1)} %param.24) | copy-start | bytes 786436
  170.5 2.2 copy-start.2
Sparse Core Ops, SparseCore 0:
  9.5 49.2 all-gather.1

commit v8 on v7

--- a/solution.py
+++ b/solution.py
@@ -20,7 +20,7 @@
     return lax.ppermute(block, axis, route)
 
 
-def ring_reduce_kernel(nx, ny, part_ref, out_ref, recv1, send1, acc, recv2, send2,
+def ring_reduce_kernel(nx, ny, splits, part_ref, out_ref, recv1, send1, acc, recv2, send2,
                        s1_send, s1_recv, s2_send, s2_recv):
     me = lax.axis_index("seq")
     col = lax.axis_index("exp")
@@ -30,9 +30,9 @@
     y_down = x * ny + (y + ny - 1) % ny
     x_up = ((x + 1) % nx) * ny + y
     x_down = ((x + nx - 1) % nx) * ny + y
-    half_x = nx // 2
     rows = part_ref.shape[2]
-    half_r = rows // 2
+    piece = rows // splits
+    quarter = rows // 4
 
     barrier = pltpu.get_barrier_semaphore()
     for peer in (y_up, y_down, x_up, x_down):
@@ -40,18 +40,24 @@
                             device_id_type=pl.DeviceIdType.MESH)
     pl.semaphore_wait(barrier, 4)
 
-    lanes = ((y_up, 0, half_x, 1), (y_down, half_x, nx, -1))
+    lanes = []
+    for a in range(nx):
+        for p in range(splits):
+            if a < nx // 2:
+                lanes.append((y_up, 1, a, p * piece))
+            else:
+                lanes.append((y_down, -1, a, p * piece))
     copies1 = []
     for k in range(ny - 1):
         step_copies = []
-        for d, (peer, lo, hi, sign) in enumerate(lanes):
+        for d, (peer, sign, a, r0) in enumerate(lanes):
             c = (y - sign * (k + 1) + 2 * ny) % ny
             if k == 0:
-                src = part_ref.at[lo:hi, c]
+                src = part_ref.at[a, c, r0:r0 + piece]
             else:
                 copies1[k - 1][d].wait_recv()
                 send1[d, k] = (recv1[d, k - 1].astype(jnp.float32)
-                               + part_ref[lo:hi, c].astype(jnp.float32)).astype(send1.dtype)
+                               + part_ref[a, c, r0:r0 + piece].astype(jnp.float32)).astype(send1.dtype)
                 src = send1.at[d, k]
             cp = pltpu.make_async_remote_copy(
                 src_ref=src, dst_ref=recv1.at[d, k],
@@ -60,21 +66,22 @@
             cp.start()
             step_copies.append(cp)
         copies1.append(step_copies)
-    for d, (peer, lo, hi, sign) in enumerate(lanes):
+    for d, (peer, sign, a, r0) in enumerate(lanes):
         copies1[ny - 2][d].wait_recv()
-        acc[lo:hi] = recv1[d, ny - 2].astype(jnp.float32) + part_ref[lo:hi, y].astype(jnp.float32)
-
-    lanes2 = ((x_up, 0, half_r, 1), (x_down, half_r, rows, -1))
+        acc[a, r0:r0 + piece] = (recv1[d, ny - 2].astype(jnp.float32)
+                                 + part_ref[a, y, r0:r0 + piece].astype(jnp.float32))
+
+    lanes2 = [(x_up, 1, 0), (x_up, 1, quarter), (x_down, -1, 2 * quarter), (x_down, -1, 3 * quarter)]
     copies2 = []
     for k in range(nx - 1):
         step_copies = []
-        for d, (peer, lo, hi, sign) in enumerate(lanes2):
+        for d, (peer, sign, r0) in enumerate(lanes2):
             c = (x - sign * (k + 1) + 2 * nx) % nx
             if k == 0:
-                src = acc.at[c, lo:hi]
+                src = acc.at[c, r0:r0 + quarter]
             else:
                 copies2[k - 1][d].wait_recv()
-                send2[d, k] = recv2[d, k - 1] + acc[c, lo:hi]
+                send2[d, k] = recv2[d, k - 1] + acc[c, r0:r0 + quarter]
                 src = send2.at[d, k]
             cp = pltpu.make_async_remote_copy(
                 src_ref=src, dst_ref=recv2.at[d, k],
@@ -83,36 +90,35 @@
             cp.start()
             step_copies.append(cp)
         copies2.append(step_copies)
-    for d, (peer, lo, hi, sign) in enumerate(lanes2):
+    for d, (peer, sign, r0) in enumerate(lanes2):
         copies2[nx - 2][d].wait_recv()
-        out_ref[lo:hi] = (recv2[d, nx - 2] + acc[x, lo:hi]).astype(out_ref.dtype)
+        out_ref[r0:r0 + quarter] = (recv2[d, nx - 2] + acc[x, r0:r0 + quarter]).astype(out_ref.dtype)
     for step_copies in copies1 + copies2:
         for cp in step_copies:
             cp.wait_send()
 
 
-def ring_reduce(part, nx, ny):
+def ring_reduce(part, nx, ny, splits=2):
     width = part.shape[-1]
     rows = part.shape[0] // (nx * ny)
     part = part.reshape(nx, ny, rows, width)
-    half_x = nx // 2
-    half_r = rows // 2
+    n1 = nx * splits
     vmem = pltpu.MemorySpace.VMEM
     return pl.pallas_call(
-        functools.partial(ring_reduce_kernel, nx, ny),
+        functools.partial(ring_reduce_kernel, nx, ny, splits),
         out_shape=jax.ShapeDtypeStruct((rows, width), jnp.bfloat16),
         in_specs=[pl.BlockSpec(memory_space=vmem)],
         out_specs=pl.BlockSpec(memory_space=vmem),
         scratch_shapes=[
-            pltpu.VMEM((2, ny - 1, half_x, rows, width), jnp.bfloat16),
-            pltpu.VMEM((2, ny - 1, half_x, rows, width), jnp.bfloat16),
+            pltpu.VMEM((n1, ny - 1, rows // splits, width), jnp.bfloat16),
+            pltpu.VMEM((n1, ny - 1, rows // splits, width), jnp.bfloat16),
             pltpu.VMEM((nx, rows, width), jnp.float32),
-            pltpu.VMEM((2, nx - 1, half_r, width), jnp.float32),
-            pltpu.VMEM((2, nx - 1, half_r, width), jnp.float32),
-            pltpu.SemaphoreType.DMA((2, ny - 1)),
-            pltpu.SemaphoreType.DMA((2, ny - 1)),
-            pltpu.SemaphoreType.DMA((2, nx - 1)),
-            pltpu.SemaphoreType.DMA((2, nx - 1)),
+            pltpu.VMEM((4, nx - 1, rows // 4, width), jnp.float32),
+            pltpu.VMEM((4, nx - 1, rows // 4, width), jnp.float32),
+            pltpu.SemaphoreType.DMA((n1, ny - 1)),
+            pltpu.SemaphoreType.DMA((n1, ny - 1)),
+            pltpu.SemaphoreType.DMA((4, nx - 1)),
+            pltpu.SemaphoreType.DMA((4, nx - 1)),
         ],
         compiler_params=pltpu.CompilerParams(
             collective_id=1, has_side_effects=True, vmem_limit_bytes=48 * 1024 * 1024

time: 267 us -> 257 us (0.963)
  Pallas kernels: 155 us -> 147 us
    pallas_call x1, Pallas kernels: 59.9 us -> 52.1 us  [ring_reduce(): pl.pallas_call(functools.partial(ring_reduce_kernel, nx, ny, splits), out...]
  transfers between devices with their start and end apart: 2 -> 2, of which waited for: 1 -> 1; matrix products, arithmetic and copies ran while one was open for 6% -> 6% of each run, Pallas kernels for 20% -> 21%
where the time goes in v8:
time: 257 us; the launch traced here: 256 us
  Pallas kernels  147 us (57%)
  blocking collectives  34.7 us (14%)
  matrix products  18.9 us (7%)
  between operations  18.7 us (7%)
  starting transfers between devices  13.6 us (5%)
  local copies, waits for them, and re-layouts  9.96 us (4%)
  waiting for transfers between devices  8.21 us (3%)
  other arithmetic  5.16 us (2%)
    pallas_call x2, Pallas kernels, ring_gather(): pl.pallas_call(functools.partial(ring_gather_kernel, nx, ny, axis, other)...  75.8 us
    pallas_call x1, Pallas kernels, ring_reduce(): pl.pallas_call(functools.partial(ring_reduce_kernel, nx, ny, splits), out...  52.1 us
    all_to_all x1, blocking collectives, local(): lax.all_to_all(summed, 'exp', split_axis=0, concat_axis=0, tiled=True)  22.9 us
    pallas_call x1, Pallas kernels, shift_exchange(): pl.pallas_call(functools.partial(shift_exchange_kernel, tuple(offsets), a...  19 us
    all_to_all x1, starting transfers between devices, local(): lax.all_to_all(heads_out, 'exp', split_axis=0, concat_axis=1, tiled=True)  13.6 us
    all_to_all x1, blocking collectives, local(): lax.all_to_all(outgoing, 'exp', split_axis=0, concat_axis=0, tiled=True)  11.8 us
    dot_general x1, matrix products, expert_terms(): jnp.einsum('nef,ekf->nek', act, down_slice, preferred_element_type=jnp.fl...  8.25 us
    all_to_all x1, waiting for transfers between devices, local(): lax.all_to_all(heads_out, 'exp', split_axis=0, concat_axis=1, tiled=True)  7.48 us
  transfers between devices with their start and end apart: 2, of which 1 were waited for; matrix products, arithmetic and copies ran while one was open for 6% of the time, Pallas kernels for 21%

profile of v8, /device:TPU:1, one launch (start us, length us, event | category | flops | bytes accessed | tf_op | source)
XLA Modules:
  0.0 256.2 jit_solution(9070746574916019343)
XLA Ops:
  6.5 0.7 all-gather.2.cloned.1.call-update
  7.4 1.0 fusion.78
  8.3 0.9 fusion.80.block_ref
  9.3 33.8 %shard_map.127 = bf16[8,2,32,1024]{3,2,1,0:T(8,128)(2,1)S(1)} custom-call(bf16[32,1024]{1,0:T(8,128)(2,1)S(1)} %fusion.80.block_ref), custom_call_target="tpu_custom_call" | custom-call | tf_op jit(solution)/shard_map/pallas_call | solution.py:296
  43.7 1.5 convolution_convert_fusion.1
  45.3 0.8 slice.93.block_ref
  46.4 19.0 %shard_map.128 = bf16[6,512,128]{2,1,0:T(8,128)(2,1)} custom-call(bf16[512,128]{1,0:T(8,128)(2,1)} %slice.93.block_ref), custom_call_target="tpu_custom_call" | custom-call | tf_op jit(solution)/shard_map/pallas_call | solution.py:158
  65.4 1.3 slice_bitcast_fusion.5
  66.6 1.6 fusion.118
  75.0 0.3 convolution_bitcast_fusion.6
  75.4 0.3 convolution_bitcast_fusion.5
  76.4 0.4 fusion.28
  76.9 0.4 fusion.32
  77.3 0.4 fusion.36
  77.8 0.4 fusion.17
  78.2 0.4 fusion.20
  78.6 0.8 reshape.585
  79.4 13.6 %all-to-all-start = ((bf16[16,2,1024]{2,1,0:T(2,128)(2,1)}), bf16[16,2,1024]{2,1,0:T(2,128)(2,1)S(1)}, u32[]{:S(2)}, u32[]{:S(2)}) async-start(bf16[16,2,1024]{2,1,0:T(2,128)(2,1)} %reshape.585), calls=%async_computation | async-start | bytes 131072 | tf_op jit(solution)/shard_map/all_to_all | solution.py:400
  93.4 7.5 %all-to-all-done = bf16[16,2,1024]{2,1,0:T(2,128)(2,1)S(1)} async-done(((bf16[16,2,1024]{2,1,0:T(2,128)(2,1)}), bf16[16,2,1024]{2,1,0:T(2,128)(2,1)S(1)}, u32[]{:S(2)}, u32[]{:S(2)}) %all-to-all-start) | async-done | bytes 65568 | tf_op jit(solution)/shard_map/all_to_all | solution.py:400
  101.3 2.2 multiply_reduce_fusion
  103.7 0.5 broadcast.544
  104.3 0.7 reduce.28
  105.0 11.8 %all_to_all.29 = bf16[16,2,2048]{2,1,0:T(2,128)(2,1)S(1)} all-to-all(bf16[16,2,2048]{2,1,0:T(2,128)(2,1)S(1)} %reshape.587), channel_id=1, replica_groups=mesh['seq'=32,'exp'=16] {'exp'}, dimensions={0} | all-to-all | bytes 262144 | tf_op jit(solution)/shard_map/all_to_all | solution.py:426
  117.0 42.0 %shard_map.129 = bf16[4,8,64,1024]{3,2,1,0:T(8,128)(2,1)S(1)} custom-call(bf16[64,1024]{1,0:T(8,128)(2,1)S(1)} %bitcast.138), custom_call_target="tpu_custom_call" | custom-call | tf_op jit(solution)/shard_map/pallas_call | solution.py:296
  159.0 1.9 copy-done.1
  160.9 1.2 convolution_bitcast_fusion.1
  162.2 8.2 %convolution_convert_fusion = bf16[2048,1024]{1,0:T(8,128)(2,1)} fusion(bf16[2048,1024]{1,0:T(8,128)(2,1)} %bitcast.135, f32[2048,1,128]{2,0,1:T(8,128)S(1)} %convolution_bitcast_fusion.1, bf16[1,1024,128]{2,1,0:T(8,128)(2,1)S(1)} %copy-done, bf16[1,1024,128]{2,1,0:T(8,128)(2,1)S(1)} %copy-done.7), kind=kOutput, calls=%fused_computation | convolution fusion | flops 1077411840 | bytes 9961472 | tf_op jit(solution)/shard_map/nef,ekf->nek/dot_general | solution.py:321
  170.5 2.2 copy-done.2
  172.6 52.1 %shard_map.130 = bf16[64,1024]{1,0:T(8,128)(2,1)S(1)} custom-call(bf16[4,8,64,1024]{3,2,1,0:T(8,128)(2,1)S(1)} %bitcast.136), custom_call_target="tpu_custom_call" | custom-call | tf_op jit(solution)/shard_map/pallas_call | solution.py:107
  224.7 0.7 reduce.29
  225.5 22.9 %all_to_all.30 = bf16[16,2,2048]{2,1,0:T(2,128)(2,1)S(1)} all-to-all(bf16[16,2,2048]{2,1,0:T(2,128)(2,1)S(1)} %reshape.589), channel_id=1, replica_groups=mesh['seq'=32,'exp'=16] {'exp'}, dimensions={0} | all-to-all | bytes 262144 | tf_op jit(solution)/shard_map/all_to_all | solution.py:438
  248.5 0.8 fusion.19
  (46 shorter events, 5.1 us)
Async XLA Ops:
  6.5 155.7 %copy-start = (bf16[1,1024,128]{2,1,0:T(8,128)(2,1)S(1)}, bf16[1,1024,128]{2,1,0:T(8,128)(2,1)}, u32[]{:S(2)}) copy-start(bf16[1,1024,128]{2,1,0:T(8,128)(2,1)} %param.25) | copy-start | bytes 786436
  6.5 94.7 %all-gather.2.cloned.1.call-start = ((), (), s32[]{:S(2)}) async-start(), calls=%async_computation.3 | async-start | bytes 2228224 | tf_op jit(solution)/shard_map/all_gather | solution.py:403
  76.9 16.2 %copy-start.6 = (s32[32]{0:T(128)S(1)}, s32[32]{0:T(128)}, u32[]{:S(2)}) copy-start(s32[32]{0:T(128)} %param.14) | copy-start | bytes 388
  76.9 24.4 %copy-start.3 = (bf16[32,1024]{1,0:T(8,128)(2,1)S(1)}, bf16[32,1024]{1,0:T(8,128)(2,1)}, u32[]{:S(2)}) copy-start(bf16[32,1024]{1,0:T(8,128)(2,1)} %param.13) | copy-start | bytes 196612
  77.8 25.7 %copy-start.5 = (f32[1024]{0:T(1024)S(1)}, f32[1024]{0:T(1024)}, u32[]{:S(2)}) copy-start(f32[1024]{0:T(1024)} %param.22) | copy-start | bytes 12292
  79.4 21.4 %all-to-all-start = ((bf16[16,2,1024]{2,1,0:T(2,128)(2,1)}), bf16[16,2,1024]{2,1,0:T(2,128)(2,1)S(1)}, u32[]{:S(2)}, u32[]{:S(2)}) async-start(bf16[16,2,1024]{2,1,0:T(2,128)(2,1)} %reshape.585), calls=%async_computation | async-start | bytes 131072 | tf_op jit(solution)/shard_map/all_to_all | solution.py:400
  101.2 59.7 %copy-start.4 = (bf16[1,1024,128]{2,1,0:T(8,128)(2,1)S(1)}, bf16[1,1024,128]{2,1,0:T(8,128)(2,1)}, u32[]{:S(2)}) copy-start(bf16[1,1024,128]{2,1,0:T(8,128)(2,1)} %param.23) | copy-start | bytes 786436
  159.0 1.9 copy-start.1
  159.0 3.2 %copy-start.7 = (bf16[1,1024,128]{2,1,0:T(8,128)(2,1)S(1)}, bf16[1,1024,128]{2,1,0:T(8,128)(2,1)}, u32[]{:S(2)}) copy-start(bf16[1,1024,128]{2,1,0:T(8,128)(2,1)} %param.24) | copy-start | bytes 786436
  170.5 2.2 copy-start.2
Sparse Core Ops, SparseCore 0:
  9.5 49.2 all-gather.1

commit v9 on v8

--- a/solution.py
+++ b/solution.py
@@ -201,7 +201,7 @@
     )(x)
 
 
-def ring_gather_kernel(nx, ny, axis, other, block_ref, out_ref, local_sem, send_sems, recv_sems):
+def ring_gather_kernel(nx, ny, axis, other, pieces, block_ref, out_ref, local_sem, send_sems, recv_sems):
     me = lax.axis_index(axis)
     col = lax.axis_index(other)
     x = me // ny
@@ -259,10 +259,13 @@
         return steps
 
     plans = []
-    for lo, hi, first, second in ((0, hr, "y", "x"), (hr, rows, "x", "y")):
-        s1 = ring(first, 1, lo, hi)
-        s2 = ring(second, 2, lo, hi)
-        plans.append((s1, s2))
+    step = hr // pieces
+    for p in range(pieces):
+        for base, first, second in ((0, "y", "x"), (hr, "x", "y")):
+            lo = base + p * step
+            s1 = ring(first, 1, lo, lo + step)
+            s2 = ring(second, 2, lo, lo + step)
+            plans.append((s1, s2))
 
     started = []
 
@@ -290,11 +293,11 @@
         cp.wait_send()
 
 
-def ring_gather(block, nx, ny, axis="seq", other="exp", cid=3):
+def ring_gather(block, nx, ny, axis="seq", other="exp", cid=3, pieces=1):
     vmem = pltpu.MemorySpace.VMEM
-    n_sems = 4 * (nx // 2 + ny // 2) + 4
+    n_sems = 4 * pieces * (nx // 2 + ny // 2) + 4
     return pl.pallas_call(
-        functools.partial(ring_gather_kernel, nx, ny, axis, other),
+        functools.partial(ring_gather_kernel, nx, ny, axis, other, pieces),
         out_shape=jax.ShapeDtypeStruct((nx, ny) + block.shape, block.dtype),
         in_specs=[pl.BlockSpec(memory_space=vmem)],
         out_specs=pl.BlockSpec(memory_space=vmem),
@@ -427,7 +430,7 @@
     n_seq = lax.axis_size("seq")
     y_size = Y_RING if n_seq % Y_RING == 0 else n_seq
     gathered = ring_gather(
-        arrived.reshape(arrived.shape[0], width), n_seq // y_size, y_size
+        arrived.reshape(arrived.shape[0], width), n_seq // y_size, y_size, pieces=2
     ).reshape((n_seq * arrived.shape[0],) + arrived.shape[1:])
     n_seq = lax.axis_size("seq")
     y_size = Y_RING if n_seq % Y_RING == 0 else n_seq

time: 257 us -> 252 us (0.981)
  Pallas kernels: 147 us -> 141 us
    pallas_call x2, Pallas kernels: 75.8 us -> 72.2 us  [ring_gather(): pl.pallas_call(functools.partial(ring_gather_kernel, nx, ny, axis, other,...]
where the time goes in v9:
time: 252 us; the launch traced here: 251 us
  Pallas kernels  141 us (56%)
  blocking collectives  35.3 us (14%)
  matrix products  18.9 us (7%)
  between operations  18.7 us (7%)
  starting transfers between devices  13.6 us (5%)
  local copies, waits for them, and re-layouts  9.96 us (4%)
  waiting for transfers between devices  8.21 us (3%)
  other arithmetic  5.16 us (2%)
    pallas_call x2, Pallas kernels, ring_gather(): pl.pallas_call(functools.partial(ring_gather_kernel, nx, ny, axis, other,...  72.2 us
    pallas_call x1, Pallas kernels, ring_reduce(): pl.pallas_call(functools.partial(ring_reduce_kernel, nx, ny, splits), out...  49.8 us
    all_to_all x1, blocking collectives, local(): lax.all_to_all(summed, 'exp', split_axis=0, concat_axis=0, tiled=True)  23.6 us
    pallas_call x1, Pallas kernels, shift_exchange(): pl.pallas_call(functools.partial(shift_exchange_kernel, tuple(offsets), a...  19 us
    all_to_all x1, starting transfers between devices, local(): lax.all_to_all(heads_out, 'exp', split_axis=0, concat_axis=1, tiled=True)  13.6 us
    all_to_all x1, blocking collectives, local(): lax.all_to_all(outgoing, 'exp', split_axis=0, concat_axis=0, tiled=True)  11.8 us
    dot_general x1, matrix products, expert_terms(): jnp.einsum('nef,ekf->nek', act, down_slice, preferred_element_type=jnp.fl...  8.25 us
    all_to_all x1, waiting for transfers between devices, local(): lax.all_to_all(heads_out, 'exp', split_axis=0, concat_axis=1, tiled=True)  7.48 us
  transfers between devices with their start and end apart: 2, of which 1 were waited for; matrix products, arithmetic and copies ran while one was open for 6% of the time, Pallas kernels for 21%

profile of v9, /device:TPU:1, one launch (start us, length us, event | category | flops | bytes accessed | tf_op | source)
XLA Modules:
  0.0 251.1 jit_solution(9653388743278374338)
XLA Ops:
  6.5 0.7 all-gather.2.cloned.1.call-update
  7.4 1.0 fusion.78
  8.3 0.9 fusion.80.block_ref
  9.3 33.8 %shard_map.127 = bf16[8,2,32,1024]{3,2,1,0:T(8,128)(2,1)S(1)} custom-call(bf16[32,1024]{1,0:T(8,128)(2,1)S(1)} %fusion.80.block_ref), custom_call_target="tpu_custom_call" | custom-call | tf_op jit(solution)/shard_map/pallas_call | solution.py:299
  43.7 1.5 convolution_convert_fusion.1
  45.3 0.8 slice.93.block_ref
  46.4 19.0 %shard_map.128 = bf16[6,512,128]{2,1,0:T(8,128)(2,1)} custom-call(bf16[512,128]{1,0:T(8,128)(2,1)} %slice.93.block_ref), custom_call_target="tpu_custom_call" | custom-call | tf_op jit(solution)/shard_map/pallas_call | solution.py:158
  65.4 1.3 slice_bitcast_fusion.5
  66.6 1.6 fusion.118
  75.0 0.3 convolution_bitcast_fusion.6
  75.4 0.3 convolution_bitcast_fusion.5
  76.4 0.4 fusion.28
  76.9 0.4 fusion.32
  77.3 0.4 fusion.36
  77.8 0.4 fusion.17
  78.2 0.4 fusion.20
  78.6 0.8 reshape.585
  79.4 13.6 %all-to-all-start = ((bf16[16,2,1024]{2,1,0:T(2,128)(2,1)}), bf16[16,2,1024]{2,1,0:T(2,128)(2,1)S(1)}, u32[]{:S(2)}, u32[]{:S(2)}) async-start(bf16[16,2,1024]{2,1,0:T(2,128)(2,1)} %reshape.585), calls=%async_computation | async-start | bytes 131072 | tf_op jit(solution)/shard_map/all_to_all | solution.py:403
  93.4 7.5 %all-to-all-done = bf16[16,2,1024]{2,1,0:T(2,128)(2,1)S(1)} async-done(((bf16[16,2,1024]{2,1,0:T(2,128)(2,1)}), bf16[16,2,1024]{2,1,0:T(2,128)(2,1)S(1)}, u32[]{:S(2)}, u32[]{:S(2)}) %all-to-all-start) | async-done | bytes 65568 | tf_op jit(solution)/shard_map/all_to_all | solution.py:403
  101.3 2.2 multiply_reduce_fusion
  103.7 0.5 broadcast.544
  104.3 0.7 reduce.28
  105.0 11.8 %all_to_all.29 = bf16[16,2,2048]{2,1,0:T(2,128)(2,1)S(1)} all-to-all(bf16[16,2,2048]{2,1,0:T(2,128)(2,1)S(1)} %reshape.587), channel_id=1, replica_groups=mesh['seq'=32,'exp'=16] {'exp'}, dimensions={0} | all-to-all | bytes 262144 | tf_op jit(solution)/shard_map/all_to_all | solution.py:429
  117.0 38.4 %shard_map.129 = bf16[4,8,64,1024]{3,2,1,0:T(8,128)(2,1)S(1)} custom-call(bf16[64,1024]{1,0:T(8,128)(2,1)S(1)} %bitcast.138), custom_call_target="tpu_custom_call" | custom-call | tf_op jit(solution)/shard_map/pallas_call | solution.py:299
  155.4 1.9 copy-done.1
  157.4 1.2 convolution_bitcast_fusion.1
  158.6 8.2 %convolution_convert_fusion = bf16[2048,1024]{1,0:T(8,128)(2,1)} fusion(bf16[2048,1024]{1,0:T(8,128)(2,1)} %bitcast.135, f32[2048,1,128]{2,0,1:T(8,128)S(1)} %convolution_bitcast_fusion.1, bf16[1,1024,128]{2,1,0:T(8,128)(2,1)S(1)} %copy-done, bf16[1,1024,128]{2,1,0:T(8,128)(2,1)S(1)} %copy-done.7), kind=kOutput, calls=%fused_computation | convolution fusion | flops 1077411840 | bytes 9961472 | tf_op jit(solution)/shard_map/nef,ekf->nek/dot_general | solution.py:324
  166.9 2.2 copy-done.2
  169.1 49.8 %shard_map.130 = bf16[64,1024]{1,0:T(8,128)(2,1)S(1)} custom-call(bf16[4,8,64,1024]{3,2,1,0:T(8,128)(2,1)S(1)} %bitcast.136), custom_call_target="tpu_custom_call" | custom-call | tf_op jit(solution)/shard_map/pallas_call | solution.py:107
  218.9 0.7 reduce.29
  219.7 23.6 %all_to_all.30 = bf16[16,2,2048]{2,1,0:T(2,128)(2,1)S(1)} all-to-all(bf16[16,2,2048]{2,1,0:T(2,128)(2,1)S(1)} %reshape.589), channel_id=1, replica_groups=mesh['seq'=32,'exp'=16] {'exp'}, dimensions={0} | all-to-all | bytes 262144 | tf_op jit(solution)/shard_map/all_to_all | solution.py:441
  243.4 0.8 fusion.19
  (46 shorter events, 5.1 us)
Async XLA Ops:
  6.5 152.1 %copy-start = (bf16[1,1024,128]{2,1,0:T(8,128)(2,1)S(1)}, bf16[1,1024,128]{2,1,0:T(8,128)(2,1)}, u32[]{:S(2)}) copy-start(bf16[1,1024,128]{2,1,0:T(8,128)(2,1)} %param.25) | copy-start | bytes 786436
  6.5 94.7 %all-gather.2.cloned.1.call-start = ((), (), s32[]{:S(2)}) async-start(), calls=%async_computation.3 | async-start | bytes 2228224 | tf_op jit(solution)/shard_map/all_gather | solution.py:406
  76.9 16.2 %copy-start.6 = (s32[32]{0:T(128)S(1)}, s32[32]{0:T(128)}, u32[]{:S(2)}) copy-start(s32[32]{0:T(128)} %param.14) | copy-start | bytes 388
  76.9 24.4 %copy-start.3 = (bf16[32,1024]{1,0:T(8,128)(2,1)S(1)}, bf16[32,1024]{1,0:T(8,128)(2,1)}, u32[]{:S(2)}) copy-start(bf16[32,1024]{1,0:T(8,128)(2,1)} %param.13) | copy-start | bytes 196612
  77.8 25.7 %copy-start.5 = (f32[1024]{0:T(1024)S(1)}, f32[1024]{0:T(1024)}, u32[]{:S(2)}) copy-start(f32[1024]{0:T(1024)} %param.22) | copy-start | bytes 12292
  79.4 21.4 %all-to-all-start = ((bf16[16,2,1024]{2,1,0:T(2,128)(2,1)}), bf16[16,2,1024]{2,1,0:T(2,128)(2,1)S(1)}, u32[]{:S(2)}, u32[]{:S(2)}) async-start(bf16[16,2,1024]{2,1,0:T(2,128)(2,1)} %reshape.585), calls=%async_computation | async-start | bytes 131072 | tf_op jit(solution)/shard_map/all_to_all | solution.py:403
  101.2 56.1 %copy-start.4 = (bf16[1,1024,128]{2,1,0:T(8,128)(2,1)S(1)}, bf16[1,1024,128]{2,1,0:T(8,128)(2,1)}, u32[]{:S(2)}) copy-start(bf16[1,1024,128]{2,1,0:T(8,128)(2,1)} %param.23) | copy-start | bytes 786436
  155.4 1.9 copy-start.1
  155.4 3.2 %copy-start.7 = (bf16[1,1024,128]{2,1,0:T(8,128)(2,1)S(1)}, bf16[1,1024,128]{2,1,0:T(8,128)(2,1)}, u32[]{:S(2)}) copy-start(bf16[1,1024,128]{2,1,0:T(8,128)(2,1)} %param.24) | copy-start | bytes 786436
  166.9 2.2 copy-start.2
Sparse Core Ops, SparseCore 0:
  9.5 49.2 all-gather.1

commit v10 on v9

--- a/solution.py
+++ b/solution.py
@@ -124,6 +124,126 @@
             collective_id=1, has_side_effects=True, vmem_limit_bytes=48 * 1024 * 1024
         ),
     )(part)
+
+
+def ring_ffn_kernel(nx, ny, splits, tok_ref, wg_ref, wu_ref, wd_ref, out_ref, pbuf, recv1, send1,
+                    acc, recv2, send2, s1_send, s1_recv, s2_send, s2_recv):
+    me = lax.axis_index("seq")
+    col = lax.axis_index("exp")
+    x = me // ny
+    y = me % ny
+    y_up = x * ny + (y + 1) % ny
+    y_down = x * ny + (y + ny - 1) % ny
+    x_up = ((x + 1) % nx) * ny + y
+    x_down = ((x + nx - 1) % nx) * ny + y
+    rows = tok_ref.shape[2]
+    width = tok_ref.shape[3]
+    piece = rows // splits
+    quarter = rows // 4
+    half_x = nx // 2
+
+    def partials(c_up, c_down):
+        tok = jnp.concatenate(
+            [tok_ref[0:half_x, c_up].reshape(half_x * rows, width),
+             tok_ref[half_x:nx, c_down].reshape((nx - half_x) * rows, width)], axis=0)
+        gate = jnp.dot(tok, wg_ref[...], preferred_element_type=jnp.float32)
+        upward = jnp.dot(tok, wu_ref[...], preferred_element_type=jnp.float32)
+        act = (gate / (1.0 + jnp.exp(-gate)) * upward).astype(jnp.bfloat16)
+        down = lax.dot_general(act, wd_ref[...], (((1,), (1,)), ((), ())),
+                               preferred_element_type=jnp.float32)
+        pbuf[...] = down.astype(jnp.bfloat16).reshape(nx, rows, width)
+
+    barrier = pltpu.get_barrier_semaphore()
+    for peer in (y_up, y_down, x_up, x_down):
+        pl.semaphore_signal(barrier, inc=1, device_id=(peer, col),
+                            device_id_type=pl.DeviceIdType.MESH)
+    pl.semaphore_wait(barrier, 4)
+
+    lanes = []
+    for a in range(nx):
+        for p in range(splits):
+            if a < half_x:
+                lanes.append((y_up, 1, a, p * piece))
+            else:
+                lanes.append((y_down, -1, a, p * piece))
+    copies1 = []
+    for k in range(ny - 1):
+        partials((y - k - 1 + ny) % ny, (y + k + 1) % ny)
+        step_copies = []
+        for d, (peer, sign, a, r0) in enumerate(lanes):
+            if k == 0:
+                send1[d, k] = pbuf[a, r0:r0 + piece]
+            else:
+                copies1[k - 1][d].wait_recv()
+                send1[d, k] = (recv1[d, k - 1].astype(jnp.float32)
+                               + pbuf[a, r0:r0 + piece].astype(jnp.float32)).astype(send1.dtype)
+            cp = pltpu.make_async_remote_copy(
+                src_ref=send1.at[d, k], dst_ref=recv1.at[d, k],
+                send_sem=s1_send.at[d, k], recv_sem=s1_recv.at[d, k],
+                device_id=(peer, col), device_id_type=pl.DeviceIdType.MESH)
+            cp.start()
+            step_copies.append(cp)
+        copies1.append(step_copies)
+    partials(y, y)
+    for d, (peer, sign, a, r0) in enumerate(lanes):
+        copies1[ny - 2][d].wait_recv()
+        acc[a, r0:r0 + piece] = (recv1[d, ny - 2].astype(jnp.float32)
+                                 + pbuf[a, r0:r0 + piece].astype(jnp.float32))
+
+    lanes2 = [(x_up, 1, 0), (x_up, 1, quarter), (x_down, -1, 2 * quarter), (x_down, -1, 3 * quarter)]
+    copies2 = []
+    for k in range(nx - 1):
+        step_copies = []
+        for d, (peer, sign, r0) in enumerate(lanes2):
+            c = (x - sign * (k + 1) + 2 * nx) % nx
+            if k == 0:
+                src = acc.at[c, r0:r0 + quarter]
+            else:
+                copies2[k - 1][d].wait_recv()
+                send2[d, k] = recv2[d, k - 1] + acc[c, r0:r0 + quarter]
+                src = send2.at[d, k]
+            cp = pltpu.make_async_remote_copy(
+                src_ref=src, dst_ref=recv2.at[d, k],
+                send_sem=s2_send.at[d, k], recv_sem=s2_recv.at[d, k],
+                device_id=(peer, col), device_id_type=pl.DeviceIdType.MESH)
+            cp.start()
+            step_copies.append(cp)
+        copies2.append(step_copies)
+    for d, (peer, sign, r0) in enumerate(lanes2):
+        copies2[nx - 2][d].wait_recv()
+        out_ref[r0:r0 + quarter] = (recv2[d, nx - 2] + acc[x, r0:r0 + quarter]).astype(out_ref.dtype)
+    for step_copies in copies1 + copies2:
+        for cp in step_copies:
+            cp.wait_send()
+
+
+def ring_ffn(tokens, w_gate, w_up, w_down, nx, ny, splits=2):
+    width = tokens.shape[-1]
+    rows = tokens.shape[0] // (nx * ny)
+    tokens = tokens.reshape(nx, ny, rows, width)
+    n1 = nx * splits
+    vmem = pltpu.MemorySpace.VMEM
+    return pl.pallas_call(
+        functools.partial(ring_ffn_kernel, nx, ny, splits),
+        out_shape=jax.ShapeDtypeStruct((rows, width), jnp.bfloat16),
+        in_specs=[pl.BlockSpec(memory_space=vmem)] * 4,
+        out_specs=pl.BlockSpec(memory_space=vmem),
+        scratch_shapes=[
+            pltpu.VMEM((nx, rows, width), jnp.bfloat16),
+            pltpu.VMEM((n1, ny - 1, rows // splits, width), jnp.bfloat16),
+            pltpu.VMEM((n1, ny - 1, rows // splits, width), jnp.bfloat16),
+            pltpu.VMEM((nx, rows, width), jnp.float32),
+            pltpu.VMEM((4, nx - 1, rows // 4, width), jnp.float32),
+            pltpu.VMEM((4, nx - 1, rows // 4, width), jnp.float32),
+            pltpu.SemaphoreType.DMA((n1, ny - 1)),
+            pltpu.SemaphoreType.DMA((n1, ny - 1)),
+            pltpu.SemaphoreType.DMA((4, nx - 1)),
+            pltpu.SemaphoreType.DMA((4, nx - 1)),
+        ],
+        compiler_params=pltpu.CompilerParams(
+            collective_id=5, has_side_effects=True, vmem_limit_bytes=56 * 1024 * 1024
+        ),
+    )(tokens, w_gate, w_up, w_down)
 
 
 def shift_exchange_kernel(offsets, axis, other, block_ref, out_ref, send_sems, recv_sems):
@@ -434,10 +554,10 @@
     ).reshape((n_seq * arrived.shape[0],) + arrived.shape[1:])
     n_seq = lax.axis_size("seq")
     y_size = Y_RING if n_seq % Y_RING == 0 else n_seq
-    partial = expert_terms(gathered, w_gate, w_up, w_down).astype(jnp.bfloat16)
-    summed = ring_reduce(
-        partial.reshape(partial.shape[0], width), n_seq // y_size, y_size
-    ).reshape((-1,) + partial.shape[1:])
+    summed = ring_ffn(
+        gathered.reshape(gathered.shape[0], width),
+        w_gate[0], w_up[0], w_down[0], n_seq // y_size, y_size,
+    ).reshape((-1,) + gathered.shape[1:])
     returned = lax.all_to_all(summed, "exp", split_axis=0, concat_axis=0, tiled=True)
     expert_out = jnp.dot(
         jnp.transpose(selector),

time: 252 us -> 247 us (0.980)
  matrix products: 18.9 us -> 10.3 us
  starting transfers between devices: 13.6 us -> 16.5 us
    dot_general x2 -> x0, matrix products: 9.49 us -> none  [the longest x1 8.25 us: expert_terms(): jnp.einsum('nef,ekf->nek', act, down_slice, preferred_element_type=jnp.fl...]
    pallas_call x1, Pallas kernels: 49.8 us -> 54.6 us  [ring_ffn(): pl.pallas_call(functools.partial(ring_ffn_kernel, nx, ny, splits), out_sh...]
    all_to_all x1, starting transfers between devices: 13.6 us -> 16.5 us  [local(): lax.all_to_all(heads_out, 'exp', split_axis=0, concat_axis=1, tiled=True)]
    unnamed x23 -> x27, local copies, waits for them, and re-layouts: 5.5 us -> 3.34 us
  transfers between devices with their start and end apart: 2 -> 2, of which waited for: 1 -> 1; matrix products, arithmetic and copies ran while one was open for 6% -> 7% of each run, Pallas kernels for 21% -> 21%
where the time goes in v10:
time: 247 us; the launch traced here: 246 us
  Pallas kernels  143 us (58%)
  blocking collectives  35.2 us (14%)
  between operations  18.9 us (8%)
  starting transfers between devices  16.5 us (7%)
  matrix products  10.3 us (4%)
  local copies, waits for them, and re-layouts  8.59 us (3%)
  waiting for transfers between devices  8.21 us (3%)
  other arithmetic  6.06 us (2%)
    pallas_call x2, Pallas kernels, ring_gather(): pl.pallas_call(functools.partial(ring_gather_kernel, nx, ny, axis, other,...  69.9 us
    pallas_call x1, Pallas kernels, ring_ffn(): pl.pallas_call(functools.partial(ring_ffn_kernel, nx, ny, splits), out_sh...  54.6 us
    all_to_all x1, blocking collectives, local(): lax.all_to_all(summed, 'exp', split_axis=0, concat_axis=0, tiled=True)  23.4 us
    pallas_call x1, Pallas kernels, shift_exchange(): pl.pallas_call(functools.partial(shift_exchange_kernel, tuple(offsets), a...  18.2 us
    all_to_all x1, starting transfers between devices, local(): lax.all_to_all(heads_out, 'exp', split_axis=0, concat_axis=1, tiled=True)  16.5 us
    all_to_all x1, blocking collectives, local(): lax.all_to_all(outgoing, 'exp', split_axis=0, concat_axis=0, tiled=True)  11.8 us
    all_to_all x1, waiting for transfers between devices, local(): lax.all_to_all(heads_out, 'exp', split_axis=0, concat_axis=1, tiled=True)  7.48 us
  transfers between devices with their start and end apart: 2, of which 1 were waited for; matrix products, arithmetic and copies ran while one was open for 7% of the time, Pallas kernels for 21%

profile of v10, /device:TPU:1, one launch (start us, length us, event | category | flops | bytes accessed | tf_op | source)
XLA Modules:
  0.0 246.4 jit_solution(13853849776165709281)
XLA Ops:
  6.5 0.7 all-gather.2.cloned.1.call-update
  8.0 1.0 fusion.65
  9.0 0.9 fusion.67.block_ref
  9.9 33.8 %shard_map.127 = bf16[8,2,32,1024]{3,2,1,0:T(8,128)(2,1)S(1)} custom-call(bf16[32,1024]{1,0:T(8,128)(2,1)S(1)} %fusion.67.block_ref), custom_call_target="tpu_custom_call" | custom-call | tf_op jit(solution)/shard_map/pallas_call | solution.py:419
  43.7 1.5 convolution_convert_fusion
  45.2 0.8 slice.93.block_ref
  46.0 18.2 %shard_map.128 = bf16[6,512,128]{2,1,0:T(8,128)(2,1)} custom-call(bf16[512,128]{1,0:T(8,128)(2,1)} %slice.93.block_ref), custom_call_target="tpu_custom_call" | custom-call | tf_op jit(solution)/shard_map/pallas_call | solution.py:278
  64.2 2.0 slice_bitcast_fusion.5
  66.2 0.3 fusion.110
  67.3 1.3 fusion.107
  68.5 1.6 fusion.104
  76.6 0.3 convolution_bitcast_fusion.3
  76.9 0.3 convolution_bitcast_fusion.4
  77.3 0.3 convolution_bitcast_fusion.5
  77.6 0.4 fusion.24
  78.1 0.4 fusion.20
  78.5 0.4 fusion.28
  79.0 0.4 fusion.14
  79.3 0.3 fusion.17
  79.8 0.8 reshape.557
  80.6 16.5 %all-to-all-start = ((bf16[16,2,1024]{2,1,0:T(2,128)(2,1)}), bf16[16,2,1024]{2,1,0:T(2,128)(2,1)S(1)}, u32[]{:S(2)}, u32[]{:S(2)}) async-start(bf16[16,2,1024]{2,1,0:T(2,128)(2,1)} %reshape.557), calls=%async_computation | async-start | bytes 131072 | tf_op jit(solution)/shard_map/all_to_all | solution.py:523
  97.4 7.5 %all-to-all-done = bf16[16,2,1024]{2,1,0:T(2,128)(2,1)S(1)} async-done(((bf16[16,2,1024]{2,1,0:T(2,128)(2,1)}), bf16[16,2,1024]{2,1,0:T(2,128)(2,1)S(1)}, u32[]{:S(2)}, u32[]{:S(2)}) %all-to-all-start) | async-done | bytes 65568 | tf_op jit(solution)/shard_map/all_to_all | solution.py:523
  105.3 2.2 multiply_reduce_fusion
  107.7 0.5 broadcast.542
  108.2 0.7 reduce.28
  109.0 11.8 %all_to_all.29 = bf16[16,2,2048]{2,1,0:T(2,128)(2,1)S(1)} all-to-all(bf16[16,2,2048]{2,1,0:T(2,128)(2,1)S(1)} %reshape.559), channel_id=1, replica_groups=mesh['seq'=32,'exp'=16] {'exp'}, dimensions={0} | all-to-all | bytes 262144 | tf_op jit(solution)/shard_map/all_to_all | solution.py:549
  121.0 36.1 %shard_map.129.tok_ref = bf16[4,8,64,1024]{3,2,1,0:T(8,128)(2,1)S(1)} custom-call(bf16[64,1024]{1,0:T(8,128)(2,1)S(1)} %bitcast.94), custom_call_target="tpu_custom_call" | custom-call | tf_op jit(solution)/shard_map/pallas_call | solution.py:419
  157.0 1.9 copy-done
  159.0 54.6 %shard_map.130 = bf16[64,1024]{1,0:T(8,128)(2,1)} custom-call(bf16[4,8,64,1024]{3,2,1,0:T(8,128)(2,1)} %copy-done, bf16[1024,128]{1,0:T(8,128)(2,1)} %bitcast.98, bf16[1024,128]{1,0:T(8,128)(2,1)} %bitcast.99, bf16[1024,128]{1,0:T(8,128)(2,1)} %bitcast.100), custom_call_target="tpu_custom_call" | custom-call | tf_op jit(solution)/shard_map/pallas_call | solution.py:226
  213.5 1.6 reduce.29
  215.2 23.4 %all_to_all.30 = bf16[16,2,2048]{2,1,0:T(2,128)(2,1)S(1)} all-to-all(bf16[16,2,2048]{2,1,0:T(2,128)(2,1)S(1)} %reshape.561), channel_id=1, replica_groups=mesh['seq'=32,'exp'=16] {'exp'}, dimensions={0} | all-to-all | bytes 262144 | tf_op jit(solution)/shard_map/all_to_all | solution.py:561
  238.8 0.8 fusion.16
  (48 shorter events, 4.1 us)
Async XLA Ops:
  6.5 98.7 %all-gather.2.cloned.1.call-start = ((), (), s32[]{:S(2)}) async-start(), calls=%async_computation.3 | async-start | bytes 2228224 | tf_op jit(solution)/shard_map/all_gather | solution.py:526
  66.2 0.7 copy-start.6
  67.3 7.6 %copy-start.4 = (bf16[512,128]{1,0:T(8,128)(2,1)S(1)}, bf16[512,128]{1,0:T(8,128)(2,1)}, u32[]{:S(2)}) copy-start(bf16[512,128]{1,0:T(8,128)(2,1)} %get-tuple-element.24) | copy-start | bytes 393220
  67.3 7.9 %copy-start.3 = (bf16[512,128]{1,0:T(8,128)(2,1)S(1)}, bf16[512,128]{1,0:T(8,128)(2,1)}, u32[]{:S(2)}) copy-start(bf16[512,128]{1,0:T(8,128)(2,1)} %get-tuple-element.25) | copy-start | bytes 393220
  68.5 7.0 %copy-start.2 = (bf16[512,128]{1,0:T(8,128)(2,1)S(1)}, bf16[512,128]{1,0:T(8,128)(2,1)}, u32[]{:S(2)}) copy-start(bf16[512,128]{1,0:T(8,128)(2,1)} %get-tuple-element.20) | copy-start | bytes 393220
  71.1 4.8 %copy-start.7 = (bf16[512,128]{1,0:T(8,128)(2,1)S(1)}, bf16[512,128]{1,0:T(8,128)(2,1)}, u32[]{:S(2)}) copy-start(bf16[512,128]{1,0:T(8,128)(2,1)} %copy-done.6) | copy-start | bytes 393220
  75.2 1.0 copy-start.5
  79.0 18.1 %copy-start.9 = (s32[32]{0:T(128)S(1)}, s32[32]{0:T(128)}, u32[]{:S(2)}) copy-start(s32[32]{0:T(128)} %param.14) | copy-start | bytes 388
  79.0 26.3 %copy-start.1 = (bf16[32,1024]{1,0:T(8,128)(2,1)S(1)}, bf16[32,1024]{1,0:T(8,128)(2,1)}, u32[]{:S(2)}) copy-start(bf16[32,1024]{1,0:T(8,128)(2,1)} %param.13) | copy-start | bytes 196612
  79.7 27.8 %copy-start.8 = (f32[1024]{0:T(1024)S(1)}, f32[1024]{0:T(1024)}, u32[]{:S(2)}) copy-start(f32[1024]{0:T(1024)} %param.22) | copy-start | bytes 12292
  80.6 24.3 %all-to-all-start = ((bf16[16,2,1024]{2,1,0:T(2,128)(2,1)}), bf16[16,2,1024]{2,1,0:T(2,128)(2,1)S(1)}, u32[]{:S(2)}, u32[]{:S(2)}) async-start(bf16[16,2,1024]{2,1,0:T(2,128)(2,1)} %reshape.557), calls=%async_computation | async-start | bytes 131072 | tf_op jit(solution)/shard_map/all_to_all | solution.py:523
  157.0 1.9 copy-start
Sparse Core Ops, SparseCore 0:
  9.5 49.0 all-gather.1

commit v11 on v10

--- a/solution.py
+++ b/solution.py
@@ -480,43 +480,30 @@
     position = lax.axis_index("seq")
     head_scale = logit_scale[:, None, None]
 
-    def attend(state, kv_block, source):
-        row_top, weight_sum, numerator = state
-        key_rows = kv_block[:, :head_cols].reshape(block_len, heads_dev, head_size)
-        value_rows = kv_block[:, head_cols:].reshape(block_len, heads_dev, head_size)
-        allowed = block_pattern[position, source] > 0
-        scores = (
-            jnp.einsum("qhd,khd->hqk", query_heads, key_rows, preferred_element_type=jnp.float32)
-            * head_scale
-        )
-        block_top = jnp.max(scores, axis=2)
-        new_top = jnp.where(allowed, jnp.maximum(row_top, block_top), row_top)
-        shifted = jnp.minimum(scores - new_top[:, :, None], 0.0)
-        weights = jnp.where(allowed, jnp.exp(shifted), 0.0)
-        rescale = jnp.exp(row_top - new_top)
-        weight_sum = weight_sum * rescale + jnp.sum(weights, axis=2)
-        contrib = jnp.einsum(
-            "hqk,khd->qhd",
-            weights.astype(jnp.bfloat16),
-            value_rows,
-            preferred_element_type=jnp.float32,
-        )
-        numerator = numerator * jnp.transpose(rescale)[:, :, None] + contrib
-        return (new_top, weight_sum, numerator)
-
-    start_state = (
-        jnp.full((heads_dev, block_len), -jnp.inf, jnp.float32),
-        jnp.zeros((heads_dev, block_len), jnp.float32),
-        jnp.zeros((block_len, heads_dev, head_size), jnp.float32),
-    )
-    state = attend(start_state, key_value, position)
     offsets = [d for d in range(1, REACH + 1)] + [-d for d in range(1, REACH + 1)]
     neighbours = shift_exchange(key_value, offsets, "seq", "exp", 2)
-    for distance in range(1, REACH + 1):
-        state = attend(state, neighbours[distance - 1], (position - distance) % n_blocks)
-        state = attend(state, neighbours[REACH + distance - 1], (position + distance) % n_blocks)
+    band = jnp.concatenate([key_value[None], neighbours], axis=0)
+    n_band = band.shape[0]
+    sources = jnp.stack([position] + [(position - o) % n_blocks for o in offsets])
+    allowed = jnp.repeat(block_pattern[position, sources] > 0, block_len)
+    key_band = band[:, :, :head_cols].reshape(n_band * block_len, heads_dev, head_size)
+    value_band = band[:, :, head_cols:].reshape(n_band * block_len, heads_dev, head_size)
+    scores = (
+        jnp.einsum("qhd,khd->hqk", query_heads, key_band, preferred_element_type=jnp.float32)
+        * head_scale
+    )
+    scores = jnp.where(allowed[None, None, :], scores, -jnp.inf)
+    row_top = jnp.max(scores, axis=2, keepdims=True)
+    weights = jnp.exp(scores - row_top)
+    weight_sum = jnp.sum(weights, axis=2)
+    weighted = jnp.einsum(
+        "hqk,khd->qhd",
+        weights.astype(jnp.bfloat16),
+        value_band,
+        preferred_element_type=jnp.float32,
+    )
     heads_out = (
-        (state[2] / jnp.transpose(state[1])[:, :, None])
+        (weighted / jnp.transpose(weight_sum)[:, :, None])
         .astype(jnp.bfloat16)
         .reshape(block_len, head_cols)
     )

time: 247 us -> 238 us (0.964)
  between operations: 18.9 us -> 14.4 us
  starting transfers between devices: 16.5 us -> 13.2 us
  Pallas kernels: 143 us -> 146 us
  matrix products: 10.3 us -> 7.43 us
  local copies, waits for them, and re-layouts: 8.59 us -> 5.76 us
    pallas_call x2, Pallas kernels: 69.9 us -> 73.2 us  [ring_gather(): pl.pallas_call(functools.partial(ring_gather_kernel, nx, ny, axis, other,...]
    all_to_all x1, starting transfers between devices: 16.5 us -> 13.2 us  [local(): lax.all_to_all(heads_out, 'exp', split_axis=0, concat_axis=1, tiled=True)]
    dot_general x14 -> x2, matrix products: 5.59 us -> 2.69 us  [the longest x1 1.37 us: local(): jnp.einsum('hqk,khd->qhd', weights.astype(jnp.bfloat16), value_band, pref...]
  transfers between devices with their start and end apart: 2 -> 2, of which waited for: 1 -> 1; matrix products, arithmetic and copies ran while one was open for 7% -> 5% of each run, Pallas kernels for 21% -> 22%
where the time goes in v11:
time: 238 us
  Pallas kernels  146 us (61%)
  blocking collectives  35.6 us (15%)
  between operations  14.4 us (6%)
  starting transfers between devices  13.2 us (6%)
  waiting for transfers between devices  8.21 us (3%)
  matrix products  7.43 us (3%)
  other arithmetic  7.35 us (3%)
  local copies, waits for them, and re-layouts  5.76 us (2%)
    pallas_call x2, Pallas kernels, ring_gather(): pl.pallas_call(functools.partial(ring_gather_kernel, nx, ny, axis, other,...  73.2 us
    pallas_call x1, Pallas kernels, ring_ffn(): pl.pallas_call(functools.partial(ring_ffn_kernel, nx, ny, splits), out_sh...  53.7 us
    all_to_all x1, blocking collectives, local(): lax.all_to_all(summed, 'exp', split_axis=0, concat_axis=0, tiled=True)  23.9 us
    pallas_call x1, Pallas kernels, shift_exchange(): pl.pallas_call(functools.partial(shift_exchange_kernel, tuple(offsets), a...  18.7 us
    all_to_all x1, starting transfers between devices, local(): lax.all_to_all(heads_out, 'exp', split_axis=0, concat_axis=1, tiled=True)  13.2 us
    all_to_all x1, blocking collectives, local(): lax.all_to_all(outgoing, 'exp', split_axis=0, concat_axis=0, tiled=True)  11.8 us
    all_to_all x1, waiting for transfers between devices, local(): lax.all_to_all(heads_out, 'exp', split_axis=0, concat_axis=1, tiled=True)  7.48 us
  transfers between devices with their start and end apart: 2, of which 1 were waited for; matrix products, arithmetic and copies ran while one was open for 5% of the time, Pallas kernels for 22%

profile of v11, /device:TPU:1, one launch (start us, length us, event | category | flops | bytes accessed | tf_op | source)
XLA Modules:
  0.0 237.6 jit_solution(15430245660911341716)
XLA Ops:
  6.5 0.7 all-gather.2.cloned.1.call-update
  7.3 1.0 fusion.24
  8.3 0.9 fusion.26.block_ref
  9.2 33.9 %shard_map.127 = bf16[8,2,32,1024]{3,2,1,0:T(8,128)(2,1)S(1)} custom-call(bf16[32,1024]{1,0:T(8,128)(2,1)S(1)} %fusion.26.block_ref), custom_call_target="tpu_custom_call" | custom-call | tf_op jit(solution)/shard_map/pallas_call | solution.py:419
  43.1 1.5 convolution_convert_fusion
  44.6 0.8 slice_bitcast_fusion
  45.4 18.7 %shard_map.128 = bf16[6,512,128]{2,1,0:T(8,128)(2,1)} custom-call(bf16[512,128]{1,0:T(8,128)(2,1)} %get-tuple-element.8.block_ref), custom_call_target="tpu_custom_call" | custom-call | tf_op jit(solution)/shard_map/pallas_call | solution.py:278
  64.9 0.7 gather_fusion
  65.7 1.7 pad_maximum_fusion
  67.4 1.3 fusion.40
  68.8 1.1 fusion
  69.9 1.4 fusion.16
  71.3 0.1 copy.24
  71.4 0.8 reshape.366
  72.2 13.2 %all-to-all-start = ((bf16[16,2,1024]{2,1,0:T(2,128)(2,1)}), bf16[16,2,1024]{2,1,0:T(2,128)(2,1)S(1)}, u32[]{:S(2)}, u32[]{:S(2)}) async-start(bf16[16,2,1024]{2,1,0:T(2,128)(2,1)} %reshape.366), calls=%async_computation | async-start | bytes 131072 | tf_op jit(solution)/shard_map/all_to_all | solution.py:510
  85.5 0.2 select_reduce_fusion
  85.7 7.5 %all-to-all-done = bf16[16,2,1024]{2,1,0:T(2,128)(2,1)S(1)} async-done(((bf16[16,2,1024]{2,1,0:T(2,128)(2,1)}), bf16[16,2,1024]{2,1,0:T(2,128)(2,1)S(1)}, u32[]{:S(2)}, u32[]{:S(2)}) %all-to-all-start) | async-done | bytes 65568 | tf_op jit(solution)/shard_map/all_to_all | solution.py:510
  93.1 0.1 reshape.367
  93.4 0.1 all_to_all.23
  93.5 2.2 multiply_reduce_fusion
  95.7 0.2 fusion.5
  96.0 0.5 broadcast.139
  96.5 0.7 reduce.4
  97.3 11.8 %all_to_all.29 = bf16[16,2,2048]{2,1,0:T(2,128)(2,1)S(1)} all-to-all(bf16[16,2,2048]{2,1,0:T(2,128)(2,1)S(1)} %reshape.368), channel_id=1, replica_groups=mesh['seq'=32,'exp'=16] {'exp'}, dimensions={0} | all-to-all | bytes 262144 | tf_op jit(solution)/shard_map/all_to_all | solution.py:536
  109.0 0.1 reshape.369
  109.2 39.3 %shard_map.129.tok_ref = bf16[4,8,64,1024]{3,2,1,0:T(8,128)(2,1)S(1)} custom-call(bf16[64,1024]{1,0:T(8,128)(2,1)S(1)} %bitcast.46), custom_call_target="tpu_custom_call" | custom-call | tf_op jit(solution)/shard_map/pallas_call | solution.py:419
  148.6 1.9 copy-done.1
  150.5 53.7 %shard_map.130 = bf16[64,1024]{1,0:T(8,128)(2,1)} custom-call(bf16[4,8,64,1024]{3,2,1,0:T(8,128)(2,1)} %copy-done.1, bf16[1024,128]{1,0:T(8,128)(2,1)} %bitcast.52, bf16[1024,128]{1,0:T(8,128)(2,1)} %bitcast.53, bf16[1024,128]{1,0:T(8,128)(2,1)} %bitcast.54), custom_call_target="tpu_custom_call" | custom-call | tf_op jit(solution)/shard_map/pallas_call | solution.py:226
  204.2 1.6 reduce.5
  205.9 23.9 %all_to_all.30 = bf16[16,2,2048]{2,1,0:T(2,128)(2,1)S(1)} all-to-all(bf16[16,2,2048]{2,1,0:T(2,128)(2,1)S(1)} %reshape.370), channel_id=1, replica_groups=mesh['seq'=32,'exp'=16] {'exp'}, dimensions={0} | all-to-all | bytes 262144 | tf_op jit(solution)/shard_map/all_to_all | solution.py:548
  229.7 0.1 reshape.371
  229.9 0.8 fusion.9
  (25 shorter events, 0.7 us)
Async XLA Ops:
  6.5 58.4 %copy-start = (s32[32,32]{1,0:T(8,128)S(1)}, s32[32,32]{1,0:T(8,128)}, u32[]{:S(2)}) copy-start(s32[32,32]{1,0:T(8,128)} %param.15) | copy-start | bytes 12292
  6.5 87.0 %all-gather.2.cloned.1.call-start = ((), (), s32[]{:S(2)}) async-start(), calls=%async_computation.3 | async-start | bytes 2228224 | tf_op jit(solution)/shard_map/all_gather | solution.py:513
  68.8 16.6 %copy-start.4 = (s32[32]{0:T(128)S(1)}, s32[32]{0:T(128)}, u32[]{:S(2)}) copy-start(s32[32]{0:T(128)} %param.14) | copy-start | bytes 388
  68.8 24.8 %copy-start.2 = (bf16[32,1024]{1,0:T(8,128)(2,1)S(1)}, bf16[32,1024]{1,0:T(8,128)(2,1)}, u32[]{:S(2)}) copy-start(bf16[32,1024]{1,0:T(8,128)(2,1)} %param.13) | copy-start | bytes 196612
  69.9 25.8 %copy-start.3 = (f32[1024]{0:T(1024)S(1)}, f32[1024]{0:T(1024)}, u32[]{:S(2)}) copy-start(f32[1024]{0:T(1024)} %param.22) | copy-start | bytes 12292
  72.2 21.0 %all-to-all-start = ((bf16[16,2,1024]{2,1,0:T(2,128)(2,1)}), bf16[16,2,1024]{2,1,0:T(2,128)(2,1)S(1)}, u32[]{:S(2)}, u32[]{:S(2)}) async-start(bf16[16,2,1024]{2,1,0:T(2,128)(2,1)} %reshape.366), calls=%async_computation | async-start | bytes 131072 | tf_op jit(solution)/shard_map/all_to_all | solution.py:510
  148.6 1.9 copy-start.1
Sparse Core Ops, SparseCore 0:
  9.5 49.1 all-gather.1

commit v12 on v11

--- a/solution.py
+++ b/solution.py
@@ -470,7 +470,7 @@
     normed_attn = rms_scale(inputs, gain_attn).astype(jnp.bfloat16)
     projector = jnp.concatenate([w_query, w_key, w_value], axis=1)
     joined_qkv = jnp.dot(
-        ring_gather(normed_attn, n_exp // CORES, CORES, "exp", "seq", 4).reshape(n_exp * row_count, width),
+        ring_gather(normed_attn, n_exp // CORES, CORES, "exp", "seq", 4, pieces=2).reshape(n_exp * row_count, width),
         projector,
         preferred_element_type=jnp.float32,
     ).astype(jnp.bfloat16)
@@ -543,7 +543,7 @@
     y_size = Y_RING if n_seq % Y_RING == 0 else n_seq
     summed = ring_ffn(
         gathered.reshape(gathered.shape[0], width),
-        w_gate[0], w_up[0], w_down[0], n_seq // y_size, y_size,
+        w_gate[0], w_up[0], w_down[0], n_seq // y_size, y_size, splits=4,
     ).reshape((-1,) + gathered.shape[1:])
     returned = lax.all_to_all(summed, "exp", split_axis=0, concat_axis=0, tiled=True)
     expert_out = jnp.dot(

time: 238 us -> 238 us (level)
    pallas_call x2, Pallas kernels: 73.2 us -> 69 us  [ring_gather(): pl.pallas_call(functools.partial(ring_gather_kernel, nx, ny, axis, other,...]
where the time goes in v12:
time: 238 us
  Pallas kernels  145 us (61%)
  blocking collectives  35.3 us (15%)
  between operations  14.4 us (6%)
  starting transfers between devices  13.8 us (6%)
  waiting for transfers between devices  8.21 us (3%)
  matrix products  7.43 us (3%)
  other arithmetic  7.35 us (3%)
  local copies, waits for them, and re-layouts  5.76 us (2%)
    pallas_call x2, Pallas kernels, ring_gather(): pl.pallas_call(functools.partial(ring_gather_kernel, nx, ny, axis, other,...  69 us
    pallas_call x1, Pallas kernels, ring_ffn(): pl.pallas_call(functools.partial(ring_ffn_kernel, nx, ny, splits), out_sh...  55.5 us
    all_to_all x1, blocking collectives, local(): lax.all_to_all(summed, 'exp', split_axis=0, concat_axis=0, tiled=True)  23.5 us
    pallas_call x1, Pallas kernels, shift_exchange(): pl.pallas_call(functools.partial(shift_exchange_kernel, tuple(offsets), a...  20.9 us
    all_to_all x1, starting transfers between devices, local(): lax.all_to_all(heads_out, 'exp', split_axis=0, concat_axis=1, tiled=True)  13.8 us
    all_to_all x1, blocking collectives, local(): lax.all_to_all(outgoing, 'exp', split_axis=0, concat_axis=0, tiled=True)  11.8 us
    all_to_all x1, waiting for transfers between devices, local(): lax.all_to_all(heads_out, 'exp', split_axis=0, concat_axis=1, tiled=True)  7.48 us
  transfers between devices with their start and end apart: 2, of which 1 were waited for; matrix products, arithmetic and copies ran while one was open for 5% of the time, Pallas kernels for 22%

profile of v12, /device:TPU:1, one launch (start us, length us, event | category | flops | bytes accessed | tf_op | source)
XLA Modules:
  0.0 237.6 jit_solution(16137744821697244747)
XLA Ops:
  6.5 0.7 all-gather.2.cloned.1.call-update
  7.3 1.0 fusion.24
  8.3 0.9 fusion.26.block_ref
  9.2 32.5 %shard_map.127 = bf16[8,2,32,1024]{3,2,1,0:T(8,128)(2,1)S(1)} custom-call(bf16[32,1024]{1,0:T(8,128)(2,1)S(1)} %fusion.26.block_ref), custom_call_target="tpu_custom_call" | custom-call | tf_op jit(solution)/shard_map/pallas_call | solution.py:419
  41.8 1.5 convolution_convert_fusion
  43.3 0.8 slice_bitcast_fusion
  44.0 20.9 %shard_map.128 = bf16[6,512,128]{2,1,0:T(8,128)(2,1)} custom-call(bf16[512,128]{1,0:T(8,128)(2,1)} %get-tuple-element.8.block_ref), custom_call_target="tpu_custom_call" | custom-call | tf_op jit(solution)/shard_map/pallas_call | solution.py:278
  65.8 0.7 gather_fusion
  66.6 1.7 pad_maximum_fusion
  68.3 1.3 fusion.40
  69.6 1.1 fusion
  70.8 1.4 fusion.16
  72.1 0.1 copy.24
  72.3 0.8 reshape.366
  73.0 13.8 %all-to-all-start = ((bf16[16,2,1024]{2,1,0:T(2,128)(2,1)}), bf16[16,2,1024]{2,1,0:T(2,128)(2,1)S(1)}, u32[]{:S(2)}, u32[]{:S(2)}) async-start(bf16[16,2,1024]{2,1,0:T(2,128)(2,1)} %reshape.366), calls=%async_computation | async-start | bytes 131072 | tf_op jit(solution)/shard_map/all_to_all | solution.py:510
  87.0 0.2 select_reduce_fusion
  87.2 7.5 %all-to-all-done = bf16[16,2,1024]{2,1,0:T(2,128)(2,1)S(1)} async-done(((bf16[16,2,1024]{2,1,0:T(2,128)(2,1)}), bf16[16,2,1024]{2,1,0:T(2,128)(2,1)S(1)}, u32[]{:S(2)}, u32[]{:S(2)}) %all-to-all-start) | async-done | bytes 65568 | tf_op jit(solution)/shard_map/all_to_all | solution.py:510
  94.7 0.1 reshape.367
  94.9 0.1 all_to_all.23
  95.0 2.2 multiply_reduce_fusion
  97.2 0.2 fusion.5
  97.5 0.5 broadcast.139
  98.0 0.7 reduce.4
  98.8 11.8 %all_to_all.29 = bf16[16,2,2048]{2,1,0:T(2,128)(2,1)S(1)} all-to-all(bf16[16,2,2048]{2,1,0:T(2,128)(2,1)S(1)} %reshape.368), channel_id=1, replica_groups=mesh['seq'=32,'exp'=16] {'exp'}, dimensions={0} | all-to-all | bytes 262144 | tf_op jit(solution)/shard_map/all_to_all | solution.py:536
  110.6 0.1 reshape.369
  110.7 36.5 %shard_map.129.tok_ref = bf16[4,8,64,1024]{3,2,1,0:T(8,128)(2,1)S(1)} custom-call(bf16[64,1024]{1,0:T(8,128)(2,1)S(1)} %bitcast.46), custom_call_target="tpu_custom_call" | custom-call | tf_op jit(solution)/shard_map/pallas_call | solution.py:419
  147.3 1.9 copy-done.1
  149.2 55.5 %shard_map.130 = bf16[64,1024]{1,0:T(8,128)(2,1)} custom-call(bf16[4,8,64,1024]{3,2,1,0:T(8,128)(2,1)} %copy-done.1, bf16[1024,128]{1,0:T(8,128)(2,1)} %bitcast.52, bf16[1024,128]{1,0:T(8,128)(2,1)} %bitcast.53, bf16[1024,128]{1,0:T(8,128)(2,1)} %bitcast.54), custom_call_target="tpu_custom_call" | custom-call | tf_op jit(solution)/shard_map/pallas_call | solution.py:226
  204.6 1.6 reduce.5
  206.3 23.5 %all_to_all.30 = bf16[16,2,2048]{2,1,0:T(2,128)(2,1)S(1)} all-to-all(bf16[16,2,2048]{2,1,0:T(2,128)(2,1)S(1)} %reshape.370), channel_id=1, replica_groups=mesh['seq'=32,'exp'=16] {'exp'}, dimensions={0} | all-to-all | bytes 262144 | tf_op jit(solution)/shard_map/all_to_all | solution.py:548
  229.8 0.1 reshape.371
  230.0 0.8 fusion.9
  (25 shorter events, 0.7 us)
Async XLA Ops:
  6.5 59.2 %copy-start = (s32[32,32]{1,0:T(8,128)S(1)}, s32[32,32]{1,0:T(8,128)}, u32[]{:S(2)}) copy-start(s32[32,32]{1,0:T(8,128)} %param.15) | copy-start | bytes 12292
  6.5 88.5 %all-gather.2.cloned.1.call-start = ((), (), s32[]{:S(2)}) async-start(), calls=%async_computation.3 | async-start | bytes 2228224 | tf_op jit(solution)/shard_map/all_gather | solution.py:513
  69.6 17.2 %copy-start.4 = (s32[32]{0:T(128)S(1)}, s32[32]{0:T(128)}, u32[]{:S(2)}) copy-start(s32[32]{0:T(128)} %param.14) | copy-start | bytes 388
  69.6 25.4 %copy-start.2 = (bf16[32,1024]{1,0:T(8,128)(2,1)S(1)}, bf16[32,1024]{1,0:T(8,128)(2,1)}, u32[]{:S(2)}) copy-start(bf16[32,1024]{1,0:T(8,128)(2,1)} %param.13) | copy-start | bytes 196612
  70.8 26.5 %copy-start.3 = (f32[1024]{0:T(1024)S(1)}, f32[1024]{0:T(1024)}, u32[]{:S(2)}) copy-start(f32[1024]{0:T(1024)} %param.22) | copy-start | bytes 12292
  73.0 21.6 %all-to-all-start = ((bf16[16,2,1024]{2,1,0:T(2,128)(2,1)}), bf16[16,2,1024]{2,1,0:T(2,128)(2,1)S(1)}, u32[]{:S(2)}, u32[]{:S(2)}) async-start(bf16[16,2,1024]{2,1,0:T(2,128)(2,1)} %reshape.366), calls=%async_computation | async-start | bytes 131072 | tf_op jit(solution)/shard_map/all_to_all | solution.py:510
  147.2 1.9 copy-start.1
Sparse Core Ops, SparseCore 0:
  9.5 49.5 all-gather.1

commit v13 on v12

--- a/solution.py
+++ b/solution.py
@@ -126,8 +126,8 @@
     )(part)
 
 
-def ring_ffn_kernel(nx, ny, splits, tok_ref, wg_ref, wu_ref, wd_ref, out_ref, pbuf, recv1, send1,
-                    acc, recv2, send2, s1_send, s1_recv, s2_send, s2_recv):
+def ring_ffn_kernel(nx, ny, splits, tok_ref, wg_ref, wu_ref, wd_ref, out_ref, ret_ref, pbuf, recv1, send1,
+                    acc, recv2, send2, s1_send, s1_recv, s2_send, s2_recv, r_send, r_recv):
     me = lax.axis_index("seq")
     col = lax.axis_index("exp")
     x = me // ny
@@ -153,11 +153,16 @@
                                preferred_element_type=jnp.float32)
         pbuf[...] = down.astype(jnp.bfloat16).reshape(nx, rows, width)
 
+    n_exp = lax.axis_size("exp")
+    group = rows // n_exp
     barrier = pltpu.get_barrier_semaphore()
     for peer in (y_up, y_down, x_up, x_down):
         pl.semaphore_signal(barrier, inc=1, device_id=(peer, col),
                             device_id_type=pl.DeviceIdType.MESH)
-    pl.semaphore_wait(barrier, 4)
+    for k in range(1, n_exp):
+        pl.semaphore_signal(barrier, inc=1, device_id=(me, (col + k) % n_exp),
+                            device_id_type=pl.DeviceIdType.MESH)
+    pl.semaphore_wait(barrier, 4 + n_exp - 1)
 
     lanes = []
     for a in range(nx):
@@ -212,12 +217,26 @@
     for d, (peer, sign, r0) in enumerate(lanes2):
         copies2[nx - 2][d].wait_recv()
         out_ref[r0:r0 + quarter] = (recv2[d, nx - 2] + acc[x, r0:r0 + quarter]).astype(out_ref.dtype)
+    back = []
+    for k in range(1, n_exp):
+        peer = (col + k) % n_exp
+        cp = pltpu.make_async_remote_copy(
+            src_ref=out_ref.at[pl.ds(peer * group, group)], dst_ref=ret_ref.at[col],
+            send_sem=r_send.at[k - 1], recv_sem=r_recv.at[k - 1],
+            device_id=(me, peer), device_id_type=pl.DeviceIdType.MESH)
+        cp.start()
+        back.append(cp)
+    own = pltpu.make_async_copy(out_ref.at[pl.ds(col * group, group)], ret_ref.at[col], r_send.at[n_exp - 1])
+    own.start()
+    own.wait()
     for step_copies in copies1 + copies2:
         for cp in step_copies:
             cp.wait_send()
-
-
-def ring_ffn(tokens, w_gate, w_up, w_down, nx, ny, splits=2):
+    for cp in back:
+        cp.wait()
+
+
+def ring_ffn(tokens, w_gate, w_up, w_down, nx, ny, n_exp, splits=2):
     width = tokens.shape[-1]
     rows = tokens.shape[0] // (nx * ny)
     tokens = tokens.reshape(nx, ny, rows, width)
@@ -225,9 +244,10 @@
     vmem = pltpu.MemorySpace.VMEM
     return pl.pallas_call(
         functools.partial(ring_ffn_kernel, nx, ny, splits),
-        out_shape=jax.ShapeDtypeStruct((rows, width), jnp.bfloat16),
+        out_shape=(jax.ShapeDtypeStruct((rows, width), jnp.bfloat16),
+                   jax.ShapeDtypeStruct((n_exp, rows // n_exp, width), jnp.bfloat16)),
         in_specs=[pl.BlockSpec(memory_space=vmem)] * 4,
-        out_specs=pl.BlockSpec(memory_space=vmem),
+        out_specs=(pl.BlockSpec(memory_space=vmem), pl.BlockSpec(memory_space=vmem)),
         scratch_shapes=[
             pltpu.VMEM((nx, rows, width), jnp.bfloat16),
             pltpu.VMEM((n1, ny - 1, rows // splits, width), jnp.bfloat16),
@@ -239,6 +259,8 @@
             pltpu.SemaphoreType.DMA((n1, ny - 1)),
             pltpu.SemaphoreType.DMA((4, nx - 1)),
             pltpu.SemaphoreType.DMA((4, nx - 1)),
+            pltpu.SemaphoreType.DMA((n_exp,)),
+            pltpu.SemaphoreType.DMA((n_exp - 1,)),
         ],
         compiler_params=pltpu.CompilerParams(
             collective_id=5, has_side_effects=True, vmem_limit_bytes=56 * 1024 * 1024
@@ -541,11 +563,10 @@
     ).reshape((n_seq * arrived.shape[0],) + arrived.shape[1:])
     n_seq = lax.axis_size("seq")
     y_size = Y_RING if n_seq % Y_RING == 0 else n_seq
-    summed = ring_ffn(
+    returned = ring_ffn(
         gathered.reshape(gathered.shape[0], width),
-        w_gate[0], w_up[0], w_down[0], n_seq // y_size, y_size, splits=4,
-    ).reshape((-1,) + gathered.shape[1:])
-    returned = lax.all_to_all(summed, "exp", split_axis=0, concat_axis=0, tiled=True)
+        w_gate[0], w_up[0], w_down[0], n_seq // y_size, y_size, n_exp,
+    )[1].reshape((-1,) + gathered.shape[1:])
     expert_out = jnp.dot(
         jnp.transpose(selector),
         returned.reshape(n_slots, width),

time: 238 us -> 238 us (level)
  Pallas kernels: 145 us -> 169 us
  blocking collectives: 35.3 us -> 11.8 us
    pallas_call x1, Pallas kernels: 55.5 us -> 79.3 us  [ring_ffn(): pl.pallas_call(functools.partial(ring_ffn_kernel, nx, ny, splits), out_sh...]
    all_to_all x1 -> x0, blocking collectives: 23.5 us -> none  [local(): lax.all_to_all(summed, 'exp', split_axis=0, concat_axis=0, tiled=True)]
  transfers between devices with their start and end apart: 2 -> 2, of which waited for: 1 -> 1; matrix products, arithmetic and copies ran while one was open for 5% -> 5% of each run, Pallas kernels for 22% -> 23%
where the time goes in v13:
time: 238 us; the launch traced here: 237 us
  Pallas kernels  169 us (71%)
  between operations  14.4 us (6%)
  starting transfers between devices  13.8 us (6%)
  blocking collectives  11.8 us (5%)
  waiting for transfers between devices  8.21 us (3%)
  matrix products  7.43 us (3%)
  local copies, waits for them, and re-layouts  6.49 us (3%)
  other arithmetic  5.76 us (2%)
    pallas_call x1, Pallas kernels, ring_ffn(): pl.pallas_call(functools.partial(ring_ffn_kernel, nx, ny, splits), out_sh...  79.3 us
    pallas_call x2, Pallas kernels, ring_gather(): pl.pallas_call(functools.partial(ring_gather_kernel, nx, ny, axis, other,...  69 us
    pallas_call x1, Pallas kernels, shift_exchange(): pl.pallas_call(functools.partial(shift_exchange_kernel, tuple(offsets), a...  20.9 us
    all_to_all x1, starting transfers between devices, local(): lax.all_to_all(heads_out, 'exp', split_axis=0, concat_axis=1, tiled=True)  13.8 us
    all_to_all x1, blocking collectives, local(): lax.all_to_all(outgoing, 'exp', split_axis=0, concat_axis=0, tiled=True)  11.8 us
    all_to_all x1, waiting for transfers between devices, local(): lax.all_to_all(heads_out, 'exp', split_axis=0, concat_axis=1, tiled=True)  7.48 us
  transfers between devices with their start and end apart: 2, of which 1 were waited for; matrix products, arithmetic and copies ran while one was open for 5% of the time, Pallas kernels for 23%

profile of v13, /device:TPU:1, one launch (start us, length us, event | category | flops | bytes accessed | tf_op | source)
XLA Modules:
  0.0 237.1 jit_solution(827762863994482590)
XLA Ops:
  6.5 0.7 all-gather.2.cloned.1.call-update
  7.3 1.0 fusion.24
  8.3 0.9 fusion.26.block_ref
  9.2 32.5 %shard_map.127 = bf16[8,2,32,1024]{3,2,1,0:T(8,128)(2,1)S(1)} custom-call(bf16[32,1024]{1,0:T(8,128)(2,1)S(1)} %fusion.26.block_ref), custom_call_target="tpu_custom_call" | custom-call | tf_op jit(solution)/shard_map/pallas_call | solution.py:441
  41.8 1.5 convolution_convert_fusion
  43.3 0.8 slice_bitcast_fusion
  44.0 20.9 %shard_map.128 = bf16[6,512,128]{2,1,0:T(8,128)(2,1)} custom-call(bf16[512,128]{1,0:T(8,128)(2,1)} %get-tuple-element.10.block_ref), custom_call_target="tpu_custom_call" | custom-call | tf_op jit(solution)/shard_map/pallas_call | solution.py:300
  65.7 0.1 stack.31
  65.8 0.7 gather_fusion
  66.6 1.7 pad_maximum_fusion
  68.3 1.3 fusion.38
  69.6 1.1 fusion
  70.8 1.4 fusion.16
  72.1 0.1 copy.23
  72.3 0.8 reshape.358
  73.0 13.8 %all-to-all-start = ((bf16[16,2,1024]{2,1,0:T(2,128)(2,1)}), bf16[16,2,1024]{2,1,0:T(2,128)(2,1)S(1)}, u32[]{:S(2)}, u32[]{:S(2)}) async-start(bf16[16,2,1024]{2,1,0:T(2,128)(2,1)} %reshape.358), calls=%async_computation | async-start | bytes 131072 | tf_op jit(solution)/shard_map/all_to_all | solution.py:532
  87.0 0.2 select_reduce_fusion
  87.2 7.5 %all-to-all-done = bf16[16,2,1024]{2,1,0:T(2,128)(2,1)S(1)} async-done(((bf16[16,2,1024]{2,1,0:T(2,128)(2,1)}), bf16[16,2,1024]{2,1,0:T(2,128)(2,1)S(1)}, u32[]{:S(2)}, u32[]{:S(2)}) %all-to-all-start) | async-done | bytes 65568 | tf_op jit(solution)/shard_map/all_to_all | solution.py:532
  94.7 0.1 reshape.359
  94.9 0.1 all_to_all.20
  95.0 2.2 multiply_reduce_fusion
  97.2 0.2 fusion.5
  97.5 0.5 broadcast.139
  98.0 0.7 reduce.4
  98.7 0.1 reshape.360
  98.8 11.8 %all_to_all.24 = bf16[16,2,2048]{2,1,0:T(2,128)(2,1)S(1)} all-to-all(bf16[16,2,2048]{2,1,0:T(2,128)(2,1)S(1)} %reshape.360), channel_id=1, replica_groups=mesh['seq'=32,'exp'=16] {'exp'}, dimensions={0} | all-to-all | bytes 262144 | tf_op jit(solution)/shard_map/all_to_all | solution.py:558
  110.6 0.1 reshape.361
  110.7 36.5 %shard_map.129.tok_ref = bf16[4,8,64,1024]{3,2,1,0:T(8,128)(2,1)S(1)} custom-call(bf16[64,1024]{1,0:T(8,128)(2,1)S(1)} %bitcast.43), custom_call_target="tpu_custom_call" | custom-call | tf_op jit(solution)/shard_map/pallas_call | solution.py:441
  147.3 1.9 copy-done.1
  149.2 79.3 %shard_map.130 = (bf16[64,1024]{1,0:T(8,128)(2,1)}, bf16[16,4,1024]{2,1,0:T(4,128)(2,1)}) custom-call(bf16[4,8,64,1024]{3,2,1,0:T(8,128)(2,1)} %copy-done.1, bf16[1024,128]{1,0:T(8,128)(2,1)} %bitcast.48, bf16[1024,128]{1,0:T(8,128)(2,1)} %bitcast.49, bf16[1024,128]{1,0:T(8,128)(2,1)} %bitcast.50), custom_call_target="tpu_custom_call" | custom-call | tf_op jit(solution)/shard_map/pallas_call | solution.py:245
  228.5 0.9 reshape_reshape.3
  229.5 0.8 fusion.9
  (22 shorter events, 0.4 us)
Async XLA Ops:
  6.5 59.2 %copy-start = (s32[32,32]{1,0:T(8,128)S(1)}, s32[32,32]{1,0:T(8,128)}, u32[]{:S(2)}) copy-start(s32[32,32]{1,0:T(8,128)} %param.15) | copy-start | bytes 12292
  6.5 88.5 %all-gather.2.cloned.1.call-start = ((), (), s32[]{:S(2)}) async-start(), calls=%async_computation.2 | async-start | bytes 2228224 | tf_op jit(solution)/shard_map/all_gather | solution.py:535
  69.6 17.2 %copy-start.4 = (s32[32]{0:T(128)S(1)}, s32[32]{0:T(128)}, u32[]{:S(2)}) copy-start(s32[32]{0:T(128)} %param.14) | copy-start | bytes 388
  69.6 25.4 %copy-start.2 = (bf16[32,1024]{1,0:T(8,128)(2,1)S(1)}, bf16[32,1024]{1,0:T(8,128)(2,1)}, u32[]{:S(2)}) copy-start(bf16[32,1024]{1,0:T(8,128)(2,1)} %param.13) | copy-start | bytes 196612
  70.8 26.5 %copy-start.3 = (f32[1024]{0:T(1024)S(1)}, f32[1024]{0:T(1024)}, u32[]{:S(2)}) copy-start(f32[1024]{0:T(1024)} %param.22) | copy-start | bytes 12292
  73.0 21.6 %all-to-all-start = ((bf16[16,2,1024]{2,1,0:T(2,128)(2,1)}), bf16[16,2,1024]{2,1,0:T(2,128)(2,1)S(1)}, u32[]{:S(2)}, u32[]{:S(2)}) async-start(bf16[16,2,1024]{2,1,0:T(2,128)(2,1)} %reshape.358), calls=%async_computation | async-start | bytes 131072 | tf_op jit(solution)/shard_map/all_to_all | solution.py:532
  147.2 1.9 copy-start.1
Sparse Core Ops, SparseCore 0:
  9.5 49.5 all-gather.1

commit v14 on v13

--- a/solution.py
+++ b/solution.py
@@ -343,7 +343,8 @@
     )(x)
 
 
-def ring_gather_kernel(nx, ny, axis, other, pieces, block_ref, out_ref, local_sem, send_sems, recv_sems):
+def ring_gather_kernel(nx, ny, axis, other, pieces, route, block_ref, out_ref, local_sem, send_sems, recv_sems,
+                       r_send, r_recv):
     me = lax.axis_index(axis)
     col = lax.axis_index(other)
     x = me // ny
@@ -356,13 +357,38 @@
         return (idx, col) if axis == "seq" else (col, idx)
 
     peers = [dev(x, y + 1), dev(x, y - 1), dev(x + 1, y), dev(x - 1, y)]
+    n_other = lax.axis_size(other)
     barrier = pltpu.get_barrier_semaphore()
     for peer in peers:
         pl.semaphore_signal(barrier, inc=1, device_id=peer, device_id_type=pl.DeviceIdType.MESH)
-    pl.semaphore_wait(barrier, 4)
-
-    own = pltpu.make_async_copy(block_ref, out_ref.at[x, y], local_sem.at[0])
-    own.start()
+    if route:
+        for k in range(1, n_other):
+            pl.semaphore_signal(barrier, inc=1, device_id=(me, (col + k) % n_other),
+                                device_id_type=pl.DeviceIdType.MESH)
+    pl.semaphore_wait(barrier, 4 + (n_other - 1 if route else 0))
+
+    if route:
+        group = rows // n_other
+        routed = []
+        for k in range(1, n_other):
+            peer = (col + k) % n_other
+            cp = pltpu.make_async_remote_copy(
+                src_ref=block_ref.at[pl.ds(peer * group, group)],
+                dst_ref=out_ref.at[x, y, pl.ds(col * group, group)],
+                send_sem=r_send.at[k - 1], recv_sem=r_recv.at[k - 1],
+                device_id=(me, peer), device_id_type=pl.DeviceIdType.MESH)
+            cp.start()
+            routed.append(cp)
+        own = pltpu.make_async_copy(block_ref.at[pl.ds(col * group, group)],
+                                    out_ref.at[x, y, pl.ds(col * group, group)], local_sem.at[0])
+        own.start()
+        own.wait()
+        for cp in routed:
+            cp.wait()
+        block_ref = out_ref.at[x, y]
+    else:
+        own = pltpu.make_async_copy(block_ref, out_ref.at[x, y], local_sem.at[0])
+        own.start()
     sem_count = [0]
 
     def unit(axis, stage, u, lo, hi):
@@ -426,7 +452,8 @@
     for s1, _ in plans:
         for lane in s1:
             lane[-1][1].wait_recv()
-    own.wait()
+    if not route:
+        own.wait()
     run([lane for _, s2 in plans for lane in s2])
     for _, s2 in plans:
         for lane in s2:
@@ -435,11 +462,11 @@
         cp.wait_send()
 
 
-def ring_gather(block, nx, ny, axis="seq", other="exp", cid=3, pieces=1):
+def ring_gather(block, nx, ny, axis="seq", other="exp", cid=3, pieces=1, route=False, n_other=2):
     vmem = pltpu.MemorySpace.VMEM
     n_sems = 4 * pieces * (nx // 2 + ny // 2) + 4
     return pl.pallas_call(
-        functools.partial(ring_gather_kernel, nx, ny, axis, other, pieces),
+        functools.partial(ring_gather_kernel, nx, ny, axis, other, pieces, route),
         out_shape=jax.ShapeDtypeStruct((nx, ny) + block.shape, block.dtype),
         in_specs=[pl.BlockSpec(memory_space=vmem)],
         out_specs=pl.BlockSpec(memory_space=vmem),
@@ -447,6 +474,8 @@
             pltpu.SemaphoreType.DMA((1,)),
             pltpu.SemaphoreType.DMA((n_sems,)),
             pltpu.SemaphoreType.DMA((n_sems,)),
+            pltpu.SemaphoreType.DMA((n_other,)),
+            pltpu.SemaphoreType.DMA((n_other,)),
         ],
         compiler_params=pltpu.CompilerParams(
             collective_id=cid, has_side_effects=True, vmem_limit_bytes=48 * 1024 * 1024
@@ -555,12 +584,11 @@
         jnp.bfloat16
     )
     outgoing = outgoing.reshape(n_exp * capacity, experts_dev, width)
-    arrived = lax.all_to_all(outgoing, "exp", split_axis=0, concat_axis=0, tiled=True)
     n_seq = lax.axis_size("seq")
     y_size = Y_RING if n_seq % Y_RING == 0 else n_seq
     gathered = ring_gather(
-        arrived.reshape(arrived.shape[0], width), n_seq // y_size, y_size, pieces=2
-    ).reshape((n_seq * arrived.shape[0],) + arrived.shape[1:])
+        outgoing.reshape(-1, width), n_seq // y_size, y_size, pieces=2, route=True, n_other=n_exp
+    ).reshape((n_seq * outgoing.shape[0],) + outgoing.shape[1:])
     n_seq = lax.axis_size("seq")
     y_size = Y_RING if n_seq % Y_RING == 0 else n_seq
     returned = ring_ffn(

time: 238 us -> 230 us (0.966)
  blocking collectives: 11.8 us -> 0 us
  Pallas kernels: 169 us -> 175 us
    all_to_all x1 -> x0, blocking collectives: 11.8 us -> none  [local(): lax.all_to_all(outgoing, 'exp', split_axis=0, concat_axis=0, tiled=True)]
    pallas_call x2, Pallas kernels: 69 us -> 76.8 us  [ring_gather(): pl.pallas_call(functools.partial(ring_gather_kernel, nx, ny, axis, other,...]
where the time goes in v14:
time: 230 us
  Pallas kernels  175 us (76%)
  between operations  14.3 us (6%)
  starting transfers between devices  13.8 us (6%)
  waiting for transfers between devices  8.21 us (4%)
  matrix products  7.43 us (3%)
  local copies, waits for them, and re-layouts  5.73 us (2%)
  other arithmetic  5.09 us (2%)
    pallas_call x1, Pallas kernels, ring_ffn(): pl.pallas_call(functools.partial(ring_ffn_kernel, nx, ny, splits), out_sh...  77.4 us
    pallas_call x2, Pallas kernels, ring_gather(): pl.pallas_call(functools.partial(ring_gather_kernel, nx, ny, axis, other,...  76.8 us
    pallas_call x1, Pallas kernels, shift_exchange(): pl.pallas_call(functools.partial(shift_exchange_kernel, tuple(offsets), a...  21 us
    all_to_all x1, starting transfers between devices, local(): lax.all_to_all(heads_out, 'exp', split_axis=0, concat_axis=1, tiled=True)  13.8 us
    all_to_all x1, waiting for transfers between devices, local(): lax.all_to_all(heads_out, 'exp', split_axis=0, concat_axis=1, tiled=True)  7.48 us
  transfers between devices with their start and end apart: 2, of which 1 were waited for; matrix products, arithmetic and copies ran while one was open for 5% of the time, Pallas kernels for 23%

profile of v14, /device:TPU:1, one launch (start us, length us, event | category | flops | bytes accessed | tf_op | source)
XLA Modules:
  0.0 229.8 jit_solution(14094254808007708302)
XLA Ops:
  6.5 0.7 all-gather.2.cloned.1.call-update
  7.3 1.0 fusion.23
  8.3 0.9 fusion.25.block_ref
  9.2 32.6 %shard_map.127 = bf16[8,2,32,1024]{3,2,1,0:T(8,128)(2,1)S(1)} custom-call(bf16[32,1024]{1,0:T(8,128)(2,1)S(1)} %fusion.25.block_ref), custom_call_target="tpu_custom_call" | custom-call | tf_op jit(solution)/shard_map/pallas_call | solution.py:468
  41.8 1.5 convolution_convert_fusion
  43.3 0.8 slice_bitcast_fusion
  44.0 21.0 %shard_map.128 = bf16[6,512,128]{2,1,0:T(8,128)(2,1)} custom-call(bf16[512,128]{1,0:T(8,128)(2,1)} %get-tuple-element.10.block_ref), custom_call_target="tpu_custom_call" | custom-call | tf_op jit(solution)/shard_map/pallas_call | solution.py:300
  65.7 0.1 stack.31
  65.8 0.7 gather_fusion
  66.5 0.1 broadcast_in_dim.19
  66.6 1.7 pad_maximum_fusion
  68.3 1.3 fusion.37
  69.7 1.1 fusion
  70.8 1.4 fusion.15
  72.2 0.1 copy.16
  72.3 0.8 reshape.350
  73.1 13.8 %all-to-all-start = ((bf16[16,2,1024]{2,1,0:T(2,128)(2,1)}), bf16[16,2,1024]{2,1,0:T(2,128)(2,1)S(1)}, u32[]{:S(2)}, u32[]{:S(2)}) async-start(bf16[16,2,1024]{2,1,0:T(2,128)(2,1)} %reshape.350), calls=%async_computation | async-start | bytes 131072 | tf_op jit(solution)/shard_map/all_to_all | solution.py:561
  86.9 0.1 fusion.31
  87.0 0.1 reduce_window_sum.11
  87.0 0.2 select_reduce_fusion
  87.2 7.5 %all-to-all-done = bf16[16,2,1024]{2,1,0:T(2,128)(2,1)S(1)} async-done(((bf16[16,2,1024]{2,1,0:T(2,128)(2,1)}), bf16[16,2,1024]{2,1,0:T(2,128)(2,1)S(1)}, u32[]{:S(2)}, u32[]{:S(2)}) %all-to-all-start) | async-done | bytes 65568 | tf_op jit(solution)/shard_map/all_to_all | solution.py:561
  94.7 0.1 reshape.351
  94.8 0.1 copy.17
  94.9 0.1 all_to_all.17
  95.0 0.0 all-gather.2.cloned.1.call-done
  95.1 2.2 multiply_reduce_fusion
  97.3 0.2 convolution_convert_fusion.1.block_ref
  97.5 44.3 %shard_map.129.tok_ref = bf16[4,8,64,1024]{3,2,1,0:T(8,128)(2,1)S(1)} custom-call(bf16[64,1024]{1,0:T(8,128)(2,1)S(1)} %convolution_convert_fusion.1.block_ref), custom_call_target="tpu_custom_call" | custom-call | tf_op jit(solution)/shard_map/pallas_call | solution.py:468
  141.8 1.9 copy-done.1
  143.7 77.4 %shard_map.130 = (bf16[64,1024]{1,0:T(8,128)(2,1)}, bf16[16,4,1024]{2,1,0:T(4,128)(2,1)}) custom-call(bf16[4,8,64,1024]{3,2,1,0:T(8,128)(2,1)} %copy-done.1, bf16[1024,128]{1,0:T(8,128)(2,1)} %bitcast.42, bf16[1024,128]{1,0:T(8,128)(2,1)} %bitcast.43, bf16[1024,128]{1,0:T(8,128)(2,1)} %bitcast.44), custom_call_target="tpu_custom_call" | custom-call | tf_op jit(solution)/shard_map/pallas_call | solution.py:245
  221.1 0.9 reshape_reshape.3
  222.1 0.8 fusion.8
  (16 shorter events, 0.1 us)
Async XLA Ops:
  6.5 59.3 %copy-start = (s32[32,32]{1,0:T(8,128)S(1)}, s32[32,32]{1,0:T(8,128)}, u32[]{:S(2)}) copy-start(s32[32,32]{1,0:T(8,128)} %param.15) | copy-start | bytes 12292
  6.5 88.5 %all-gather.2.cloned.1.call-start = ((), (), s32[]{:S(2)}) async-start(), calls=%async_computation.1 | async-start | bytes 2228224 | tf_op jit(solution)/shard_map/all_gather | solution.py:564
  69.7 17.2 %copy-start.4 = (s32[32]{0:T(128)S(1)}, s32[32]{0:T(128)}, u32[]{:S(2)}) copy-start(s32[32]{0:T(128)} %param.14) | copy-start | bytes 388
  69.7 25.4 %copy-start.2 = (bf16[32,1024]{1,0:T(8,128)(2,1)S(1)}, bf16[32,1024]{1,0:T(8,128)(2,1)}, u32[]{:S(2)}) copy-start(bf16[32,1024]{1,0:T(8,128)(2,1)} %param.13) | copy-start | bytes 196612
  70.8 26.5 %copy-start.3 = (f32[1024]{0:T(1024)S(1)}, f32[1024]{0:T(1024)}, u32[]{:S(2)}) copy-start(f32[1024]{0:T(1024)} %param.22) | copy-start | bytes 12292
  73.1 21.6 %all-to-all-start = ((bf16[16,2,1024]{2,1,0:T(2,128)(2,1)}), bf16[16,2,1024]{2,1,0:T(2,128)(2,1)S(1)}, u32[]{:S(2)}, u32[]{:S(2)}) async-start(bf16[16,2,1024]{2,1,0:T(2,128)(2,1)} %reshape.350), calls=%async_computation | async-start | bytes 131072 | tf_op jit(solution)/shard_map/all_to_all | solution.py:561
  141.8 1.9 copy-start.1
Sparse Core Ops, SparseCore 0:
  9.5 49.5 all-gather.1

commit v15 on v14

--- a/solution.py
+++ b/solution.py
@@ -356,7 +356,11 @@
         idx = (a + nx) % nx * ny + (b + ny) % ny
         return (idx, col) if axis == "seq" else (col, idx)
 
-    peers = [dev(x, y + 1), dev(x, y - 1), dev(x + 1, y), dev(x - 1, y)]
+    peers = []
+    for d in range(1, min(2, ny // 2) + 1):
+        peers += [dev(x, y + d), dev(x, y - d)]
+    for d in range(1, min(2, nx // 2) + 1):
+        peers += [dev(x + d, y), dev(x - d, y)]
     n_other = lax.axis_size(other)
     barrier = pltpu.get_barrier_semaphore()
     for peer in peers:
@@ -365,7 +369,7 @@
         for k in range(1, n_other):
             pl.semaphore_signal(barrier, inc=1, device_id=(me, (col + k) % n_other),
                                 device_id_type=pl.DeviceIdType.MESH)
-    pl.semaphore_wait(barrier, 4 + (n_other - 1 if route else 0))
+    pl.semaphore_wait(barrier, len(peers) + (n_other - 1 if route else 0))
 
     if route:
         group = rows // n_other
@@ -403,27 +407,36 @@
         mid = (lo + hi) // 2
         steps = []
         for sign in (1, -1):
-            prev = None
-            lane = []
-            for k in range(half):
-                u = (c - sign * k + 2 * n) % n
-                a_lo, a_hi = lo, hi
-                if k == half - 1 and n % 2 == 0:
-                    a_lo, a_hi = (lo, mid) if sign == 1 else (mid, hi)
-                if stage == 1 and k == 0:
-                    src = block_ref.at[a_lo:a_hi]
-                else:
-                    src = unit(axis, stage, u, a_lo, a_hi)
-                dst = unit(axis, stage, u, a_lo, a_hi)
-                target = dev(x, y + sign) if axis == "y" else dev(x + sign, y)
+            def rows_for(d):
+                if d == half and n % 2 == 0:
+                    return (lo, mid) if sign == 1 else (mid, hi)
+                return (lo, hi)
+
+            def target(d):
+                return dev(x, y + sign * d) if axis == "y" else dev(x + sign * d, y)
+
+            direct = {}
+            for d in range(1, min(2, half) + 1):
+                a_lo, a_hi = rows_for(d)
+                src = block_ref.at[a_lo:a_hi] if stage == 1 else unit(axis, stage, c, a_lo, a_hi)
                 j = sem_count[0]
                 sem_count[0] += 1
                 cp = pltpu.make_async_remote_copy(
-                    src_ref=src, dst_ref=dst, send_sem=send_sems.at[j], recv_sem=recv_sems.at[j],
-                    device_id=target, device_id_type=pl.DeviceIdType.MESH)
-                lane.append((prev, cp))
-                prev = cp
-            steps.append(lane)
+                    src_ref=src, dst_ref=unit(axis, stage, c, a_lo, a_hi),
+                    send_sem=send_sems.at[j], recv_sem=recv_sems.at[j],
+                    device_id=target(d), device_id_type=pl.DeviceIdType.MESH)
+                direct[d] = cp
+                steps.append([(None, cp)])
+            for d in range(3, half + 1):
+                a_lo, a_hi = rows_for(d)
+                u = (c - sign * (d - 2) + 2 * n) % n
+                j = sem_count[0]
+                sem_count[0] += 1
+                cp = pltpu.make_async_remote_copy(
+                    src_ref=unit(axis, stage, u, a_lo, a_hi), dst_ref=unit(axis, stage, u, a_lo, a_hi),
+                    send_sem=send_sems.at[j], recv_sem=recv_sems.at[j],
+                    device_id=target(2), device_id_type=pl.DeviceIdType.MESH)
+                steps[len(steps) - min(2, half) + (d - 3)].append((direct[d - 2], cp))
         return steps
 
     plans = []

time: 230 us -> 236 us (1.026)
  Pallas kernels: 175 us -> 179 us
    pallas_call x1, Pallas kernels: 77.4 us -> 82.6 us  [ring_ffn(): pl.pallas_call(functools.partial(ring_ffn_kernel, nx, ny, splits), out_sh...]
  transfers between devices with their start and end apart: 2 -> 2, of which waited for: 1 -> 1; matrix products, arithmetic and copies ran while one was open for 5% -> 5% of each run, Pallas kernels for 23% -> 20%
where the time goes in v15:
time: 236 us; the launch traced here: 234 us
  Pallas kernels  179 us (76%)
  starting transfers between devices  14.7 us (6%)
  between operations  14.3 us (6%)
  waiting for transfers between devices  8.21 us (3%)
  matrix products  7.43 us (3%)
  local copies, waits for them, and re-layouts  5.72 us (2%)
  other arithmetic  5.09 us (2%)
    pallas_call x1, Pallas kernels, ring_ffn(): pl.pallas_call(functools.partial(ring_ffn_kernel, nx, ny, splits), out_sh...  82.6 us
    pallas_call x2, Pallas kernels, ring_gather(): pl.pallas_call(functools.partial(ring_gather_kernel, nx, ny, axis, other,...  76.4 us
    pallas_call x1, Pallas kernels, shift_exchange(): pl.pallas_call(functools.partial(shift_exchange_kernel, tuple(offsets), a...  19.9 us
    all_to_all x1, starting transfers between devices, local(): lax.all_to_all(heads_out, 'exp', split_axis=0, concat_axis=1, tiled=True)  14.7 us
    all_to_all x1, waiting for transfers between devices, local(): lax.all_to_all(heads_out, 'exp', split_axis=0, concat_axis=1, tiled=True)  7.48 us
  transfers between devices with their start and end apart: 2, of which 1 were waited for; matrix products, arithmetic and copies ran while one was open for 5% of the time, Pallas kernels for 20%

profile of v15, /device:TPU:1, one launch (start us, length us, event | category | flops | bytes accessed | tf_op | source)
XLA Modules:
  0.0 234.3 jit_solution(3968588369355237679)
XLA Ops:
  6.5 0.7 all-gather.2.cloned.1.call-update
  7.3 1.0 fusion.23
  8.3 0.9 fusion.25.block_ref
  9.2 27.3 %shard_map.127 = bf16[8,2,32,1024]{3,2,1,0:T(8,128)(2,1)S(1)} custom-call(bf16[32,1024]{1,0:T(8,128)(2,1)S(1)} %fusion.25.block_ref), custom_call_target="tpu_custom_call" | custom-call | tf_op jit(solution)/shard_map/pallas_call | solution.py:481
  36.5 1.5 convolution_convert_fusion
  38.0 0.8 slice_bitcast_fusion
  38.8 19.9 %shard_map.128 = bf16[6,512,128]{2,1,0:T(8,128)(2,1)} custom-call(bf16[512,128]{1,0:T(8,128)(2,1)} %get-tuple-element.10.block_ref), custom_call_target="tpu_custom_call" | custom-call | tf_op jit(solution)/shard_map/pallas_call | solution.py:300
  59.4 0.1 stack.31
  59.5 0.7 gather_fusion
  60.2 0.1 broadcast_in_dim.19
  60.3 1.7 pad_maximum_fusion
  62.0 1.3 fusion.37
  63.3 1.1 fusion
  64.5 1.4 fusion.15
  65.9 0.1 copy.16
  66.0 0.8 reshape.350
  66.8 14.7 %all-to-all-start = ((bf16[16,2,1024]{2,1,0:T(2,128)(2,1)}), bf16[16,2,1024]{2,1,0:T(2,128)(2,1)S(1)}, u32[]{:S(2)}, u32[]{:S(2)}) async-start(bf16[16,2,1024]{2,1,0:T(2,128)(2,1)} %reshape.350), calls=%async_computation | async-start | bytes 131072 | tf_op jit(solution)/shard_map/all_to_all | solution.py:574
  81.4 0.1 fusion.31
  81.5 0.1 reduce_window_sum.11
  81.6 0.2 select_reduce_fusion
  81.8 7.5 %all-to-all-done = bf16[16,2,1024]{2,1,0:T(2,128)(2,1)S(1)} async-done(((bf16[16,2,1024]{2,1,0:T(2,128)(2,1)}), bf16[16,2,1024]{2,1,0:T(2,128)(2,1)S(1)}, u32[]{:S(2)}, u32[]{:S(2)}) %all-to-all-start) | async-done | bytes 65568 | tf_op jit(solution)/shard_map/all_to_all | solution.py:574
  89.3 0.1 reshape.351
  89.4 0.1 copy.17
  89.5 0.1 all_to_all.17
  89.6 0.0 all-gather.2.cloned.1.call-done
  89.6 2.2 multiply_reduce_fusion
  91.8 0.2 convolution_convert_fusion.1.block_ref
  92.1 49.1 %shard_map.129.tok_ref = bf16[4,8,64,1024]{3,2,1,0:T(8,128)(2,1)S(1)} custom-call(bf16[64,1024]{1,0:T(8,128)(2,1)S(1)} %convolution_convert_fusion.1.block_ref), custom_call_target="tpu_custom_call" | custom-call | tf_op jit(solution)/shard_map/pallas_call | solution.py:481
  141.2 1.9 copy-done.1
  143.1 82.6 %shard_map.130 = (bf16[64,1024]{1,0:T(8,128)(2,1)}, bf16[16,4,1024]{2,1,0:T(4,128)(2,1)}) custom-call(bf16[4,8,64,1024]{3,2,1,0:T(8,128)(2,1)} %copy-done.1, bf16[1024,128]{1,0:T(8,128)(2,1)} %bitcast.42, bf16[1024,128]{1,0:T(8,128)(2,1)} %bitcast.43, bf16[1024,128]{1,0:T(8,128)(2,1)} %bitcast.44), custom_call_target="tpu_custom_call" | custom-call | tf_op jit(solution)/shard_map/pallas_call | solution.py:245
  225.7 0.9 reshape_reshape.3
  226.6 0.8 fusion.8
  (16 shorter events, 0.1 us)
Async XLA Ops:
  6.5 53.0 %copy-start = (s32[32,32]{1,0:T(8,128)S(1)}, s32[32,32]{1,0:T(8,128)}, u32[]{:S(2)}) copy-start(s32[32,32]{1,0:T(8,128)} %param.15) | copy-start | bytes 12292
  6.5 83.1 %all-gather.2.cloned.1.call-start = ((), (), s32[]{:S(2)}) async-start(), calls=%async_computation.1 | async-start | bytes 2228224 | tf_op jit(solution)/shard_map/all_gather | solution.py:577
  63.3 18.1 %copy-start.4 = (s32[32]{0:T(128)S(1)}, s32[32]{0:T(128)}, u32[]{:S(2)}) copy-start(s32[32]{0:T(128)} %param.14) | copy-start | bytes 388
  63.3 26.3 %copy-start.2 = (bf16[32,1024]{1,0:T(8,128)(2,1)S(1)}, bf16[32,1024]{1,0:T(8,128)(2,1)}, u32[]{:S(2)}) copy-start(bf16[32,1024]{1,0:T(8,128)(2,1)} %param.13) | copy-start | bytes 196612
  64.5 27.4 %copy-start.3 = (f32[1024]{0:T(1024)S(1)}, f32[1024]{0:T(1024)}, u32[]{:S(2)}) copy-start(f32[1024]{0:T(1024)} %param.22) | copy-start | bytes 12292
  66.8 22.5 %all-to-all-start = ((bf16[16,2,1024]{2,1,0:T(2,128)(2,1)}), bf16[16,2,1024]{2,1,0:T(2,128)(2,1)S(1)}, u32[]{:S(2)}, u32[]{:S(2)}) async-start(bf16[16,2,1024]{2,1,0:T(2,128)(2,1)} %reshape.350), calls=%async_computation | async-start | bytes 131072 | tf_op jit(solution)/shard_map/all_to_all | solution.py:574
  141.2 1.9 copy-start.1
Sparse Core Ops, SparseCore 0:
  9.5 50.8 all-gather.1

commit v16 on v15

--- a/solution.py
+++ b/solution.py
@@ -343,7 +343,7 @@
     )(x)
 
 
-def ring_gather_kernel(nx, ny, axis, other, pieces, route, block_ref, out_ref, local_sem, send_sems, recv_sems,
+def ring_gather_kernel(nx, ny, axis, other, pieces, route, skip, block_ref, out_ref, local_sem, send_sems, recv_sems,
                        r_send, r_recv):
     me = lax.axis_index(axis)
     col = lax.axis_index(other)
@@ -357,9 +357,10 @@
         return (idx, col) if axis == "seq" else (col, idx)
 
     peers = []
-    for d in range(1, min(2, ny // 2) + 1):
+    reach = 2 if skip else 1
+    for d in range(1, min(reach, ny // 2) + 1):
         peers += [dev(x, y + d), dev(x, y - d)]
-    for d in range(1, min(2, nx // 2) + 1):
+    for d in range(1, min(reach, nx // 2) + 1):
         peers += [dev(x + d, y), dev(x - d, y)]
     n_other = lax.axis_size(other)
     barrier = pltpu.get_barrier_semaphore()
@@ -439,13 +440,43 @@
                 steps[len(steps) - min(2, half) + (d - 3)].append((direct[d - 2], cp))
         return steps
 
+    def ring_chain(axis, stage, lo, hi):
+        n = ny if axis == "y" else nx
+        c = y if axis == "y" else x
+        half = n // 2
+        mid = (lo + hi) // 2
+        steps = []
+        for sign in (1, -1):
+            prev = None
+            lane = []
+            for k in range(half):
+                u = (c - sign * k + 2 * n) % n
+                a_lo, a_hi = lo, hi
+                if k == half - 1 and n % 2 == 0:
+                    a_lo, a_hi = (lo, mid) if sign == 1 else (mid, hi)
+                if stage == 1 and k == 0:
+                    src = block_ref.at[a_lo:a_hi]
+                else:
+                    src = unit(axis, stage, u, a_lo, a_hi)
+                dst = unit(axis, stage, u, a_lo, a_hi)
+                target = dev(x, y + sign) if axis == "y" else dev(x + sign, y)
+                j = sem_count[0]
+                sem_count[0] += 1
+                cp = pltpu.make_async_remote_copy(
+                    src_ref=src, dst_ref=dst, send_sem=send_sems.at[j], recv_sem=recv_sems.at[j],
+                    device_id=target, device_id_type=pl.DeviceIdType.MESH)
+                lane.append((prev, cp))
+                prev = cp
+            steps.append(lane)
+        return steps
+
     plans = []
     step = hr // pieces
     for p in range(pieces):
         for base, first, second in ((0, "y", "x"), (hr, "x", "y")):
             lo = base + p * step
-            s1 = ring(first, 1, lo, lo + step)
-            s2 = ring(second, 2, lo, lo + step)
+            s1 = (ring if skip else ring_chain)(first, 1, lo, lo + step)
+            s2 = (ring if skip else ring_chain)(second, 2, lo, lo + step)
             plans.append((s1, s2))
 
     started = []
@@ -475,11 +506,12 @@
         cp.wait_send()
 
 
-def ring_gather(block, nx, ny, axis="seq", other="exp", cid=3, pieces=1, route=False, n_other=2):
+def ring_gather(block, nx, ny, axis="seq", other="exp", cid=3, pieces=1, route=False, n_other=2,
+                skip=False):
     vmem = pltpu.MemorySpace.VMEM
     n_sems = 4 * pieces * (nx // 2 + ny // 2) + 4
     return pl.pallas_call(
-        functools.partial(ring_gather_kernel, nx, ny, axis, other, pieces, route),
+        functools.partial(ring_gather_kernel, nx, ny, axis, other, pieces, route, skip),
         out_shape=jax.ShapeDtypeStruct((nx, ny) + block.shape, block.dtype),
         in_specs=[pl.BlockSpec(memory_space=vmem)],
         out_specs=pl.BlockSpec(memory_space=vmem),
@@ -534,7 +566,7 @@
     normed_attn = rms_scale(inputs, gain_attn).astype(jnp.bfloat16)
     projector = jnp.concatenate([w_query, w_key, w_value], axis=1)
     joined_qkv = jnp.dot(
-        ring_gather(normed_attn, n_exp // CORES, CORES, "exp", "seq", 4, pieces=2).reshape(n_exp * row_count, width),
+        ring_gather(normed_attn, n_exp // CORES, CORES, "exp", "seq", 4, pieces=2, skip=True).reshape(n_exp * row_count, width),
         projector,
         preferred_element_type=jnp.float32,
     ).astype(jnp.bfloat16)

time: 236 us -> 227 us (0.962)
  Pallas kernels: 179 us -> 171 us
    pallas_call x2, Pallas kernels: 76.4 us -> 72.3 us  [ring_gather(): pl.pallas_call(functools.partial(ring_gather_kernel, nx, ny, axis, other,...]
    pallas_call x1, Pallas kernels: 82.6 us -> 78.7 us  [ring_ffn(): pl.pallas_call(functools.partial(ring_ffn_kernel, nx, ny, splits), out_sh...]
  transfers between devices with their start and end apart: 2 -> 2, of which waited for: 1 -> 1; matrix products, arithmetic and copies ran while one was open for 5% -> 5% of each run, Pallas kernels for 20% -> 21%
where the time goes in v16:
time: 227 us; the launch traced here: 226 us
  Pallas kernels  171 us (75%)
  starting transfers between devices  14.7 us (6%)
  between operations  14.3 us (6%)
  waiting for transfers between devices  8.21 us (4%)
  matrix products  7.43 us (3%)
  local copies, waits for them, and re-layouts  5.72 us (3%)
  other arithmetic  5.09 us (2%)
    pallas_call x1, Pallas kernels, ring_ffn(): pl.pallas_call(functools.partial(ring_ffn_kernel, nx, ny, splits), out_sh...  78.7 us
    pallas_call x2, Pallas kernels, ring_gather(): pl.pallas_call(functools.partial(ring_gather_kernel, nx, ny, axis, other,...  72.3 us
    pallas_call x1, Pallas kernels, shift_exchange(): pl.pallas_call(functools.partial(shift_exchange_kernel, tuple(offsets), a...  19.9 us
    all_to_all x1, starting transfers between devices, local(): lax.all_to_all(heads_out, 'exp', split_axis=0, concat_axis=1, tiled=True)  14.7 us
    all_to_all x1, waiting for transfers between devices, local(): lax.all_to_all(heads_out, 'exp', split_axis=0, concat_axis=1, tiled=True)  7.48 us
  transfers between devices with their start and end apart: 2, of which 1 were waited for; matrix products, arithmetic and copies ran while one was open for 5% of the time, Pallas kernels for 21%

profile of v16, /device:TPU:1, one launch (start us, length us, event | category | flops | bytes accessed | tf_op | source)
XLA Modules:
  0.0 226.4 jit_solution(11673386753509721519)
XLA Ops:
  6.5 0.7 all-gather.2.cloned.1.call-update
  7.3 1.0 fusion.23
  8.3 0.9 fusion.25.block_ref
  9.2 27.3 %shard_map.127 = bf16[8,2,32,1024]{3,2,1,0:T(8,128)(2,1)S(1)} custom-call(bf16[32,1024]{1,0:T(8,128)(2,1)S(1)} %fusion.25.block_ref), custom_call_target="tpu_custom_call" | custom-call | tf_op jit(solution)/shard_map/pallas_call | solution.py:513
  36.5 1.5 convolution_convert_fusion
  38.0 0.8 slice_bitcast_fusion
  38.8 19.9 %shard_map.128 = bf16[6,512,128]{2,1,0:T(8,128)(2,1)} custom-call(bf16[512,128]{1,0:T(8,128)(2,1)} %get-tuple-element.10.block_ref), custom_call_target="tpu_custom_call" | custom-call | tf_op jit(solution)/shard_map/pallas_call | solution.py:300
  59.4 0.1 stack.31
  59.5 0.7 gather_fusion
  60.2 0.1 broadcast_in_dim.19
  60.3 1.7 pad_maximum_fusion
  62.0 1.3 fusion.37
  63.3 1.1 fusion
  64.5 1.4 fusion.15
  65.9 0.1 copy.16
  66.0 0.8 reshape.350
  66.8 14.7 %all-to-all-start = ((bf16[16,2,1024]{2,1,0:T(2,128)(2,1)}), bf16[16,2,1024]{2,1,0:T(2,128)(2,1)S(1)}, u32[]{:S(2)}, u32[]{:S(2)}) async-start(bf16[16,2,1024]{2,1,0:T(2,128)(2,1)} %reshape.350), calls=%async_computation | async-start | bytes 131072 | tf_op jit(solution)/shard_map/all_to_all | solution.py:606
  81.4 0.1 fusion.31
  81.5 0.1 reduce_window_sum.11
  81.6 0.2 select_reduce_fusion
  81.8 7.5 %all-to-all-done = bf16[16,2,1024]{2,1,0:T(2,128)(2,1)S(1)} async-done(((bf16[16,2,1024]{2,1,0:T(2,128)(2,1)}), bf16[16,2,1024]{2,1,0:T(2,128)(2,1)S(1)}, u32[]{:S(2)}, u32[]{:S(2)}) %all-to-all-start) | async-done | bytes 65568 | tf_op jit(solution)/shard_map/all_to_all | solution.py:606
  89.3 0.1 reshape.351
  89.4 0.1 copy.17
  89.5 0.1 all_to_all.17
  89.6 0.0 all-gather.2.cloned.1.call-done
  89.6 2.2 multiply_reduce_fusion
  91.8 0.2 convolution_convert_fusion.1.block_ref
  92.1 45.0 %shard_map.129.tok_ref = bf16[4,8,64,1024]{3,2,1,0:T(8,128)(2,1)S(1)} custom-call(bf16[64,1024]{1,0:T(8,128)(2,1)S(1)} %convolution_convert_fusion.1.block_ref), custom_call_target="tpu_custom_call" | custom-call | tf_op jit(solution)/shard_map/pallas_call | solution.py:513
  137.1 1.9 copy-done.1
  139.0 78.7 %shard_map.130 = (bf16[64,1024]{1,0:T(8,128)(2,1)}, bf16[16,4,1024]{2,1,0:T(4,128)(2,1)}) custom-call(bf16[4,8,64,1024]{3,2,1,0:T(8,128)(2,1)} %copy-done.1, bf16[1024,128]{1,0:T(8,128)(2,1)} %bitcast.42, bf16[1024,128]{1,0:T(8,128)(2,1)} %bitcast.43, bf16[1024,128]{1,0:T(8,128)(2,1)} %bitcast.44), custom_call_target="tpu_custom_call" | custom-call | tf_op jit(solution)/shard_map/pallas_call | solution.py:245
  217.8 0.9 reshape_reshape.3
  218.7 0.8 fusion.8
  (16 shorter events, 0.1 us)
Async XLA Ops:
  6.5 53.0 %copy-start = (s32[32,32]{1,0:T(8,128)S(1)}, s32[32,32]{1,0:T(8,128)}, u32[]{:S(2)}) copy-start(s32[32,32]{1,0:T(8,128)} %param.15) | copy-start | bytes 12292
  6.5 83.1 %all-gather.2.cloned.1.call-start = ((), (), s32[]{:S(2)}) async-start(), calls=%async_computation.1 | async-start | bytes 2228224 | tf_op jit(solution)/shard_map/all_gather | solution.py:609
  63.3 18.1 %copy-start.4 = (s32[32]{0:T(128)S(1)}, s32[32]{0:T(128)}, u32[]{:S(2)}) copy-start(s32[32]{0:T(128)} %param.14) | copy-start | bytes 388
  63.3 26.3 %copy-start.2 = (bf16[32,1024]{1,0:T(8,128)(2,1)S(1)}, bf16[32,1024]{1,0:T(8,128)(2,1)}, u32[]{:S(2)}) copy-start(bf16[32,1024]{1,0:T(8,128)(2,1)} %param.13) | copy-start | bytes 196612
  64.5 27.4 %copy-start.3 = (f32[1024]{0:T(1024)S(1)}, f32[1024]{0:T(1024)}, u32[]{:S(2)}) copy-start(f32[1024]{0:T(1024)} %param.22) | copy-start | bytes 12292
  66.8 22.5 %all-to-all-start = ((bf16[16,2,1024]{2,1,0:T(2,128)(2,1)}), bf16[16,2,1024]{2,1,0:T(2,128)(2,1)S(1)}, u32[]{:S(2)}, u32[]{:S(2)}) async-start(bf16[16,2,1024]{2,1,0:T(2,128)(2,1)} %reshape.350), calls=%async_computation | async-start | bytes 131072 | tf_op jit(solution)/shard_map/all_to_all | solution.py:606
  137.1 1.9 copy-start.1
Sparse Core Ops, SparseCore 0:
  9.5 50.8 all-gather.1

commit v17 on v16

--- a/solution.py
+++ b/solution.py
@@ -566,7 +566,7 @@
     normed_attn = rms_scale(inputs, gain_attn).astype(jnp.bfloat16)
     projector = jnp.concatenate([w_query, w_key, w_value], axis=1)
     joined_qkv = jnp.dot(
-        ring_gather(normed_attn, n_exp // CORES, CORES, "exp", "seq", 4, pieces=2, skip=True).reshape(n_exp * row_count, width),
+        ring_gather(normed_attn, n_exp // CORES, CORES, "exp", "seq", 4, skip=True).reshape(n_exp * row_count, width),
         projector,
         preferred_element_type=jnp.float32,
     ).astype(jnp.bfloat16)

time: 227 us -> 225 us (level)
  Pallas kernels: 171 us -> 168 us
    pallas_call x1, Pallas kernels: 78.7 us -> 76.4 us  [ring_ffn(): pl.pallas_call(functools.partial(ring_ffn_kernel, nx, ny, splits), out_sh...]
where the time goes in v17:
time: 225 us
  Pallas kernels  168 us (75%)
  starting transfers between devices  15.7 us (7%)
  between operations  14.3 us (6%)
  waiting for transfers between devices  8.21 us (4%)
  matrix products  7.45 us (3%)
  local copies, waits for them, and re-layouts  5.73 us (3%)
  other arithmetic  5.09 us (2%)
    pallas_call x1, Pallas kernels, ring_ffn(): pl.pallas_call(functools.partial(ring_ffn_kernel, nx, ny, splits), out_sh...  76.4 us
    pallas_call x2, Pallas kernels, ring_gather(): pl.pallas_call(functools.partial(ring_gather_kernel, nx, ny, axis, other,...  71.7 us
    pallas_call x1, Pallas kernels, shift_exchange(): pl.pallas_call(functools.partial(shift_exchange_kernel, tuple(offsets), a...  19.9 us
    all_to_all x1, starting transfers between devices, local(): lax.all_to_all(heads_out, 'exp', split_axis=0, concat_axis=1, tiled=True)  15.7 us
    all_to_all x1, waiting for transfers between devices, local(): lax.all_to_all(heads_out, 'exp', split_axis=0, concat_axis=1, tiled=True)  7.48 us
  transfers between devices with their start and end apart: 2, of which 1 were waited for; matrix products, arithmetic and copies ran while one was open for 5% of the time, Pallas kernels for 21%

profile of v17, /device:TPU:1, one launch (start us, length us, event | category | flops | bytes accessed | tf_op | source)
XLA Modules:
  0.0 224.5 jit_solution(12970668068083292925)
XLA Ops:
  6.5 0.7 all-gather.2.cloned.1.call-update
  7.3 1.0 fusion.23
  8.3 0.9 fusion.25.block_ref
  9.2 26.5 %shard_map.127 = bf16[8,2,32,1024]{3,2,1,0:T(8,128)(2,1)S(1)} custom-call(bf16[32,1024]{1,0:T(8,128)(2,1)S(1)} %fusion.25.block_ref), custom_call_target="tpu_custom_call" | custom-call | tf_op jit(solution)/shard_map/pallas_call | solution.py:513
  35.8 1.5 convolution_convert_fusion
  37.3 0.8 slice_bitcast_fusion
  38.0 19.9 %shard_map.128 = bf16[6,512,128]{2,1,0:T(8,128)(2,1)} custom-call(bf16[512,128]{1,0:T(8,128)(2,1)} %get-tuple-element.10.block_ref), custom_call_target="tpu_custom_call" | custom-call | tf_op jit(solution)/shard_map/pallas_call | solution.py:300
  58.6 0.1 stack.31
  58.8 0.7 gather_fusion
  59.4 0.1 broadcast_in_dim.19
  59.5 1.7 pad_maximum_fusion
  61.3 1.3 fusion.37
  62.6 1.1 fusion
  63.7 1.4 fusion.15
  65.1 0.1 copy.16
  65.2 0.8 reshape.350
  66.0 15.7 %all-to-all-start = ((bf16[16,2,1024]{2,1,0:T(2,128)(2,1)}), bf16[16,2,1024]{2,1,0:T(2,128)(2,1)S(1)}, u32[]{:S(2)}, u32[]{:S(2)}) async-start(bf16[16,2,1024]{2,1,0:T(2,128)(2,1)} %reshape.350), calls=%async_computation | async-start | bytes 131072 | tf_op jit(solution)/shard_map/all_to_all | solution.py:606
  81.7 0.1 fusion.31
  81.8 0.1 reduce_window_sum.11
  81.8 0.2 select_reduce_fusion
  82.0 7.5 %all-to-all-done = bf16[16,2,1024]{2,1,0:T(2,128)(2,1)S(1)} async-done(((bf16[16,2,1024]{2,1,0:T(2,128)(2,1)}), bf16[16,2,1024]{2,1,0:T(2,128)(2,1)S(1)}, u32[]{:S(2)}, u32[]{:S(2)}) %all-to-all-start) | async-done | bytes 65568 | tf_op jit(solution)/shard_map/all_to_all | solution.py:606
  89.5 0.1 reshape.351
  89.6 0.1 copy.17
  89.7 0.1 all_to_all.17
  89.9 0.0 all-gather.2.cloned.1.call-done
  89.9 2.2 multiply_reduce_fusion
  92.1 0.2 convolution_convert_fusion.1.block_ref
  92.3 45.2 %shard_map.129.tok_ref = bf16[4,8,64,1024]{3,2,1,0:T(8,128)(2,1)S(1)} custom-call(bf16[64,1024]{1,0:T(8,128)(2,1)S(1)} %convolution_convert_fusion.1.block_ref), custom_call_target="tpu_custom_call" | custom-call | tf_op jit(solution)/shard_map/pallas_call | solution.py:513
  137.6 1.9 copy-done.1
  139.5 76.4 %shard_map.130 = (bf16[64,1024]{1,0:T(8,128)(2,1)}, bf16[16,4,1024]{2,1,0:T(4,128)(2,1)}) custom-call(bf16[4,8,64,1024]{3,2,1,0:T(8,128)(2,1)} %copy-done.1, bf16[1024,128]{1,0:T(8,128)(2,1)} %bitcast.42, bf16[1024,128]{1,0:T(8,128)(2,1)} %bitcast.43, bf16[1024,128]{1,0:T(8,128)(2,1)} %bitcast.44), custom_call_target="tpu_custom_call" | custom-call | tf_op jit(solution)/shard_map/pallas_call | solution.py:245
  215.9 0.9 reshape_reshape.3
  216.8 0.8 fusion.8
  (16 shorter events, 0.1 us)
Async XLA Ops:
  6.5 52.2 %copy-start = (s32[32,32]{1,0:T(8,128)S(1)}, s32[32,32]{1,0:T(8,128)}, u32[]{:S(2)}) copy-start(s32[32,32]{1,0:T(8,128)} %param.15) | copy-start | bytes 12292
  6.5 83.3 %all-gather.2.cloned.1.call-start = ((), (), s32[]{:S(2)}) async-start(), calls=%async_computation.1 | async-start | bytes 2228224 | tf_op jit(solution)/shard_map/all_gather | solution.py:609
  62.6 19.1 %copy-start.4 = (s32[32]{0:T(128)S(1)}, s32[32]{0:T(128)}, u32[]{:S(2)}) copy-start(s32[32]{0:T(128)} %param.14) | copy-start | bytes 388
  62.6 27.3 %copy-start.2 = (bf16[32,1024]{1,0:T(8,128)(2,1)S(1)}, bf16[32,1024]{1,0:T(8,128)(2,1)}, u32[]{:S(2)}) copy-start(bf16[32,1024]{1,0:T(8,128)(2,1)} %param.13) | copy-start | bytes 196612
  63.7 28.3 %copy-start.3 = (f32[1024]{0:T(1024)S(1)}, f32[1024]{0:T(1024)}, u32[]{:S(2)}) copy-start(f32[1024]{0:T(1024)} %param.22) | copy-start | bytes 12292
  66.0 23.5 %all-to-all-start = ((bf16[16,2,1024]{2,1,0:T(2,128)(2,1)}), bf16[16,2,1024]{2,1,0:T(2,128)(2,1)S(1)}, u32[]{:S(2)}, u32[]{:S(2)}) async-start(bf16[16,2,1024]{2,1,0:T(2,128)(2,1)} %reshape.350), calls=%async_computation | async-start | bytes 131072 | tf_op jit(solution)/shard_map/all_to_all | solution.py:606
  137.6 1.9 copy-start.1
Sparse Core Ops, SparseCore 0:
  9.5 50.0 all-gather.1
